TPU v7x, 32 devices: a whole 2x2x4 slice. The times are simulated.
32 devices in a mesh: wide: 8 (over z, core), sub: 4 (over y, x).
Axes of the slice: x: 2, y: 2, z: 4, core: 2. Of those that a mesh axis runs over, the one named last changes fastest.
Arguments:
- passages: bfloat16 [64, 1024], P('sub'), may hold values from -6 to 6
- enc_weight: bfloat16 [1024, 16384], P(None, ('wide', 'sub')), may hold values from -0.1875 to 0.1875
- enc_bias: float32 [16384], P(('wide', 'sub')), may hold values from -4 to 4
- dec_weight: bfloat16 [16384, 1024], P(('wide', 'sub')), may hold values from -0.09375 to 0.09375
- dec_bias: float32 [1024], replicated, may hold values from -4 to 4
- active: int32 [64, 16384], P(None, ('wide', 'sub')), may hold values 0 or 1
Outputs:
- grad_enc: bfloat16 [1024, 16384], P(None, ('wide', 'sub'))
- grad_enc_bias: float32 [16384], P(('wide', 'sub'))
- grad_dec: bfloat16 [16384, 1024], P(('wide', 'sub'))
- grad_dec_bias: float32 [1024], replicated
- grad_input: float32 [64, 1024], P('sub')
All inputs are finite; a program needn't handle non-finite values. No bound on the sum of `active` on one device may be relied on, other than what follows from the above.
Results may differ from a plain program's by a relative error of at most 0.014.
Values may be sent and summed in bfloat16 or wider, within the bound.
No kernel may reach another device: no remote copies, remote signals or barrier semaphores. Data moves between devices by JAX's collectives and lax.ppermute only.
A program may use at most 64 MiB of HBM per device.

v0:
```python
import jax
import jax.numpy as jnp
from jax import lax
from jax.sharding import PartitionSpec as P


def per_device(passages, enc_weight, enc_bias, dec_weight, dec_bias, active):
    gate = active.astype(jnp.float32)
    every = lax.all_gather(passages, "sub", axis=0, tiled=True)
    pre = jnp.dot(every, enc_weight, preferred_element_type=jnp.float32) + enc_bias
    codes = (gate * pre).astype(jnp.bfloat16)
    block = codes
    mine = lax.psum_scatter(
        jnp.dot(block, dec_weight, preferred_element_type=jnp.float32),
        "sub",
        scatter_dimension=0,
        tiled=True,
    )
    mine = lax.psum(mine, "wide")
    own_resid = (mine + dec_bias - passages.astype(jnp.float32)).astype(jnp.bfloat16)
    resid = lax.all_gather(own_resid, "sub", axis=0, tiled=True)
    grad_dec = lax.dot_general(
        codes, resid, (((0,), (0,)), ((), ())), preferred_element_type=jnp.float32
    ).astype(jnp.bfloat16)
    grad_dec_bias = jnp.sum(resid.astype(jnp.float32), axis=0)
    back = lax.dot_general(
        resid, dec_weight, (((1,), (1,)), ((), ())), preferred_element_type=jnp.float32
    )
    dpre = (gate * back).astype(jnp.bfloat16)
    grad_enc = lax.dot_general(
        every, dpre, (((0,), (0,)), ((), ())), preferred_element_type=jnp.float32
    ).astype(jnp.bfloat16)
    grad_enc_bias = jnp.sum(dpre.astype(jnp.float32), axis=0)
    block = dpre
    summed = lax.psum_scatter(
        lax.dot_general(
            block, enc_weight, (((1,), (1,)), ((), ())), preferred_element_type=jnp.float32
        ).astype(jnp.bfloat16),
        "sub",
        scatter_dimension=0,
        tiled=True,
    ).astype(jnp.float32)
    summed = lax.psum(summed.astype(jnp.bfloat16), "wide").astype(jnp.float32)
    grad_input = summed - own_resid.astype(jnp.float32)
    return (grad_enc, grad_enc_bias, grad_dec, grad_dec_bias, grad_input)


def solution(mesh):
    in_specs = (
        P("sub", None),
        P(None, ("wide", "sub")),
        P(("wide", "sub")),
        P(("wide", "sub"), None),
        P(),
        P(None, ("wide", "sub")),
    )
    out_specs = (
        P(None, ("wide", "sub")),
        P(("wide", "sub")),
        P(("wide", "sub"), None),
        P(),
        P("sub", None),
    )
    return jax.shard_map(
        per_device, mesh=mesh, in_specs=in_specs, out_specs=out_specs, check_vma=False
    )
```

profile of v0, /device:TPU:0, one launch (start us, length us, event | category | flops | bytes accessed | tf_op | source)
XLA Modules:
  0.0 172.2 jit_solution(11498883005300085821)
XLA Ops:
  7.2 0.0 copy-start
  7.2 0.0 reduce-scatter.3.cloned.1.call-start
  7.2 10.3 %all_gather.6 = bf16[64,1024]{1,0:T(8,128)(2,1)S(1)} all-gather(bf16[16,1024]{1,0:T(8,128)(2,1)} %param.6), channel_id=1, replica_groups=mesh['wide'=8,'sub'=4] {'sub'}, dimensions={0}, use_global_device_ids=true | all-gather | bytes 163840 | tf_op jit(solution)/shard_map/all_gather | solution.py:9
  17.5 1.6 fusion.3
  19.1 0.0 copy-done
  19.1 0.0 copy-start.3
  19.1 0.0 copy-start.4
  19.1 0.0 copy-start.2
  19.2 1.0 fusion.4
  20.2 0.0 copy-start.1
  20.2 0.0 reduce-scatter.3.cloned.1.call-update
  20.2 0.0 all-reduce.2.cloned.1.call-start
  20.2 24.7 %reduce-scatter.3.cloned.1.call-done = f32[16,1024]{1,0:T(8,128)} async-done(((f32[64,1024]{1,0:T(8,128)}), f32[16,1024]{1,0:T(8,128)}) %reduce-scatter.3.cloned.1.call-update) | async-done | bytes 65552 | tf_op jit(solution)/shard_map/reduce_scatter | solution.py:13
  44.9 0.0 all-reduce.2.cloned.1.call-update
  44.9 0.0 reduce-scatter.5.cloned.1.call-start
  45.0 57.0 %all-reduce.2.cloned.1.call-done = f32[16,1024]{1,0:T(8,128)} async-done(((f32[16,1024]{1,0:T(8,128)}), f32[16,1024]{1,0:T(8,128)}) %all-reduce.2.cloned.1.call-update) | async-done | bytes 65552 | tf_op jit(solution)/shard_map/psum | solution.py:19
  102.0 0.0 copy-done.3
  102.0 0.0 copy-done.4
  102.0 0.9 subtract_convert_fusion
  102.8 8.4 %all_gather.7 = bf16[64,1024]{1,0:T(8,128)(2,1)S(1)} all-gather(bf16[16,1024]{1,0:T(8,128)(2,1)S(1)} %subtract_convert_fusion), channel_id=1, replica_groups=mesh['wide'=8,'sub'=4] {'sub'}, dimensions={0}, use_global_device_ids=true | all-gather | bytes 163840 | tf_op jit(solution)/shard_map/all_gather | solution.py:21
  111.2 0.0 copy-done.2
  111.2 1.0 convert_reduce_fusion.1
  112.3 0.0 copy-done.1
  112.3 1.1 convolution_convert_fusion.2
  113.4 0.5 fusion
  113.8 0.0 reduce-scatter.5.cloned.1.call-update
  113.8 0.6 convert_reduce_fusion
  114.5 1.3 copy.11
  115.8 1.4 convolution_convert_fusion
  117.2 19.1 %reduce-scatter.5.cloned.1.call-done = bf16[16,1024]{1,0:T(8,128)(2,1)} async-done(((bf16[64,1024]{1,0:T(8,128)(2,1)}), bf16[16,1024]{1,0:T(8,128)(2,1)}) %reduce-scatter.5.cloned.1.call-update) | async-done | bytes 32784 | tf_op jit(solution)/shard_map/reduce_scatter | solution.py:35
  136.3 28.7 %psum.15 = bf16[16,1024]{1,0:T(8,128)(2,1)S(1)} all-reduce(bf16[16,1024]{1,0:T(8,128)(2,1)} %reduce-scatter.5.cloned.1.call-done), channel_id=1, replica_groups=mesh['wide'=8,'sub'=4] {'wide'}, use_global_device_ids=true, to_apply=%region_5.0 | all-reduce | flops 16384 | bytes 65536 | tf_op jit(solution)/shard_map/psum | solution.py:43
  165.0 0.6 convert_subtract_fusion
Async XLA Ops:
  7.2 11.9 %copy-start = (bf16[512,1024]{1,0:T(8,128)(2,1)S(1)}, bf16[512,1024]{1,0:T(8,128)(2,1)}, u32[]{:S(2)}) copy-start(bf16[512,1024]{1,0:T(8,128)(2,1)} %param.9) | copy-start | bytes 3145732
  7.2 37.7 %reduce-scatter.3.cloned.1.call-start = ((), (), s32[]{:S(2)}) async-start(), calls=%async_computation.2 | async-start | bytes 327680 | tf_op jit(solution)/shard_map/reduce_scatter | solution.py:13
  19.1 82.8 %copy-start.3 = (bf16[16,1024]{1,0:T(8,128)(2,1)S(1)}, bf16[16,1024]{1,0:T(8,128)(2,1)}, u32[]{:S(2)}) copy-start(bf16[16,1024]{1,0:T(8,128)(2,1)} %param.6) | copy-start | bytes 98308
  19.1 82.8 %copy-start.4 = (f32[1024]{0:T(1024)S(1)}, f32[1024]{0:T(1024)}, u32[]{:S(2)}) copy-start(f32[1024]{0:T(1024)} %param.10) | copy-start | bytes 12292
  19.1 92.1 %copy-start.2 = (s32[64,512]{1,0:T(8,128)S(1)}, s32[64,512]{1,0:T(8,128)}, u32[]{:S(2)}) copy-start(s32[64,512]{1,0:T(8,128)} %param.11) | copy-start | bytes 393220
  20.2 92.1 %copy-start.1 = (bf16[1024,512]{1,0:T(8,128)(2,1)S(1)}, bf16[1024,512]{1,0:T(8,128)(2,1)}, u32[]{:S(2)}) copy-start(bf16[1024,512]{1,0:T(8,128)(2,1)} %param.7) | copy-start | bytes 3145732
  20.2 81.8 %all-reduce.2.cloned.1.call-start = ((), (), s32[]{:S(2)}) async-start(), calls=%async_computation.3 | async-start | bytes 131072 | tf_op jit(solution)/shard_map/psum | solution.py:19
  44.9 91.4 %reduce-scatter.5.cloned.1.call-start = ((), (), s32[]{:S(2)}) async-start(), calls=%async_computation.4 | async-start | bytes 163840 | tf_op jit(solution)/shard_map/reduce_scatter | solution.py:35
Sparse Core Ops, SparseCore 0:
  20.3 24.5 reduce-scatter.2
  47.2 54.6 all-reduce.1
  114.0 22.3 reduce-scatter.4
where the time goes:
time: 173 us; the launch traced here: 172 us
  waiting for transfers between devices  101 us (58%)
  blocking collectives  47.4 us (27%)
  between operations  13.8 us (8%)
  matrix products  6.6 us (4%)
  other arithmetic  2.11 us (1%)
    psum x1, waiting for transfers between devices, per_device(): mine = lax.psum(mine, 'wide')  57 us
    psum x1, blocking collectives, per_device(): summed = lax.psum(summed.astype(jnp.bfloat16), 'wide').astype(jnp.float32)  28.7 us
    reduce_scatter x1, waiting for transfers between devices, per_device(): lax.psum_scatter(jnp.dot(block, dec_weight, preferred_element_type=jnp.fl...  24.7 us
    reduce_scatter x1, waiting for transfers between devices, per_device(): lax.psum_scatter(lax.dot_general(block, enc_weight, (((1,), (1,)), ((), (...  19.1 us
    all_gather x1, blocking collectives, per_device(): every = lax.all_gather(passages, 'sub', axis=0, tiled=True)  10.3 us
    all_gather x1, blocking collectives, per_device(): resid = lax.all_gather(own_resid, 'sub', axis=0, tiled=True)  8.42 us
  transfers between devices with their start and end apart: 3, of which 3 were waited for; matrix products, arithmetic and copies ran while one was open for 2% of the time, Pallas kernels for 0%

commit v1 on v0

v1 whole, which is shorter than its diff:
```python
import jax
import jax.numpy as jnp
from jax import lax
from jax.sharding import PartitionSpec as P

AXES = ("wide", "sub")


def swap(x, size, mask):
    return lax.ppermute(x, AXES, [(i, i ^ mask) for i in range(size)])


def crossing(mask, core):
    return mask ^ core if mask.bit_count() % 2 else mask


def make_per_device(wide, sub):
    size = wide * sub
    core = sub
    sub_bits = [b for b in (1 << k for k in range(sub.bit_length())) if b < sub]
    z_bits = [b for b in (1 << k for k in range(size.bit_length())) if 2 * sub <= b < size]

    def rounds(bits):
        out = []
        for k in range(0, len(bits), 2):
            pair = bits[k : k + 2]
            out.append(pair if len(pair) == 1 else [pair[0], pair[1], pair[0] ^ pair[1]])
        return out

    def total(parts):
        parts = [p.astype(jnp.float32) for p in parts]
        while len(parts) > 1:
            parts = [parts[k] + parts[k + 1] for k in range(0, len(parts), 2)]
        return parts[0]

    def sum_over(x, bits, order=lambda got, mask: got):
        for masks in rounds(bits):
            got = [swap(x, size, crossing(m, core)) for m in masks]
            x = total([x] + [order(g, m) for g, m in zip(got, masks)])
            yield_last = x
            x = x.astype(jnp.bfloat16)
        return yield_last

    def per_device(passages, enc_weight, enc_bias, dec_weight, dec_bias, active):
        rows, width = passages.shape
        half = width // 2
        me = lax.axis_index(AXES)
        mine = lax.axis_index("sub")
        odd = me
        for k in (16, 8, 4, 2, 1):
            odd = odd ^ (odd >> k)
        high = (odd & 1) == 1

        blocks = [passages] + [swap(passages, size, crossing(k, core)) for k in range(1, sub)]
        every = jnp.concatenate(blocks, axis=0)
        gate = jnp.concatenate(
            [lax.dynamic_slice_in_dim(active, (mine ^ k) * rows, rows, 0) for k in range(sub)], axis=0
        ).astype(jnp.float32)

        def pick(x):
            keep = jnp.where(high, x[:, half:], x[:, :half])
            send = jnp.where(high, x[:, :half], x[:, half:])
            return keep, send.astype(jnp.bfloat16)

        def join(own, other):
            left = jnp.where(high, other, own)
            right = jnp.where(high, own, other)
            return jnp.concatenate([left, right], axis=1)

        def reorder(got, mask):
            parts = [got[(k ^ mask) * rows : ((k ^ mask) + 1) * rows] for k in range(sub)]
            return jnp.concatenate(parts, axis=0)

        pre = jnp.dot(every, enc_weight, preferred_element_type=jnp.float32) + enc_bias
        codes = (gate * pre).astype(jnp.bfloat16)
        part = jnp.dot(codes, dec_weight, preferred_element_type=jnp.float32)
        keep, send = pick(part)
        x = (keep + swap(send, size, core).astype(jnp.float32)).astype(jnp.bfloat16)
        x = sum_over(x, sub_bits, reorder).astype(jnp.bfloat16)
        recon = sum_over(x, z_bits)
        base = dec_bias - every.astype(jnp.float32)
        own = (recon + jnp.where(high, base[:, half:], base[:, :half])).astype(jnp.bfloat16)
        resid = join(own, swap(own, size, core))

        back = lax.dot_general(
            resid, dec_weight, (((1,), (1,)), ((), ())), preferred_element_type=jnp.float32
        )
        dpre = (gate * back).astype(jnp.bfloat16)
        grad = lax.dot_general(
            dpre, enc_weight, (((1,), (1,)), ((), ())), preferred_element_type=jnp.float32
        )
        keep, send = pick(grad)
        x = keep + swap(send, size, core).astype(jnp.float32)
        x = x.astype(jnp.bfloat16)
        got = [swap(x[k * rows : (k + 1) * rows], size, crossing(k, core)) for k in range(1, sub)]
        x = total([x[:rows]] + got).astype(jnp.bfloat16)
        own = sum_over(x, z_bits).astype(jnp.bfloat16)
        summed = join(own, swap(own, size, core))
        grad_input = summed.astype(jnp.float32) - resid[:rows].astype(jnp.float32)

        grad_dec = lax.dot_general(
            codes, resid, (((0,), (0,)), ((), ())), preferred_element_type=jnp.float32
        ).astype(jnp.bfloat16)
        grad_dec_bias = jnp.sum(resid.astype(jnp.float32), axis=0)
        grad_enc = lax.dot_general(
            every, dpre, (((0,), (0,)), ((), ())), preferred_element_type=jnp.float32
        ).astype(jnp.bfloat16)
        grad_enc_bias = jnp.sum(dpre.astype(jnp.float32), axis=0)
        return (grad_enc, grad_enc_bias, grad_dec, grad_dec_bias, grad_input)

    return per_device


def solution(mesh):
    in_specs = (
        P("sub", None),
        P(None, ("wide", "sub")),
        P(("wide", "sub")),
        P(("wide", "sub"), None),
        P(),
        P(None, ("wide", "sub")),
    )
    out_specs = (
        P(None, ("wide", "sub")),
        P(("wide", "sub")),
        P(("wide", "sub"), None),
        P(),
        P("sub", None),
    )
    per_device = make_per_device(mesh.shape["wide"], mesh.shape["sub"])
    return jax.shard_map(
        per_device, mesh=mesh, in_specs=in_specs, out_specs=out_specs, check_vma=False
    )
```

time: 173 us -> 49.3 us (0.28)
  waiting for transfers between devices: 101 us -> 19.5 us
  blocking collectives: 47.4 us -> 0 us
  starting transfers between devices: 0.12 us -> 19.4 us
  between operations: 13.8 us -> 0.77 us
    psum x1 -> x0, waiting for transfers between devices: 57 us -> none  [per_device(): mine = lax.psum(mine, 'wide')]
    reduce_scatter x2 -> x0, waiting for transfers between devices: 43.8 us -> none  [the longest x1 24.7 us: per_device(): lax.psum_scatter(jnp.dot(block, dec_weight, preferred_element_type=jnp.fl...]
    psum x1 -> x0, blocking collectives: 28.7 us -> none  [per_device(): summed = lax.psum(summed.astype(jnp.bfloat16), 'wide').astype(jnp.float32)]
    ppermute x0 -> x19, waiting for transfers between devices: none -> 19.5 us  [swap(): return lax.ppermute(x, AXES, [(i, i ^ mask) for i in range(size)])]
    ppermute x0 -> x19, starting transfers between devices: none -> 19.4 us  [swap(): return lax.ppermute(x, AXES, [(i, i ^ mask) for i in range(size)])]
    all_gather x2 -> x0, blocking collectives: 18.7 us -> none  [the longest x1 10.3 us: per_device(): every = lax.all_gather(passages, 'sub', axis=0, tiled=True)]
  transfers between devices with their start and end apart: 3 -> 19, of which waited for: 3 -> 14; matrix products, arithmetic and copies ran while one was open for 2% -> 10% of each run, Pallas kernels for 0% -> 0%
where the time goes in v1:
time: 49.3 us; the launch traced here: 49 us
  waiting for transfers between devices  19.5 us (40%)
  starting transfers between devices  19.4 us (39%)
  matrix products  6.15 us (12%)
  local copies, waits for them, and re-layouts  1.63 us (3%)
  other arithmetic  1.5 us (3%)
  between operations  0.77 us (2%)
    ppermute x19, waiting for transfers between devices, swap(): return lax.ppermute(x, AXES, [(i, i ^ mask) for i in range(size)])  19.5 us
    ppermute x19, starting transfers between devices, swap(): return lax.ppermute(x, AXES, [(i, i ^ mask) for i in range(size)])  19.4 us
    dot_general x1, matrix products, per_device(): jnp.dot(every, enc_weight, preferred_element_type=jnp.float32) + enc_bias  1.52 us
    dot_general x1, matrix products, per_device(): lax.dot_general(every, dpre, (((0,), (0,)), ((), ())), preferred_element_...  1.43 us
    dot_general x1, matrix products, per_device(): lax.dot_general(codes, resid, (((0,), (0,)), ((), ())), preferred_element...  1.43 us
    dot_general x1, matrix products, per_device(): lax.dot_general(resid, dec_weight, (((1,), (1,)), ((), ())), preferred_el...  1.04 us
  transfers between devices with their start and end apart: 19, of which 14 were waited for; matrix products, arithmetic and copies ran while one was open for 10% of the time, Pallas kernels for 0%

profile of v1, /device:TPU:0, one launch (start us, length us, event | category | flops | bytes accessed | tf_op | source)
XLA Modules:
  0.0 49.0 jit_solution(14021067169468793966)
XLA Ops:
  0.6 0.0 copy-start
  0.6 2.5 %collective-permute-start.1 = (bf16[16,1024]{1,0:T(8,128)(2,1)}, bf16[16,1024]{1,0:T(8,128)(2,1)S(1)}, u32[]{:S(2)}, u32[]{:S(2)}) collective-permute-start(bf16[16,1024]{1,0:T(8,128)(2,1)} %param.6), channel_id=1, source_target_pairs={{0,6},{1,7},{2,4},{3,5},{4,2},{5,3},{6,0},{7,1},{8,14},{9,15},{10,... | collective-permute-start | bytes 98312 | tf_op jit(solution)/shard_map/ppermute | solution.py:10
  3.1 1.8 %collective-permute-start = (bf16[16,1024]{1,0:T(8,128)(2,1)}, bf16[16,1024]{1,0:T(8,128)(2,1)S(1)}, u32[]{:S(2)}, u32[]{:S(2)}) collective-permute-start(bf16[16,1024]{1,0:T(8,128)(2,1)} %param.6), channel_id=1, source_target_pairs={{0,5},{1,4},{2,7},{3,6},{4,1},{5,0},{6,3},{7,2},{8,13},{9,12},{10,... | collective-permute-start | bytes 98312 | tf_op jit(solution)/shard_map/ppermute | solution.py:10
  4.9 0.0 collective-permute-start.2
  4.9 0.8 %constant_dynamic-slice_fusion.3 = (s32[16,512]{1,0:T(8,128)S(1)}, s32[16,512]{1,0:T(8,128)S(1)}, s32[16,512]{1,0:T(8,128)S(1)}, s32[16,512]{1,0:T(8,128)S(1)}) fusion(s32[64,512]{1,0:T(8,128)} %param.11, s32[]{:T(128)S(6)} %select_n.58, s32[]{:T(128)S(6)} %select_n.59, s32[]{:T(128)S(6)} %select_n.61, s32[]{:T(128)S(6)} %select_n.60), kind=kLoop, calls=%fused_computation.37 | loop fusion | bytes 262160 | tf_op jit(solution)/shard_map/dynamic_slice | solution.py:57
  5.7 0.8 %constant_dynamic-update-slice_fusion.3 = bf16[64,1024]{1,0:T(8,128)(2,1)S(1)} fusion(bf16[16,1024]{1,0:T(8,128)(2,1)} %param.6), kind=kLoop, calls=%fused_computation.33 | loop fusion | bytes 65536
  6.5 0.3 collective-permute-done
  6.8 0.0 collective-permute-done.1
  6.8 3.1 %collective-permute-done.2 = bf16[16,1024]{1,0:T(8,128)(2,1)S(1)} collective-permute-done((bf16[16,1024]{1,0:T(8,128)(2,1)}, bf16[16,1024]{1,0:T(8,128)(2,1)S(1)}, u32[]{:S(2)}, u32[]{:S(2)}) %collective-permute-start.2) | collective-permute-done | bytes 32800 | tf_op jit(solution)/shard_map/ppermute | solution.py:10
  9.9 1.5 %fusion.2 = bf16[64,512]{1,0:T(8,128)(2,1)S(1)} fusion(bf16[64,1024]{1,0:T(8,128)(2,1)S(1)} %constant_dynamic-update-slice_fusion, bf16[1024,512]{1,0:T(8,128)(2,1)} %param.7, s32[16,512]{1,0:T(8,128)S(1)} %get-tuple-element.9, s32[16,512]{1,0:T(8,128)S(1)} %get-tuple-element.10, s32[16,512]{1,0:T(8,128)S(1)} %get-tuple-element.8, ...), kind=kOutput, calls=%fused_computation.6 | convolution fusion | flops 67338240 | bytes 1378304 | tf_op jit(solution)/shard_map/dot_general | solution.py:74
  11.5 0.0 copy-done
  11.5 0.0 copy-start.2
  11.5 0.3 fusion.12
  11.8 0.1 collective-permute-start.3
  11.9 1.2 %collective-permute-done.3 = bf16[64,512]{1,0:T(8,128)(2,1)S(1)} collective-permute-done((bf16[64,512]{1,0:T(8,128)(2,1)S(1)}, bf16[64,512]{1,0:T(8,128)(2,1)S(1)}, u32[]{:S(2)}, u32[]{:S(2)}) %collective-permute-start.3) | collective-permute-done | bytes 65568 | tf_op jit(solution)/shard_map/ppermute | solution.py:10
  13.2 0.3 collective-permute-start.5
  13.5 1.5 %collective-permute-start.6 = (bf16[64,512]{1,0:T(8,128)(2,1)S(1)}, bf16[64,512]{1,0:T(8,128)(2,1)S(1)}, u32[]{:S(2)}, u32[]{:S(2)}) collective-permute-start(bf16[64,512]{1,0:T(8,128)(2,1)S(1)} %add_convert_fusion.3), channel_id=1, source_target_pairs={{0,3},{1,2},{2,1},{3,0},{4,7},{5,6},{6,5},{7,4},{8,11},{9,10},{10,... | collective-permute-start | bytes 196616 | tf_op jit(solution)/shard_map/ppermute | solution.py:10
  15.0 1.2 %collective-permute-start.4 = (bf16[64,512]{1,0:T(8,128)(2,1)S(1)}, bf16[64,512]{1,0:T(8,128)(2,1)S(1)}, u32[]{:S(2)}, u32[]{:S(2)}) collective-permute-start(bf16[64,512]{1,0:T(8,128)(2,1)S(1)} %add_convert_fusion.3), channel_id=1, source_target_pairs={{0,5},{1,4},{2,7},{3,6},{4,1},{5,0},{6,3},{7,2},{8,13},{9,12},{10,... | collective-permute-start | bytes 196616 | tf_op jit(solution)/shard_map/ppermute | solution.py:10
  16.2 1.1 %collective-permute-done.5 = bf16[64,512]{1,0:T(8,128)(2,1)S(1)} collective-permute-done((bf16[64,512]{1,0:T(8,128)(2,1)S(1)}, bf16[64,512]{1,0:T(8,128)(2,1)S(1)}, u32[]{:S(2)}, u32[]{:S(2)}) %collective-permute-start.5) | collective-permute-done | bytes 65568 | tf_op jit(solution)/shard_map/ppermute | solution.py:10
  17.3 2.1 %collective-permute-done.6 = bf16[64,512]{1,0:T(8,128)(2,1)S(1)} collective-permute-done((bf16[64,512]{1,0:T(8,128)(2,1)S(1)}, bf16[64,512]{1,0:T(8,128)(2,1)S(1)}, u32[]{:S(2)}, u32[]{:S(2)}) %collective-permute-start.6) | collective-permute-done | bytes 65568 | tf_op jit(solution)/shard_map/ppermute | solution.py:10
  19.4 0.2 collective-permute-done.4
  19.6 3.7 %collective-permute-start.9 = (bf16[64,512]{1,0:T(8,128)(2,1)S(1)}, bf16[64,512]{1,0:T(8,128)(2,1)S(1)}, u32[]{:S(2)}, u32[]{:S(2)}) collective-permute-start(bf16[64,512]{1,0:T(8,128)(2,1)S(1)} %add_convert_fusion.2), channel_id=1, source_target_pairs={{0,24},{1,25},{2,26},{3,27},{4,28},{5,29},{6,30},{7,31},{8,16},{9,... | collective-permute-start | bytes 196616 | tf_op jit(solution)/shard_map/ppermute | solution.py:10
  23.3 0.0 collective-permute-start.8
  23.3 0.5 %collective-permute-start.7 = (bf16[64,512]{1,0:T(8,128)(2,1)S(1)}, bf16[64,512]{1,0:T(8,128)(2,1)S(1)}, u32[]{:S(2)}, u32[]{:S(2)}) collective-permute-start(bf16[64,512]{1,0:T(8,128)(2,1)S(1)} %add_convert_fusion.2), channel_id=1, source_target_pairs={{0,12},{1,13},{2,14},{3,15},{4,8},{5,9},{6,10},{7,11},{8,4},{9,5},... | collective-permute-start | bytes 196616 | tf_op jit(solution)/shard_map/ppermute | solution.py:10
  23.8 0.0 copy-done.2
  23.8 0.0 copy-start.1
  23.9 2.3 %collective-permute-done.9 = bf16[64,512]{1,0:T(8,128)(2,1)S(1)} collective-permute-done((bf16[64,512]{1,0:T(8,128)(2,1)S(1)}, bf16[64,512]{1,0:T(8,128)(2,1)S(1)}, u32[]{:S(2)}, u32[]{:S(2)}) %collective-permute-start.9) | collective-permute-done | bytes 65568 | tf_op jit(solution)/shard_map/ppermute | solution.py:10
  26.1 2.9 %collective-permute-done.8 = bf16[64,512]{1,0:T(8,128)(2,1)S(1)} collective-permute-done((bf16[64,512]{1,0:T(8,128)(2,1)S(1)}, bf16[64,512]{1,0:T(8,128)(2,1)S(1)}, u32[]{:S(2)}, u32[]{:S(2)}) %collective-permute-start.8) | collective-permute-done | bytes 65568 | tf_op jit(solution)/shard_map/ppermute | solution.py:10
  29.0 0.0 collective-permute-done.7
  29.0 0.1 fusion.4
  29.0 0.3 collective-permute-start.10
  29.3 1.0 %collective-permute-done.10 = bf16[64,512]{1,0:T(8,128)(2,1)S(1)} collective-permute-done((bf16[64,512]{1,0:T(8,128)(2,1)S(1)}, bf16[64,512]{1,0:T(8,128)(2,1)S(1)}, u32[]{:S(2)}, u32[]{:S(2)}) %collective-permute-start.10) | collective-permute-done | bytes 65568 | tf_op jit(solution)/shard_map/ppermute | solution.py:10
  30.4 1.0 %convert_reduce_fusion.1 = (f32[512]{0:T(512)}, bf16[64,512]{1,0:T(8,128)(2,1)S(1)}) fusion(bf16[512,1024]{1,0:T(8,128)(2,1)S(1)} %copy-done, bf16[64,512]{1,0:T(8,128)(2,1)S(1)} %get-tuple-element.6, bf16[64,512]{1,0:T(8,128)(2,1)S(1)} %get-tuple-element.5, s32[16,512]{1,0:T(8,128)S(1)} %get-tuple-element.9, s32[16,512]{1,0:T(8,128)S(1)} %get-tuple-element.10, ...), kind=kOutput, calls=%fused_computation.18 | convolution fusion | flops 67632640 | bytes 1378304 | tf_op jit(solution)/shard_map/dot_general | solution.py:85
  31.4 0.0 copy-done.1
  31.4 0.4 fusion.13
  31.9 0.3 collective-permute-start.11
  32.2 1.0 %collective-permute-done.11 = bf16[64,512]{1,0:T(8,128)(2,1)S(1)} collective-permute-done((bf16[64,512]{1,0:T(8,128)(2,1)S(1)}, bf16[64,512]{1,0:T(8,128)(2,1)S(1)}, u32[]{:S(2)}, u32[]{:S(2)}) %collective-permute-start.11) | collective-permute-done | bytes 65568 | tf_op jit(solution)/shard_map/ppermute | solution.py:10
  33.3 0.9 %collective-permute-start.12 = (bf16[16,512]{1,0:T(8,128)(2,1)S(1)}, bf16[16,512]{1,0:T(8,128)(2,1)S(1)}, u32[]{:S(2)}, u32[]{:S(2)}) collective-permute-start(bf16[16,512]{1,0:T(8,128)(2,1)S(1)} %get-tuple-element.11), channel_id=1, source_target_pairs={{0,5},{1,4},{2,7},{3,6},{4,1},{5,0},{6,3},{7,2},{8,13},{9,12},{10,... | collective-permute-start | bytes 49160 | tf_op jit(solution)/shard_map/ppermute | solution.py:10
  34.1 1.6 %collective-permute-start.14 = (bf16[16,512]{1,0:T(8,128)(2,1)S(1)}, bf16[16,512]{1,0:T(8,128)(2,1)S(1)}, u32[]{:S(2)}, u32[]{:S(2)}) collective-permute-start(bf16[16,512]{1,0:T(8,128)(2,1)S(1)} %get-tuple-element.12), channel_id=1, source_target_pairs={{0,3},{1,2},{2,1},{3,0},{4,7},{5,6},{6,5},{7,4},{8,11},{9,10},{10,... | collective-permute-start | bytes 49160 | tf_op jit(solution)/shard_map/ppermute | solution.py:10
  35.7 0.6 %collective-permute-start.13 = (bf16[16,512]{1,0:T(8,128)(2,1)S(1)}, bf16[16,512]{1,0:T(8,128)(2,1)S(1)}, u32[]{:S(2)}, u32[]{:S(2)}) collective-permute-start(bf16[16,512]{1,0:T(8,128)(2,1)S(1)} %get-tuple-element.13), channel_id=1, source_target_pairs={{0,6},{1,7},{2,4},{3,5},{4,2},{5,3},{6,0},{7,1},{8,14},{9,15},{10,... | collective-permute-start | bytes 49160 | tf_op jit(solution)/shard_map/ppermute | solution.py:10
  36.2 0.2 collective-permute-done.12
  36.5 2.3 %collective-permute-done.14 = bf16[16,512]{1,0:T(8,128)(2,1)S(1)} collective-permute-done((bf16[16,512]{1,0:T(8,128)(2,1)S(1)}, bf16[16,512]{1,0:T(8,128)(2,1)S(1)}, u32[]{:S(2)}, u32[]{:S(2)}) %collective-permute-start.14) | collective-permute-done | bytes 16416 | tf_op jit(solution)/shard_map/ppermute | solution.py:10
  38.8 0.2 collective-permute-done.13
  38.9 2.9 %collective-permute-start.17 = (bf16[16,512]{1,0:T(8,128)(2,1)S(1)}, bf16[16,512]{1,0:T(8,128)(2,1)S(1)}, u32[]{:S(2)}, u32[]{:S(2)}) collective-permute-start(bf16[16,512]{1,0:T(8,128)(2,1)S(1)} %add_convert_fusion.5), channel_id=1, source_target_pairs={{0,24},{1,25},{2,26},{3,27},{4,28},{5,29},{6,30},{7,31},{8,16},{9,... | collective-permute-start | bytes 49160 | tf_op jit(solution)/shard_map/ppermute | solution.py:10
  41.9 0.0 collective-permute-start.16
  41.9 1.2 %collective-permute-start.15 = (bf16[16,512]{1,0:T(8,128)(2,1)S(1)}, bf16[16,512]{1,0:T(8,128)(2,1)S(1)}, u32[]{:S(2)}, u32[]{:S(2)}) collective-permute-start(bf16[16,512]{1,0:T(8,128)(2,1)S(1)} %add_convert_fusion.5), channel_id=1, source_target_pairs={{0,12},{1,13},{2,14},{3,15},{4,8},{5,9},{6,10},{7,11},{8,4},{9,5},... | collective-permute-start | bytes 49160 | tf_op jit(solution)/shard_map/ppermute | solution.py:10
  43.1 1.4 %convolution_convert_fusion.1 = bf16[1024,512]{1,0:T(8,128)(2,1)} fusion(bf16[64,1024]{1,0:T(8,128)(2,1)S(1)} %constant_dynamic-update-slice_fusion, bf16[64,512]{1,0:T(8,128)(2,1)S(1)} %get-tuple-element.27), kind=kOutput, calls=%fused_computation.1 | convolution fusion | flops 67633152 | bytes 1245184 | tf_op jit(solution)/shard_map/dot_general | solution.py:105
  44.5 0.0 collective-permute-done.17
  44.6 1.5 %collective-permute-done.16 = bf16[16,512]{1,0:T(8,128)(2,1)S(1)} collective-permute-done((bf16[16,512]{1,0:T(8,128)(2,1)S(1)}, bf16[16,512]{1,0:T(8,128)(2,1)S(1)}, u32[]{:S(2)}, u32[]{:S(2)}) %collective-permute-start.16) | collective-permute-done | bytes 16416 | tf_op jit(solution)/shard_map/ppermute | solution.py:10
  46.1 0.0 collective-permute-done.15
  46.1 0.2 collective-permute-start.18
  46.3 1.4 %convolution_convert_fusion = bf16[512,1024]{1,0:T(8,128)(2,1)} fusion(bf16[64,512]{1,0:T(8,128)(2,1)S(1)} %fusion.2, bf16[64,512]{1,0:T(8,128)(2,1)S(1)} %get-tuple-element.6, bf16[64,512]{1,0:T(8,128)(2,1)S(1)} %get-tuple-element.5), kind=kOutput, calls=%fused_computation | convolution fusion | flops 67895296 | bytes 1245184 | tf_op jit(solution)/shard_map/dot_general | solution.py:101
  47.7 0.6 %convert_reduce_fusion = f32[1024]{0:T(1024)} fusion(bf16[64,512]{1,0:T(8,128)(2,1)S(1)} %get-tuple-element.6, bf16[64,512]{1,0:T(8,128)(2,1)S(1)} %get-tuple-element.5), kind=kLoop, calls=%fused_computation.7 | loop fusion | flops 326656 | bytes 135168 | tf_op jit(solution)/shard_map/reduce_sum | solution.py:104
  48.3 0.0 collective-permute-done.18
  48.4 0.6 %convert_subtract_fusion.1 = f32[16,1024]{1,0:T(8,128)} fusion(bf16[64,512]{1,0:T(8,128)(2,1)S(1)} %get-tuple-element.5, bf16[64,512]{1,0:T(8,128)(2,1)S(1)} %get-tuple-element.6, bf16[16,512]{1,0:T(8,128)(2,1)S(1)} %get-tuple-element.25, bf16[16,512]{1,0:T(8,128)(2,1)S(1)} %get-tuple-element.24), kind=kLoop, calls=%fused_computation.22 | loop fusion | flops 147456 | bytes 229376 | tf_op jit(solution)/shard_map/sub | solution.py:99
  (17 shorter events, 0.2 us)
Async XLA Ops:
  0.6 10.8 %copy-start = (bf16[512,1024]{1,0:T(8,128)(2,1)S(1)}, bf16[512,1024]{1,0:T(8,128)(2,1)}, u32[]{:S(2)}) copy-start(bf16[512,1024]{1,0:T(8,128)(2,1)} %param.9) | copy-start | bytes 3145732
  0.6 6.2 %collective-permute-start.1 = (bf16[16,1024]{1,0:T(8,128)(2,1)}, bf16[16,1024]{1,0:T(8,128)(2,1)S(1)}, u32[]{:S(2)}, u32[]{:S(2)}) collective-permute-start(bf16[16,1024]{1,0:T(8,128)(2,1)} %param.6), channel_id=1, source_target_pairs={{0,6},{1,7},{2,4},{3,5},{4,2},{5,3},{6,0},{7,1},{8,14},{9,15},{10,... | collective-permute-start | bytes 98312 | tf_op jit(solution)/shard_map/ppermute | solution.py:10
  3.1 3.7 %collective-permute-start = (bf16[16,1024]{1,0:T(8,128)(2,1)}, bf16[16,1024]{1,0:T(8,128)(2,1)S(1)}, u32[]{:S(2)}, u32[]{:S(2)}) collective-permute-start(bf16[16,1024]{1,0:T(8,128)(2,1)} %param.6), channel_id=1, source_target_pairs={{0,5},{1,4},{2,7},{3,6},{4,1},{5,0},{6,3},{7,2},{8,13},{9,12},{10,... | collective-permute-start | bytes 98312 | tf_op jit(solution)/shard_map/ppermute | solution.py:10
  4.9 5.0 %collective-permute-start.2 = (bf16[16,1024]{1,0:T(8,128)(2,1)}, bf16[16,1024]{1,0:T(8,128)(2,1)S(1)}, u32[]{:S(2)}, u32[]{:S(2)}) collective-permute-start(bf16[16,1024]{1,0:T(8,128)(2,1)} %param.6), channel_id=1, source_target_pairs={{0,3},{1,2},{2,1},{3,0},{4,7},{5,6},{6,5},{7,4},{8,11},{9,10},{10,... | collective-permute-start | bytes 98312 | tf_op jit(solution)/shard_map/ppermute | solution.py:10
  11.5 12.3 %copy-start.2 = (f32[1024]{0:T(1024)S(1)}, f32[1024]{0:T(1024)}, u32[]{:S(2)}) copy-start(f32[1024]{0:T(1024)} %param.10) | copy-start | bytes 12292
  11.8 1.3 %collective-permute-start.3 = (bf16[64,512]{1,0:T(8,128)(2,1)S(1)}, bf16[64,512]{1,0:T(8,128)(2,1)S(1)}, u32[]{:S(2)}, u32[]{:S(2)}) collective-permute-start(bf16[64,512]{1,0:T(8,128)(2,1)S(1)} %select_convert_fusion.1), channel_id=1, source_target_pairs={{0,4},{1,5},{2,6},{3,7},{4,0},{5,1},{6,2},{7,3},{8,12},{9,13},{10,... | collective-permute-start | bytes 196616 | tf_op jit(solution)/shard_map/ppermute | solution.py:10
  13.2 4.1 %collective-permute-start.5 = (bf16[64,512]{1,0:T(8,128)(2,1)S(1)}, bf16[64,512]{1,0:T(8,128)(2,1)S(1)}, u32[]{:S(2)}, u32[]{:S(2)}) collective-permute-start(bf16[64,512]{1,0:T(8,128)(2,1)S(1)} %add_convert_fusion.3), channel_id=1, source_target_pairs={{0,6},{1,7},{2,4},{3,5},{4,2},{5,3},{6,0},{7,1},{8,14},{9,15},{10,... | collective-permute-start | bytes 196616 | tf_op jit(solution)/shard_map/ppermute | solution.py:10
  13.5 5.9 %collective-permute-start.6 = (bf16[64,512]{1,0:T(8,128)(2,1)S(1)}, bf16[64,512]{1,0:T(8,128)(2,1)S(1)}, u32[]{:S(2)}, u32[]{:S(2)}) collective-permute-start(bf16[64,512]{1,0:T(8,128)(2,1)S(1)} %add_convert_fusion.3), channel_id=1, source_target_pairs={{0,3},{1,2},{2,1},{3,0},{4,7},{5,6},{6,5},{7,4},{8,11},{9,10},{10,... | collective-permute-start | bytes 196616 | tf_op jit(solution)/shard_map/ppermute | solution.py:10
  15.0 4.6 %collective-permute-start.4 = (bf16[64,512]{1,0:T(8,128)(2,1)S(1)}, bf16[64,512]{1,0:T(8,128)(2,1)S(1)}, u32[]{:S(2)}, u32[]{:S(2)}) collective-permute-start(bf16[64,512]{1,0:T(8,128)(2,1)S(1)} %add_convert_fusion.3), channel_id=1, source_target_pairs={{0,5},{1,4},{2,7},{3,6},{4,1},{5,0},{6,3},{7,2},{8,13},{9,12},{10,... | collective-permute-start | bytes 196616 | tf_op jit(solution)/shard_map/ppermute | solution.py:10
  19.6 6.5 %collective-permute-start.9 = (bf16[64,512]{1,0:T(8,128)(2,1)S(1)}, bf16[64,512]{1,0:T(8,128)(2,1)S(1)}, u32[]{:S(2)}, u32[]{:S(2)}) collective-permute-start(bf16[64,512]{1,0:T(8,128)(2,1)S(1)} %add_convert_fusion.2), channel_id=1, source_target_pairs={{0,24},{1,25},{2,26},{3,27},{4,28},{5,29},{6,30},{7,31},{8,16},{9,... | collective-permute-start | bytes 196616 | tf_op jit(solution)/shard_map/ppermute | solution.py:10
  23.3 5.7 %collective-permute-start.8 = (bf16[64,512]{1,0:T(8,128)(2,1)S(1)}, bf16[64,512]{1,0:T(8,128)(2,1)S(1)}, u32[]{:S(2)}, u32[]{:S(2)}) collective-permute-start(bf16[64,512]{1,0:T(8,128)(2,1)S(1)} %add_convert_fusion.2), channel_id=1, source_target_pairs={{0,20},{1,21},{2,22},{3,23},{4,16},{5,17},{6,18},{7,19},{8,28},{9,... | collective-permute-start | bytes 196616 | tf_op jit(solution)/shard_map/ppermute | solution.py:10
  23.3 5.7 %collective-permute-start.7 = (bf16[64,512]{1,0:T(8,128)(2,1)S(1)}, bf16[64,512]{1,0:T(8,128)(2,1)S(1)}, u32[]{:S(2)}, u32[]{:S(2)}) collective-permute-start(bf16[64,512]{1,0:T(8,128)(2,1)S(1)} %add_convert_fusion.2), channel_id=1, source_target_pairs={{0,12},{1,13},{2,14},{3,15},{4,8},{5,9},{6,10},{7,11},{8,4},{9,5},... | collective-permute-start | bytes 196616 | tf_op jit(solution)/shard_map/ppermute | solution.py:10
  23.8 7.6 %copy-start.1 = (bf16[1024,512]{1,0:T(8,128)(2,1)S(1)}, bf16[1024,512]{1,0:T(8,128)(2,1)}, u32[]{:S(2)}) copy-start(bf16[1024,512]{1,0:T(8,128)(2,1)} %param.7) | copy-start | bytes 3145732
  29.0 1.3 %collective-permute-start.10 = (bf16[64,512]{1,0:T(8,128)(2,1)S(1)}, bf16[64,512]{1,0:T(8,128)(2,1)S(1)}, u32[]{:S(2)}, u32[]{:S(2)}) collective-permute-start(bf16[64,512]{1,0:T(8,128)(2,1)S(1)} %fusion.4), channel_id=1, source_target_pairs={{0,4},{1,5},{2,6},{3,7},{4,0},{5,1},{6,2},{7,3},{8,12},{9,13},{10,... | collective-permute-start | bytes 196616 | tf_op jit(solution)/shard_map/ppermute | solution.py:10
  31.9 1.3 %collective-permute-start.11 = (bf16[64,512]{1,0:T(8,128)(2,1)S(1)}, bf16[64,512]{1,0:T(8,128)(2,1)S(1)}, u32[]{:S(2)}, u32[]{:S(2)}) collective-permute-start(bf16[64,512]{1,0:T(8,128)(2,1)S(1)} %select_convert_fusion), channel_id=1, source_target_pairs={{0,4},{1,5},{2,6},{3,7},{4,0},{5,1},{6,2},{7,3},{8,12},{9,13},{10,... | collective-permute-start | bytes 196616 | tf_op jit(solution)/shard_map/ppermute | solution.py:10
  33.3 3.2 %collective-permute-start.12 = (bf16[16,512]{1,0:T(8,128)(2,1)S(1)}, bf16[16,512]{1,0:T(8,128)(2,1)S(1)}, u32[]{:S(2)}, u32[]{:S(2)}) collective-permute-start(bf16[16,512]{1,0:T(8,128)(2,1)S(1)} %get-tuple-element.11), channel_id=1, source_target_pairs={{0,5},{1,4},{2,7},{3,6},{4,1},{5,0},{6,3},{7,2},{8,13},{9,12},{10,... | collective-permute-start | bytes 49160 | tf_op jit(solution)/shard_map/ppermute | solution.py:10
  34.1 4.6 %collective-permute-start.14 = (bf16[16,512]{1,0:T(8,128)(2,1)S(1)}, bf16[16,512]{1,0:T(8,128)(2,1)S(1)}, u32[]{:S(2)}, u32[]{:S(2)}) collective-permute-start(bf16[16,512]{1,0:T(8,128)(2,1)S(1)} %get-tuple-element.12), channel_id=1, source_target_pairs={{0,3},{1,2},{2,1},{3,0},{4,7},{5,6},{6,5},{7,4},{8,11},{9,10},{10,... | collective-permute-start | bytes 49160 | tf_op jit(solution)/shard_map/ppermute | solution.py:10
  35.7 3.2 %collective-permute-start.13 = (bf16[16,512]{1,0:T(8,128)(2,1)S(1)}, bf16[16,512]{1,0:T(8,128)(2,1)S(1)}, u32[]{:S(2)}, u32[]{:S(2)}) collective-permute-start(bf16[16,512]{1,0:T(8,128)(2,1)S(1)} %get-tuple-element.13), channel_id=1, source_target_pairs={{0,6},{1,7},{2,4},{3,5},{4,2},{5,3},{6,0},{7,1},{8,14},{9,15},{10,... | collective-permute-start | bytes 49160 | tf_op jit(solution)/shard_map/ppermute | solution.py:10
  38.9 5.6 %collective-permute-start.17 = (bf16[16,512]{1,0:T(8,128)(2,1)S(1)}, bf16[16,512]{1,0:T(8,128)(2,1)S(1)}, u32[]{:S(2)}, u32[]{:S(2)}) collective-permute-start(bf16[16,512]{1,0:T(8,128)(2,1)S(1)} %add_convert_fusion.5), channel_id=1, source_target_pairs={{0,24},{1,25},{2,26},{3,27},{4,28},{5,29},{6,30},{7,31},{8,16},{9,... | collective-permute-start | bytes 49160 | tf_op jit(solution)/shard_map/ppermute | solution.py:10
  41.9 4.2 %collective-permute-start.16 = (bf16[16,512]{1,0:T(8,128)(2,1)S(1)}, bf16[16,512]{1,0:T(8,128)(2,1)S(1)}, u32[]{:S(2)}, u32[]{:S(2)}) collective-permute-start(bf16[16,512]{1,0:T(8,128)(2,1)S(1)} %add_convert_fusion.5), channel_id=1, source_target_pairs={{0,20},{1,21},{2,22},{3,23},{4,16},{5,17},{6,18},{7,19},{8,28},{9,... | collective-permute-start | bytes 49160 | tf_op jit(solution)/shard_map/ppermute | solution.py:10
  41.9 4.2 %collective-permute-start.15 = (bf16[16,512]{1,0:T(8,128)(2,1)S(1)}, bf16[16,512]{1,0:T(8,128)(2,1)S(1)}, u32[]{:S(2)}, u32[]{:S(2)}) collective-permute-start(bf16[16,512]{1,0:T(8,128)(2,1)S(1)} %add_convert_fusion.5), channel_id=1, source_target_pairs={{0,12},{1,13},{2,14},{3,15},{4,8},{5,9},{6,10},{7,11},{8,4},{9,5},... | collective-permute-start | bytes 49160 | tf_op jit(solution)/shard_map/ppermute | solution.py:10
  46.1 2.2 %collective-permute-start.18 = (bf16[16,512]{1,0:T(8,128)(2,1)S(1)}, bf16[16,512]{1,0:T(8,128)(2,1)S(1)}, u32[]{:S(2)}, u32[]{:S(2)}) collective-permute-start(bf16[16,512]{1,0:T(8,128)(2,1)S(1)} %add_convert_fusion.4), channel_id=1, source_target_pairs={{0,4},{1,5},{2,6},{3,7},{4,0},{5,1},{6,2},{7,3},{8,12},{9,13},{10,... | collective-permute-start | bytes 49160 | tf_op jit(solution)/shard_map/ppermute | solution.py:10

commit v2 on v1

--- a/solution.py
+++ b/solution.py
@@ -2,6 +2,7 @@
 import jax.numpy as jnp
 from jax import lax
 from jax.sharding import PartitionSpec as P
+
 
 AXES = ("wide", "sub")
 
@@ -36,10 +37,9 @@
     def sum_over(x, bits, order=lambda got, mask: got):
         for masks in rounds(bits):
             got = [swap(x, size, crossing(m, core)) for m in masks]
-            x = total([x] + [order(g, m) for g, m in zip(got, masks)])
-            yield_last = x
-            x = x.astype(jnp.bfloat16)
-        return yield_last
+            exact = total([x] + [order(g, m) for g, m in zip(got, masks)])
+            x = exact.astype(jnp.bfloat16)
+        return exact
 
     def per_device(passages, enc_weight, enc_bias, dec_weight, dec_bias, active):
         rows, width = passages.shape
@@ -71,7 +71,14 @@
             parts = [got[(k ^ mask) * rows : ((k ^ mask) + 1) * rows] for k in range(sub)]
             return jnp.concatenate(parts, axis=0)
 
-        pre = jnp.dot(every, enc_weight, preferred_element_type=jnp.float32) + enc_bias
+        pre = jnp.concatenate(
+            [
+                jnp.dot(passages, enc_weight, preferred_element_type=jnp.float32),
+                jnp.dot(every[rows:], enc_weight, preferred_element_type=jnp.float32),
+            ],
+            axis=0,
+        )
+        pre = pre + enc_bias
         codes = (gate * pre).astype(jnp.bfloat16)
         part = jnp.dot(codes, dec_weight, preferred_element_type=jnp.float32)
         keep, send = pick(part)
@@ -92,20 +99,20 @@
         keep, send = pick(grad)
         x = keep + swap(send, size, core).astype(jnp.float32)
         x = x.astype(jnp.bfloat16)
+        grad_dec = lax.dot_general(
+            codes, resid, (((0,), (0,)), ((), ())), preferred_element_type=jnp.float32
+        ).astype(jnp.bfloat16)
+        grad_enc = lax.dot_general(
+            every, dpre, (((0,), (0,)), ((), ())), preferred_element_type=jnp.float32
+        ).astype(jnp.bfloat16)
+        grad_dec_bias = jnp.sum(lax.optimization_barrier(resid).astype(jnp.float32), axis=0)
+        grad_enc_bias = jnp.sum(lax.optimization_barrier(dpre).astype(jnp.float32), axis=0)
+
         got = [swap(x[k * rows : (k + 1) * rows], size, crossing(k, core)) for k in range(1, sub)]
         x = total([x[:rows]] + got).astype(jnp.bfloat16)
         own = sum_over(x, z_bits).astype(jnp.bfloat16)
         summed = join(own, swap(own, size, core))
         grad_input = summed.astype(jnp.float32) - resid[:rows].astype(jnp.float32)
-
-        grad_dec = lax.dot_general(
-            codes, resid, (((0,), (0,)), ((), ())), preferred_element_type=jnp.float32
-        ).astype(jnp.bfloat16)
-        grad_dec_bias = jnp.sum(resid.astype(jnp.float32), axis=0)
-        grad_enc = lax.dot_general(
-            every, dpre, (((0,), (0,)), ((), ())), preferred_element_type=jnp.float32
-        ).astype(jnp.bfloat16)
-        grad_enc_bias = jnp.sum(dpre.astype(jnp.float32), axis=0)
         return (grad_enc, grad_enc_bias, grad_dec, grad_dec_bias, grad_input)
 
     return per_device
@@ -128,6 +135,7 @@
         P("sub", None),
     )
     per_device = make_per_device(mesh.shape["wide"], mesh.shape["sub"])
+
     return jax.shard_map(
         per_device, mesh=mesh, in_specs=in_specs, out_specs=out_specs, check_vma=False
     )

time: 49.3 us -> 50 us (1.014)
  waiting for transfers between devices: 19.5 us -> 20.8 us
  local copies, waits for them, and re-layouts: 1.63 us -> 0.92 us
  other arithmetic: 1.5 us -> 2.13 us
    ppermute x19, waiting for transfers between devices: 19.5 us -> 20.8 us  [swap(): return lax.ppermute(x, AXES, [(i, i ^ mask) for i in range(size)])]
    unnamed x9 -> x13, local copies, waits for them, and re-layouts: 0.79 us -> 0.05 us
    reduce_sum x1 -> x2, other arithmetic: 0.62 us -> 1.23 us  [the longest x1 0.62 us: per_device(): jnp.sum(lax.optimization_barrier(resid).astype(jnp.float32), axis=0)]
    dot_general x1, matrix products: 1.04 us -> 0.45 us  [per_device(): lax.dot_general(resid, dec_weight, (((1,), (1,)), ((), ())), preferred_el...]
    dot_general x1 -> x2, matrix products: 1.52 us -> 1.75 us  [the longest x1 1.48 us: per_device(): jnp.dot(passages, enc_weight, preferred_element_type=jnp.float32)]
  transfers between devices with their start and end apart: 19 -> 19, of which waited for: 14 -> 12; matrix products, arithmetic and copies ran while one was open for 10% -> 10% of each run, Pallas kernels for 0% -> 0%
where the time goes in v2:
time: 50 us; the launch traced here: 49.8 us
  waiting for transfers between devices  20.8 us (42%)
  starting transfers between devices  19.3 us (39%)
  matrix products  5.8 us (12%)
  other arithmetic  2.13 us (4%)
  local copies, waits for them, and re-layouts  0.92 us (2%)
  between operations  0.86 us (2%)
    ppermute x19, waiting for transfers between devices, swap(): return lax.ppermute(x, AXES, [(i, i ^ mask) for i in range(size)])  20.8 us
    ppermute x19, starting transfers between devices, swap(): return lax.ppermute(x, AXES, [(i, i ^ mask) for i in range(size)])  19.3 us
    dot_general x1, matrix products, per_device(): jnp.dot(passages, enc_weight, preferred_element_type=jnp.float32)  1.48 us
    dot_general x1, matrix products, per_device(): lax.dot_general(every, dpre, (((0,), (0,)), ((), ())), preferred_element_...  1.44 us
    dot_general x1, matrix products, per_device(): lax.dot_general(codes, resid, (((0,), (0,)), ((), ())), preferred_element...  1.43 us
  transfers between devices with their start and end apart: 19, of which 12 were waited for; matrix products, arithmetic and copies ran while one was open for 10% of the time, Pallas kernels for 0%

profile of v2, /device:TPU:0, one launch (start us, length us, event | category | flops | bytes accessed | tf_op | source)
XLA Modules:
  0.0 49.8 jit_solution(10119103646139398249)
XLA Ops:
  0.6 0.0 copy-start
  0.6 0.0 copy-start.2
  0.7 0.0 copy-start.1
  0.7 2.5 %collective-permute-start = (bf16[16,1024]{1,0:T(8,128)(2,1)}, bf16[16,1024]{1,0:T(8,128)(2,1)S(1)}, u32[]{:S(2)}, u32[]{:S(2)}) collective-permute-start(bf16[16,1024]{1,0:T(8,128)(2,1)} %param.6), channel_id=1, source_target_pairs={{0,5},{1,4},{2,7},{3,6},{4,1},{5,0},{6,3},{7,2},{8,13},{9,12},{10,... | collective-permute-start | bytes 98312 | tf_op jit(solution)/shard_map/ppermute | solution.py:11
  3.1 1.8 %collective-permute-start.1 = (bf16[16,1024]{1,0:T(8,128)(2,1)}, bf16[16,1024]{1,0:T(8,128)(2,1)S(1)}, u32[]{:S(2)}, u32[]{:S(2)}) collective-permute-start(bf16[16,1024]{1,0:T(8,128)(2,1)} %param.6), channel_id=1, source_target_pairs={{0,6},{1,7},{2,4},{3,5},{4,2},{5,3},{6,0},{7,1},{8,14},{9,15},{10,... | collective-permute-start | bytes 98312 | tf_op jit(solution)/shard_map/ppermute | solution.py:11
  4.9 0.0 collective-permute-start.2
  4.9 1.5 %fusion.17 = f32[16,512]{1,0:T(8,128)S(1)} fusion(bf16[16,1024]{1,0:T(8,128)(2,1)} %param.6, bf16[1024,512]{1,0:T(8,128)(2,1)} %param.7), kind=kOutput, calls=%fused_computation.49 | convolution fusion | flops 16777216 | bytes 1114112 | tf_op jit(solution)/shard_map/dot_general | solution.py:76
  6.4 0.0 copy-start.4
  6.4 0.8 %constant_dynamic-slice_fusion.3 = (s32[16,512]{1,0:T(8,128)S(1)}, s32[16,512]{1,0:T(8,128)S(1)}, s32[16,512]{1,0:T(8,128)S(1)}, s32[16,512]{1,0:T(8,128)S(1)}) fusion(s32[64,512]{1,0:T(8,128)} %param.11, s32[]{:T(128)S(6)} %select_n.58, s32[]{:T(128)S(6)} %select_n.59, s32[]{:T(128)S(6)} %select_n.61, s32[]{:T(128)S(6)} %select_n.60), kind=kLoop, calls=%fused_computation.43 | loop fusion | bytes 262160 | tf_op jit(solution)/shard_map/dynamic_slice | solution.py:57
  7.3 0.0 copy-done.2
  7.3 0.0 collective-permute-done
  7.3 0.0 collective-permute-done.1
  7.3 2.6 %collective-permute-done.2 = bf16[16,1024]{1,0:T(8,128)(2,1)S(1)} collective-permute-done((bf16[16,1024]{1,0:T(8,128)(2,1)}, bf16[16,1024]{1,0:T(8,128)(2,1)S(1)}, u32[]{:S(2)}, u32[]{:S(2)}) %collective-permute-start.2) | collective-permute-done | bytes 32800 | tf_op jit(solution)/shard_map/ppermute | solution.py:11
  10.0 0.0 copy-done.1
  10.0 0.3 fusion.5
  10.2 0.0 copy-done.4
  10.3 0.0 copy-done
  10.3 0.3 fusion.18
  10.6 0.0 copy-start.3
  10.6 0.1 collective-permute-start.3
  10.7 1.2 %collective-permute-done.3 = bf16[64,512]{1,0:T(8,128)(2,1)S(1)} collective-permute-done((bf16[64,512]{1,0:T(8,128)(2,1)S(1)}, bf16[64,512]{1,0:T(8,128)(2,1)S(1)}, u32[]{:S(2)}, u32[]{:S(2)}) %collective-permute-start.3) | collective-permute-done | bytes 65568 | tf_op jit(solution)/shard_map/ppermute | solution.py:11
  12.0 0.3 collective-permute-start.5
  12.3 1.5 %collective-permute-start.6 = (bf16[64,512]{1,0:T(8,128)(2,1)S(1)}, bf16[64,512]{1,0:T(8,128)(2,1)S(1)}, u32[]{:S(2)}, u32[]{:S(2)}) collective-permute-start(bf16[64,512]{1,0:T(8,128)(2,1)S(1)} %add_convert_fusion.3), channel_id=1, source_target_pairs={{0,3},{1,2},{2,1},{3,0},{4,7},{5,6},{6,5},{7,4},{8,11},{9,10},{10,... | collective-permute-start | bytes 196616 | tf_op jit(solution)/shard_map/ppermute | solution.py:11
  13.8 1.2 %collective-permute-start.4 = (bf16[64,512]{1,0:T(8,128)(2,1)S(1)}, bf16[64,512]{1,0:T(8,128)(2,1)S(1)}, u32[]{:S(2)}, u32[]{:S(2)}) collective-permute-start(bf16[64,512]{1,0:T(8,128)(2,1)S(1)} %add_convert_fusion.3), channel_id=1, source_target_pairs={{0,5},{1,4},{2,7},{3,6},{4,1},{5,0},{6,3},{7,2},{8,13},{9,12},{10,... | collective-permute-start | bytes 196616 | tf_op jit(solution)/shard_map/ppermute | solution.py:11
  15.0 1.1 %collective-permute-done.5 = bf16[64,512]{1,0:T(8,128)(2,1)S(1)} collective-permute-done((bf16[64,512]{1,0:T(8,128)(2,1)S(1)}, bf16[64,512]{1,0:T(8,128)(2,1)S(1)}, u32[]{:S(2)}, u32[]{:S(2)}) %collective-permute-start.5) | collective-permute-done | bytes 65568 | tf_op jit(solution)/shard_map/ppermute | solution.py:11
  16.1 2.1 %collective-permute-done.6 = bf16[64,512]{1,0:T(8,128)(2,1)S(1)} collective-permute-done((bf16[64,512]{1,0:T(8,128)(2,1)S(1)}, bf16[64,512]{1,0:T(8,128)(2,1)S(1)}, u32[]{:S(2)}, u32[]{:S(2)}) %collective-permute-start.6) | collective-permute-done | bytes 65568 | tf_op jit(solution)/shard_map/ppermute | solution.py:11
  18.2 0.2 collective-permute-done.4
  18.5 1.7 %collective-permute-start.7 = (bf16[64,512]{1,0:T(8,128)(2,1)S(1)}, bf16[64,512]{1,0:T(8,128)(2,1)S(1)}, u32[]{:S(2)}, u32[]{:S(2)}) collective-permute-start(bf16[64,512]{1,0:T(8,128)(2,1)S(1)} %add_convert_fusion.2), channel_id=1, source_target_pairs={{0,12},{1,13},{2,14},{3,15},{4,8},{5,9},{6,10},{7,11},{8,4},{9,5},... | collective-permute-start | bytes 196616 | tf_op jit(solution)/shard_map/ppermute | solution.py:11
  20.1 2.3 %collective-permute-start.8 = (bf16[64,512]{1,0:T(8,128)(2,1)S(1)}, bf16[64,512]{1,0:T(8,128)(2,1)S(1)}, u32[]{:S(2)}, u32[]{:S(2)}) collective-permute-start(bf16[64,512]{1,0:T(8,128)(2,1)S(1)} %add_convert_fusion.2), channel_id=1, source_target_pairs={{0,20},{1,21},{2,22},{3,23},{4,16},{5,17},{6,18},{7,19},{8,28},{9,... | collective-permute-start | bytes 196616 | tf_op jit(solution)/shard_map/ppermute | solution.py:11
  22.4 0.2 collective-permute-start.9
  22.6 0.0 copy-done.3
  22.7 0.0 collective-permute-done.7
  22.7 3.9 %collective-permute-done.8 = bf16[64,512]{1,0:T(8,128)(2,1)S(1)} collective-permute-done((bf16[64,512]{1,0:T(8,128)(2,1)S(1)}, bf16[64,512]{1,0:T(8,128)(2,1)S(1)}, u32[]{:S(2)}, u32[]{:S(2)}) %collective-permute-start.8) | collective-permute-done | bytes 65568 | tf_op jit(solution)/shard_map/ppermute | solution.py:11
  26.6 2.2 %collective-permute-done.9 = bf16[64,512]{1,0:T(8,128)(2,1)S(1)} collective-permute-done((bf16[64,512]{1,0:T(8,128)(2,1)S(1)}, bf16[64,512]{1,0:T(8,128)(2,1)S(1)}, u32[]{:S(2)}, u32[]{:S(2)}) %collective-permute-start.9) | collective-permute-done | bytes 65568 | tf_op jit(solution)/shard_map/ppermute | solution.py:11
  28.8 0.1 collective-permute-start.10
  28.9 1.2 %collective-permute-done.10 = bf16[64,512]{1,0:T(8,128)(2,1)S(1)} collective-permute-done((bf16[64,512]{1,0:T(8,128)(2,1)S(1)}, bf16[64,512]{1,0:T(8,128)(2,1)S(1)}, u32[]{:S(2)}, u32[]{:S(2)}) %collective-permute-start.10) | collective-permute-done | bytes 65568 | tf_op jit(solution)/shard_map/ppermute | solution.py:11
  30.1 0.4 fusion
  30.6 0.4 fusion.19
  31.0 1.4 %convolution_convert_fusion.1 = bf16[1024,512]{1,0:T(8,128)(2,1)} fusion(bf16[64,1024]{1,0:T(8,128)(2,1)S(1)} %constant_dynamic-update-slice_fusion, bf16[64,512]{1,0:T(8,128)(2,1)S(1)} %fusion), kind=kOutput, calls=%fused_computation.1 | convolution fusion | flops 67633152 | bytes 1245184 | tf_op jit(solution)/shard_map/dot_general | solution.py:105
  32.5 0.2 collective-permute-start.11
  32.7 1.4 %convolution_convert_fusion = bf16[512,1024]{1,0:T(8,128)(2,1)} fusion(bf16[64,512]{1,0:T(8,128)(2,1)S(1)} %fusion.4, bf16[64,512]{1,0:T(8,128)(2,1)S(1)} %get-tuple-element.6, bf16[64,512]{1,0:T(8,128)(2,1)S(1)} %get-tuple-element.5), kind=kOutput, calls=%fused_computation | convolution fusion | flops 67895296 | bytes 1245184 | tf_op jit(solution)/shard_map/dot_general | solution.py:102
  34.1 0.0 collective-permute-done.11
  34.2 0.8 %collective-permute-start.12 = (bf16[16,512]{1,0:T(8,128)(2,1)S(1)}, bf16[16,512]{1,0:T(8,128)(2,1)S(1)}, u32[]{:S(2)}, u32[]{:S(2)}) collective-permute-start(bf16[16,512]{1,0:T(8,128)(2,1)S(1)} %get-tuple-element.11), channel_id=1, source_target_pairs={{0,5},{1,4},{2,7},{3,6},{4,1},{5,0},{6,3},{7,2},{8,13},{9,12},{10,... | collective-permute-start | bytes 49160 | tf_op jit(solution)/shard_map/ppermute | solution.py:11
  35.0 0.4 collective-permute-start.13
  35.3 2.1 %collective-permute-start.14 = (bf16[16,512]{1,0:T(8,128)(2,1)S(1)}, bf16[16,512]{1,0:T(8,128)(2,1)S(1)}, u32[]{:S(2)}, u32[]{:S(2)}) collective-permute-start(bf16[16,512]{1,0:T(8,128)(2,1)S(1)} %get-tuple-element.12), channel_id=1, source_target_pairs={{0,3},{1,2},{2,1},{3,0},{4,7},{5,6},{6,5},{7,4},{8,11},{9,10},{10,... | collective-permute-start | bytes 49160 | tf_op jit(solution)/shard_map/ppermute | solution.py:11
  37.5 0.0 collective-permute-done.12
  37.5 0.6 %collective-permute-done.13 = bf16[16,512]{1,0:T(8,128)(2,1)S(1)} collective-permute-done((bf16[16,512]{1,0:T(8,128)(2,1)S(1)}, bf16[16,512]{1,0:T(8,128)(2,1)S(1)}, u32[]{:S(2)}, u32[]{:S(2)}) %collective-permute-start.13) | collective-permute-done | bytes 16416 | tf_op jit(solution)/shard_map/ppermute | solution.py:11
  38.1 1.9 %collective-permute-done.14 = bf16[16,512]{1,0:T(8,128)(2,1)S(1)} collective-permute-done((bf16[16,512]{1,0:T(8,128)(2,1)S(1)}, bf16[16,512]{1,0:T(8,128)(2,1)S(1)}, u32[]{:S(2)}, u32[]{:S(2)}) %collective-permute-start.14) | collective-permute-done | bytes 16416 | tf_op jit(solution)/shard_map/ppermute | solution.py:11
  40.0 0.2 collective-permute-start.15
  40.2 2.2 %collective-permute-start.16 = (bf16[16,512]{1,0:T(8,128)(2,1)S(1)}, bf16[16,512]{1,0:T(8,128)(2,1)S(1)}, u32[]{:S(2)}, u32[]{:S(2)}) collective-permute-start(bf16[16,512]{1,0:T(8,128)(2,1)S(1)} %add_convert_fusion.5), channel_id=1, source_target_pairs={{0,20},{1,21},{2,22},{3,23},{4,16},{5,17},{6,18},{7,19},{8,28},{9,... | collective-permute-start | bytes 49160 | tf_op jit(solution)/shard_map/ppermute | solution.py:11
  42.4 1.8 %collective-permute-start.17 = (bf16[16,512]{1,0:T(8,128)(2,1)S(1)}, bf16[16,512]{1,0:T(8,128)(2,1)S(1)}, u32[]{:S(2)}, u32[]{:S(2)}) collective-permute-start(bf16[16,512]{1,0:T(8,128)(2,1)S(1)} %add_convert_fusion.5), channel_id=1, source_target_pairs={{0,24},{1,25},{2,26},{3,27},{4,28},{5,29},{6,30},{7,31},{8,16},{9,... | collective-permute-start | bytes 49160 | tf_op jit(solution)/shard_map/ppermute | solution.py:11
  44.2 0.6 %convert_reduce_fusion = f32[1024]{0:T(1024)} fusion(bf16[64,1024]{1,0:T(8,128)(2,1)S(1)} %pad_maximum_fusion), kind=kLoop, calls=%fused_computation.4 | loop fusion | flops 130048 | bytes 135168 | tf_op jit(solution)/shard_map/reduce_sum | solution.py:108
  44.8 0.0 collective-permute-done.15
  44.8 0.0 collective-permute-done.16
  44.8 3.1 %collective-permute-done.17 = bf16[16,512]{1,0:T(8,128)(2,1)S(1)} collective-permute-done((bf16[16,512]{1,0:T(8,128)(2,1)S(1)}, bf16[16,512]{1,0:T(8,128)(2,1)S(1)}, u32[]{:S(2)}, u32[]{:S(2)}) %collective-permute-start.17) | collective-permute-done | bytes 16416 | tf_op jit(solution)/shard_map/ppermute | solution.py:11
  47.9 0.1 collective-permute-start.18
  48.0 0.6 %convert_reduce_fusion.1 = f32[512]{0:T(512)} fusion(bf16[64,512]{1,0:T(8,128)(2,1)S(1)} %fusion), kind=kLoop, calls=%fused_computation.18 | loop fusion | flops 65024 | bytes 67584 | tf_op jit(solution)/shard_map/reduce_sum | solution.py:109
  48.6 0.6 %collective-permute-done.18 = bf16[16,512]{1,0:T(8,128)(2,1)S(1)} collective-permute-done((bf16[16,512]{1,0:T(8,128)(2,1)S(1)}, bf16[16,512]{1,0:T(8,128)(2,1)S(1)}, u32[]{:S(2)}, u32[]{:S(2)}) %collective-permute-start.18) | collective-permute-done | bytes 16416 | tf_op jit(solution)/shard_map/ppermute | solution.py:11
  49.2 0.6 %convert_subtract_fusion.1 = f32[16,1024]{1,0:T(8,128)} fusion(bf16[64,512]{1,0:T(8,128)(2,1)S(1)} %get-tuple-element.5, bf16[64,512]{1,0:T(8,128)(2,1)S(1)} %get-tuple-element.6, bf16[16,512]{1,0:T(8,128)(2,1)S(1)} %get-tuple-element.25, bf16[16,512]{1,0:T(8,128)(2,1)S(1)} %get-tuple-element.24), kind=kLoop, calls=%fused_computation.28 | loop fusion | flops 147456 | bytes 229376 | tf_op jit(solution)/shard_map/sub | solution.py:115
  (21 shorter events, 0.3 us)
Async XLA Ops:
  0.6 9.7 %copy-start = (bf16[512,1024]{1,0:T(8,128)(2,1)S(1)}, bf16[512,1024]{1,0:T(8,128)(2,1)}, u32[]{:S(2)}) copy-start(bf16[512,1024]{1,0:T(8,128)(2,1)} %param.9) | copy-start | bytes 3145732
  0.6 6.6 %copy-start.2 = (bf16[16,1024]{1,0:T(8,128)(2,1)S(1)}, bf16[16,1024]{1,0:T(8,128)(2,1)}, u32[]{:S(2)}) copy-start(bf16[16,1024]{1,0:T(8,128)(2,1)} %param.6) | copy-start | bytes 98308
  0.7 9.3 %copy-start.1 = (bf16[1024,512]{1,0:T(8,128)(2,1)S(1)}, bf16[1024,512]{1,0:T(8,128)(2,1)}, u32[]{:S(2)}) copy-start(bf16[1024,512]{1,0:T(8,128)(2,1)} %param.7) | copy-start | bytes 3145732
  0.7 6.6 %collective-permute-start = (bf16[16,1024]{1,0:T(8,128)(2,1)}, bf16[16,1024]{1,0:T(8,128)(2,1)S(1)}, u32[]{:S(2)}, u32[]{:S(2)}) collective-permute-start(bf16[16,1024]{1,0:T(8,128)(2,1)} %param.6), channel_id=1, source_target_pairs={{0,5},{1,4},{2,7},{3,6},{4,1},{5,0},{6,3},{7,2},{8,13},{9,12},{10,... | collective-permute-start | bytes 98312 | tf_op jit(solution)/shard_map/ppermute | solution.py:11
  3.1 4.2 %collective-permute-start.1 = (bf16[16,1024]{1,0:T(8,128)(2,1)}, bf16[16,1024]{1,0:T(8,128)(2,1)S(1)}, u32[]{:S(2)}, u32[]{:S(2)}) collective-permute-start(bf16[16,1024]{1,0:T(8,128)(2,1)} %param.6), channel_id=1, source_target_pairs={{0,6},{1,7},{2,4},{3,5},{4,2},{5,3},{6,0},{7,1},{8,14},{9,15},{10,... | collective-permute-start | bytes 98312 | tf_op jit(solution)/shard_map/ppermute | solution.py:11
  4.9 5.0 %collective-permute-start.2 = (bf16[16,1024]{1,0:T(8,128)(2,1)}, bf16[16,1024]{1,0:T(8,128)(2,1)S(1)}, u32[]{:S(2)}, u32[]{:S(2)}) collective-permute-start(bf16[16,1024]{1,0:T(8,128)(2,1)} %param.6), channel_id=1, source_target_pairs={{0,3},{1,2},{2,1},{3,0},{4,7},{5,6},{6,5},{7,4},{8,11},{9,10},{10,... | collective-permute-start | bytes 98312 | tf_op jit(solution)/shard_map/ppermute | solution.py:11
  6.4 3.8 %copy-start.4 = (f32[512]{0:T(512)S(1)}, f32[512]{0:T(512)}, u32[]{:S(2)}) copy-start(f32[512]{0:T(512)} %param.8) | copy-start | bytes 6148
  10.6 12.0 %copy-start.3 = (f32[1024]{0:T(1024)S(1)}, f32[1024]{0:T(1024)}, u32[]{:S(2)}) copy-start(f32[1024]{0:T(1024)} %param.10) | copy-start | bytes 12292
  10.6 1.3 %collective-permute-start.3 = (bf16[64,512]{1,0:T(8,128)(2,1)S(1)}, bf16[64,512]{1,0:T(8,128)(2,1)S(1)}, u32[]{:S(2)}, u32[]{:S(2)}) collective-permute-start(bf16[64,512]{1,0:T(8,128)(2,1)S(1)} %select_convert_fusion.1), channel_id=1, source_target_pairs={{0,4},{1,5},{2,6},{3,7},{4,0},{5,1},{6,2},{7,3},{8,12},{9,13},{10,... | collective-permute-start | bytes 196616 | tf_op jit(solution)/shard_map/ppermute | solution.py:11
  12.0 4.1 %collective-permute-start.5 = (bf16[64,512]{1,0:T(8,128)(2,1)S(1)}, bf16[64,512]{1,0:T(8,128)(2,1)S(1)}, u32[]{:S(2)}, u32[]{:S(2)}) collective-permute-start(bf16[64,512]{1,0:T(8,128)(2,1)S(1)} %add_convert_fusion.3), channel_id=1, source_target_pairs={{0,6},{1,7},{2,4},{3,5},{4,2},{5,3},{6,0},{7,1},{8,14},{9,15},{10,... | collective-permute-start | bytes 196616 | tf_op jit(solution)/shard_map/ppermute | solution.py:11
  12.3 5.9 %collective-permute-start.6 = (bf16[64,512]{1,0:T(8,128)(2,1)S(1)}, bf16[64,512]{1,0:T(8,128)(2,1)S(1)}, u32[]{:S(2)}, u32[]{:S(2)}) collective-permute-start(bf16[64,512]{1,0:T(8,128)(2,1)S(1)} %add_convert_fusion.3), channel_id=1, source_target_pairs={{0,3},{1,2},{2,1},{3,0},{4,7},{5,6},{6,5},{7,4},{8,11},{9,10},{10,... | collective-permute-start | bytes 196616 | tf_op jit(solution)/shard_map/ppermute | solution.py:11
  13.8 4.6 %collective-permute-start.4 = (bf16[64,512]{1,0:T(8,128)(2,1)S(1)}, bf16[64,512]{1,0:T(8,128)(2,1)S(1)}, u32[]{:S(2)}, u32[]{:S(2)}) collective-permute-start(bf16[64,512]{1,0:T(8,128)(2,1)S(1)} %add_convert_fusion.3), channel_id=1, source_target_pairs={{0,5},{1,4},{2,7},{3,6},{4,1},{5,0},{6,3},{7,2},{8,13},{9,12},{10,... | collective-permute-start | bytes 196616 | tf_op jit(solution)/shard_map/ppermute | solution.py:11
  18.5 4.2 %collective-permute-start.7 = (bf16[64,512]{1,0:T(8,128)(2,1)S(1)}, bf16[64,512]{1,0:T(8,128)(2,1)S(1)}, u32[]{:S(2)}, u32[]{:S(2)}) collective-permute-start(bf16[64,512]{1,0:T(8,128)(2,1)S(1)} %add_convert_fusion.2), channel_id=1, source_target_pairs={{0,12},{1,13},{2,14},{3,15},{4,8},{5,9},{6,10},{7,11},{8,4},{9,5},... | collective-permute-start | bytes 196616 | tf_op jit(solution)/shard_map/ppermute | solution.py:11
  20.1 6.4 %collective-permute-start.8 = (bf16[64,512]{1,0:T(8,128)(2,1)S(1)}, bf16[64,512]{1,0:T(8,128)(2,1)S(1)}, u32[]{:S(2)}, u32[]{:S(2)}) collective-permute-start(bf16[64,512]{1,0:T(8,128)(2,1)S(1)} %add_convert_fusion.2), channel_id=1, source_target_pairs={{0,20},{1,21},{2,22},{3,23},{4,16},{5,17},{6,18},{7,19},{8,28},{9,... | collective-permute-start | bytes 196616 | tf_op jit(solution)/shard_map/ppermute | solution.py:11
  22.4 6.3 %collective-permute-start.9 = (bf16[64,512]{1,0:T(8,128)(2,1)S(1)}, bf16[64,512]{1,0:T(8,128)(2,1)S(1)}, u32[]{:S(2)}, u32[]{:S(2)}) collective-permute-start(bf16[64,512]{1,0:T(8,128)(2,1)S(1)} %add_convert_fusion.2), channel_id=1, source_target_pairs={{0,24},{1,25},{2,26},{3,27},{4,28},{5,29},{6,30},{7,31},{8,16},{9,... | collective-permute-start | bytes 196616 | tf_op jit(solution)/shard_map/ppermute | solution.py:11
  28.8 1.3 %collective-permute-start.10 = (bf16[64,512]{1,0:T(8,128)(2,1)S(1)}, bf16[64,512]{1,0:T(8,128)(2,1)S(1)}, u32[]{:S(2)}, u32[]{:S(2)}) collective-permute-start(bf16[64,512]{1,0:T(8,128)(2,1)S(1)} %fusion.2), channel_id=1, source_target_pairs={{0,4},{1,5},{2,6},{3,7},{4,0},{5,1},{6,2},{7,3},{8,12},{9,13},{10,... | collective-permute-start | bytes 196616 | tf_op jit(solution)/shard_map/ppermute | solution.py:11
  32.5 1.7 %collective-permute-start.11 = (bf16[64,512]{1,0:T(8,128)(2,1)S(1)}, bf16[64,512]{1,0:T(8,128)(2,1)S(1)}, u32[]{:S(2)}, u32[]{:S(2)}) collective-permute-start(bf16[64,512]{1,0:T(8,128)(2,1)S(1)} %select_convert_fusion), channel_id=1, source_target_pairs={{0,4},{1,5},{2,6},{3,7},{4,0},{5,1},{6,2},{7,3},{8,12},{9,13},{10,... | collective-permute-start | bytes 196616 | tf_op jit(solution)/shard_map/ppermute | solution.py:11
  34.2 3.3 %collective-permute-start.12 = (bf16[16,512]{1,0:T(8,128)(2,1)S(1)}, bf16[16,512]{1,0:T(8,128)(2,1)S(1)}, u32[]{:S(2)}, u32[]{:S(2)}) collective-permute-start(bf16[16,512]{1,0:T(8,128)(2,1)S(1)} %get-tuple-element.11), channel_id=1, source_target_pairs={{0,5},{1,4},{2,7},{3,6},{4,1},{5,0},{6,3},{7,2},{8,13},{9,12},{10,... | collective-permute-start | bytes 49160 | tf_op jit(solution)/shard_map/ppermute | solution.py:11
  35.0 3.2 %collective-permute-start.13 = (bf16[16,512]{1,0:T(8,128)(2,1)S(1)}, bf16[16,512]{1,0:T(8,128)(2,1)S(1)}, u32[]{:S(2)}, u32[]{:S(2)}) collective-permute-start(bf16[16,512]{1,0:T(8,128)(2,1)S(1)} %get-tuple-element.13), channel_id=1, source_target_pairs={{0,6},{1,7},{2,4},{3,5},{4,2},{5,3},{6,0},{7,1},{8,14},{9,15},{10,... | collective-permute-start | bytes 49160 | tf_op jit(solution)/shard_map/ppermute | solution.py:11
  35.3 4.6 %collective-permute-start.14 = (bf16[16,512]{1,0:T(8,128)(2,1)S(1)}, bf16[16,512]{1,0:T(8,128)(2,1)S(1)}, u32[]{:S(2)}, u32[]{:S(2)}) collective-permute-start(bf16[16,512]{1,0:T(8,128)(2,1)S(1)} %get-tuple-element.12), channel_id=1, source_target_pairs={{0,3},{1,2},{2,1},{3,0},{4,7},{5,6},{6,5},{7,4},{8,11},{9,10},{10,... | collective-permute-start | bytes 49160 | tf_op jit(solution)/shard_map/ppermute | solution.py:11
  40.0 4.8 %collective-permute-start.15 = (bf16[16,512]{1,0:T(8,128)(2,1)S(1)}, bf16[16,512]{1,0:T(8,128)(2,1)S(1)}, u32[]{:S(2)}, u32[]{:S(2)}) collective-permute-start(bf16[16,512]{1,0:T(8,128)(2,1)S(1)} %add_convert_fusion.5), channel_id=1, source_target_pairs={{0,12},{1,13},{2,14},{3,15},{4,8},{5,9},{6,10},{7,11},{8,4},{9,5},... | collective-permute-start | bytes 49160 | tf_op jit(solution)/shard_map/ppermute | solution.py:11
  40.2 4.6 %collective-permute-start.16 = (bf16[16,512]{1,0:T(8,128)(2,1)S(1)}, bf16[16,512]{1,0:T(8,128)(2,1)S(1)}, u32[]{:S(2)}, u32[]{:S(2)}) collective-permute-start(bf16[16,512]{1,0:T(8,128)(2,1)S(1)} %add_convert_fusion.5), channel_id=1, source_target_pairs={{0,20},{1,21},{2,22},{3,23},{4,16},{5,17},{6,18},{7,19},{8,28},{9,... | collective-permute-start | bytes 49160 | tf_op jit(solution)/shard_map/ppermute | solution.py:11
  42.4 5.5 %collective-permute-start.17 = (bf16[16,512]{1,0:T(8,128)(2,1)S(1)}, bf16[16,512]{1,0:T(8,128)(2,1)S(1)}, u32[]{:S(2)}, u32[]{:S(2)}) collective-permute-start(bf16[16,512]{1,0:T(8,128)(2,1)S(1)} %add_convert_fusion.5), channel_id=1, source_target_pairs={{0,24},{1,25},{2,26},{3,27},{4,28},{5,29},{6,30},{7,31},{8,16},{9,... | collective-permute-start | bytes 49160 | tf_op jit(solution)/shard_map/ppermute | solution.py:11
  47.9 1.2 %collective-permute-start.18 = (bf16[16,512]{1,0:T(8,128)(2,1)S(1)}, bf16[16,512]{1,0:T(8,128)(2,1)S(1)}, u32[]{:S(2)}, u32[]{:S(2)}) collective-permute-start(bf16[16,512]{1,0:T(8,128)(2,1)S(1)} %add_convert_fusion.4), channel_id=1, source_target_pairs={{0,4},{1,5},{2,6},{3,7},{4,0},{5,1},{6,2},{7,3},{8,12},{9,13},{10,... | collective-permute-start | bytes 49160 | tf_op jit(solution)/shard_map/ppermute | solution.py:11

commit v3 on v2

--- a/solution.py
+++ b/solution.py
@@ -11,8 +11,14 @@
     return lax.ppermute(x, AXES, [(i, i ^ mask) for i in range(size)])
 
 
+CROSS = 0b11011
+OWN = 0b1110
+LAST = 0b1110
+FIRST = 0b1100
+
+
 def crossing(mask, core):
-    return mask ^ core if mask.bit_count() % 2 else mask
+    return mask ^ core if (mask & CROSS).bit_count() % 2 else mask
 
 
 def make_per_device(wide, sub):
@@ -34,9 +40,12 @@
             parts = [parts[k] + parts[k + 1] for k in range(0, len(parts), 2)]
         return parts[0]
 
-    def sum_over(x, bits, order=lambda got, mask: got):
+    def sum_over(x, bits, order=lambda got, mask: got, cross=None):
         for masks in rounds(bits):
-            got = [swap(x, size, crossing(m, core)) for m in masks]
+            got = [
+                swap(x, size, crossing(m, core) if cross is None else m ^ (core if cross >> (k + 1) & 1 else 0))
+                for k, m in enumerate(masks)
+            ]
             exact = total([x] + [order(g, m) for g, m in zip(got, masks)])
             x = exact.astype(jnp.bfloat16)
         return exact
@@ -46,21 +55,16 @@
         half = width // 2
         me = lax.axis_index(AXES)
         mine = lax.axis_index("sub")
-        odd = me
+        odd = me & (CROSS | core)
         for k in (16, 8, 4, 2, 1):
             odd = odd ^ (odd >> k)
         high = (odd & 1) == 1
 
-        blocks = [passages] + [swap(passages, size, crossing(k, core)) for k in range(1, sub)]
+        blocks = [passages] + [swap(passages, size, k ^ (core if FIRST >> k & 1 else 0)) for k in range(1, sub)]
         every = jnp.concatenate(blocks, axis=0)
         gate = jnp.concatenate(
             [lax.dynamic_slice_in_dim(active, (mine ^ k) * rows, rows, 0) for k in range(sub)], axis=0
         ).astype(jnp.float32)
-
-        def pick(x):
-            keep = jnp.where(high, x[:, half:], x[:, :half])
-            send = jnp.where(high, x[:, :half], x[:, half:])
-            return keep, send.astype(jnp.bfloat16)
 
         def join(own, other):
             left = jnp.where(high, other, own)
@@ -80,25 +84,43 @@
         )
         pre = pre + enc_bias
         codes = (gate * pre).astype(jnp.bfloat16)
-        part = jnp.dot(codes, dec_weight, preferred_element_type=jnp.float32)
-        keep, send = pick(part)
-        x = (keep + swap(send, size, core).astype(jnp.float32)).astype(jnp.bfloat16)
+        mine_at = jnp.where(high, half, 0)
+        send = jnp.dot(
+            codes,
+            lax.dynamic_slice_in_dim(dec_weight, half - mine_at, half, 1),
+            preferred_element_type=jnp.float32,
+        ).astype(jnp.bfloat16)
+        got = swap(send, size, core)
+        keep = jnp.dot(
+            codes,
+            lax.dynamic_slice_in_dim(dec_weight, mine_at, half, 1),
+            preferred_element_type=jnp.float32,
+        )
+        x = (lax.optimization_barrier(keep) + got.astype(jnp.float32)).astype(jnp.bfloat16)
         x = sum_over(x, sub_bits, reorder).astype(jnp.bfloat16)
         recon = sum_over(x, z_bits)
         base = dec_bias - every.astype(jnp.float32)
         own = (recon + jnp.where(high, base[:, half:], base[:, :half])).astype(jnp.bfloat16)
-        resid = join(own, swap(own, size, core))
+        other = swap(own, size, core)
+        resid = join(own, other)
+        mine_at = jnp.where(high, half, 0)
 
-        back = lax.dot_general(
-            resid, dec_weight, (((1,), (1,)), ((), ())), preferred_element_type=jnp.float32
-        )
+        def against(part, at):
+            return lax.dot_general(
+                part,
+                lax.dynamic_slice_in_dim(dec_weight, at, half, 1),
+                (((1,), (1,)), ((), ())),
+                preferred_element_type=jnp.float32,
+            )
+
+        back = lax.optimization_barrier(against(own, mine_at))
+        back = back + against(other, half - mine_at)
         dpre = (gate * back).astype(jnp.bfloat16)
         grad = lax.dot_general(
             dpre, enc_weight, (((1,), (1,)), ((), ())), preferred_element_type=jnp.float32
         )
-        keep, send = pick(grad)
-        x = keep + swap(send, size, core).astype(jnp.float32)
-        x = x.astype(jnp.bfloat16)
+        grad = grad.astype(jnp.bfloat16)
+        x = (grad.astype(jnp.float32) + swap(grad, size, core).astype(jnp.float32)).astype(jnp.bfloat16)
         grad_dec = lax.dot_general(
             codes, resid, (((0,), (0,)), ((), ())), preferred_element_type=jnp.float32
         ).astype(jnp.bfloat16)
@@ -108,11 +130,9 @@
         grad_dec_bias = jnp.sum(lax.optimization_barrier(resid).astype(jnp.float32), axis=0)
         grad_enc_bias = jnp.sum(lax.optimization_barrier(dpre).astype(jnp.float32), axis=0)
 
-        got = [swap(x[k * rows : (k + 1) * rows], size, crossing(k, core)) for k in range(1, sub)]
+        got = [swap(x[k * rows : (k + 1) * rows], size, k ^ (core if OWN >> k & 1 else 0)) for k in range(1, sub)]
         x = total([x[:rows]] + got).astype(jnp.bfloat16)
-        own = sum_over(x, z_bits).astype(jnp.bfloat16)
-        summed = join(own, swap(own, size, core))
-        grad_input = summed.astype(jnp.float32) - resid[:rows].astype(jnp.float32)
+        grad_input = sum_over(x, z_bits, cross=LAST) - resid[:rows].astype(jnp.float32)
         return (grad_enc, grad_enc_bias, grad_dec, grad_dec_bias, grad_input)
 
     return per_device
@@ -136,6 +156,4 @@
     )
     per_device = make_per_device(mesh.shape["wide"], mesh.shape["sub"])
 
-    return jax.shard_map(
-        per_device, mesh=mesh, in_specs=in_specs, out_specs=out_specs, check_vma=False
-    )
+    return jax.shard_map(per_device, mesh=mesh, in_specs=in_specs, out_specs=out_specs, check_vma=False)

time: 50 us -> 48 us (0.960)
  waiting for transfers between devices: 20.8 us -> 17.6 us
  starting transfers between devices: 19.3 us -> 20.2 us
    ppermute x19 -> x18, waiting for transfers between devices: 20.8 us -> 17.6 us  [swap(): return lax.ppermute(x, AXES, [(i, i ^ mask) for i in range(size)])]
    ppermute x19 -> x18, starting transfers between devices: 19.3 us -> 20.2 us  [swap(): return lax.ppermute(x, AXES, [(i, i ^ mask) for i in range(size)])]
    dot_general x2 -> x4, matrix products: 0.75 us -> 1.01 us  [the longest x2 0.58 us: against(): lax.dot_general(part, lax.dynamic_slice_in_dim(dec_weight, at, half, 1),...]
  transfers between devices with their start and end apart: 19 -> 18, of which waited for: 12 -> 13; matrix products, arithmetic and copies ran while one was open for 10% -> 11% of each run, Pallas kernels for 0% -> 0%
where the time goes in v3:
time: 48 us; the launch traced here: 47.8 us
  starting transfers between devices  20.2 us (42%)
  waiting for transfers between devices  17.6 us (37%)
  matrix products  6.07 us (13%)
  other arithmetic  2.11 us (4%)
  local copies, waits for them, and re-layouts  0.92 us (2%)
  between operations  0.82 us (2%)
    ppermute x18, starting transfers between devices, swap(): return lax.ppermute(x, AXES, [(i, i ^ mask) for i in range(size)])  20.2 us
    ppermute x18, waiting for transfers between devices, swap(): return lax.ppermute(x, AXES, [(i, i ^ mask) for i in range(size)])  17.6 us
    dot_general x1, matrix products, per_device(): jnp.dot(passages, enc_weight, preferred_element_type=jnp.float32)  1.48 us
    dot_general x1, matrix products, per_device(): lax.dot_general(every, dpre, (((0,), (0,)), ((), ())), preferred_element_...  1.44 us
    dot_general x1, matrix products, per_device(): lax.dot_general(codes, resid, (((0,), (0,)), ((), ())), preferred_element...  1.43 us
  transfers between devices with their start and end apart: 18, of which 13 were waited for; matrix products, arithmetic and copies ran while one was open for 11% of the time, Pallas kernels for 0%

profile of v3, /device:TPU:0, one launch (start us, length us, event | category | flops | bytes accessed | tf_op | source)
XLA Modules:
  0.0 47.8 jit_solution(13565036563521418817)
XLA Ops:
  0.6 0.0 copy-start
  0.6 0.0 copy-start.2
  0.7 0.0 copy-start.1
  0.7 3.0 %collective-permute-start = (bf16[16,1024]{1,0:T(8,128)(2,1)}, bf16[16,1024]{1,0:T(8,128)(2,1)S(1)}, u32[]{:S(2)}, u32[]{:S(2)}) collective-permute-start(bf16[16,1024]{1,0:T(8,128)(2,1)} %param.6), channel_id=1, source_target_pairs={{0,1},{1,0},{2,3},{3,2},{4,5},{5,4},{6,7},{7,6},{8,9},{9,8},{10,11... | collective-permute-start | bytes 98312 | tf_op jit(solution)/shard_map/ppermute | solution.py:11
  3.7 0.7 %collective-permute-start.1 = (bf16[16,1024]{1,0:T(8,128)(2,1)}, bf16[16,1024]{1,0:T(8,128)(2,1)S(1)}, u32[]{:S(2)}, u32[]{:S(2)}) collective-permute-start(bf16[16,1024]{1,0:T(8,128)(2,1)} %param.6), channel_id=1, source_target_pairs={{0,6},{1,7},{2,4},{3,5},{4,2},{5,3},{6,0},{7,1},{8,14},{9,15},{10,... | collective-permute-start | bytes 98312 | tf_op jit(solution)/shard_map/ppermute | solution.py:11
  4.4 0.6 %collective-permute-start.2 = (bf16[16,1024]{1,0:T(8,128)(2,1)}, bf16[16,1024]{1,0:T(8,128)(2,1)S(1)}, u32[]{:S(2)}, u32[]{:S(2)}) collective-permute-start(bf16[16,1024]{1,0:T(8,128)(2,1)} %param.6), channel_id=1, source_target_pairs={{0,7},{1,6},{2,5},{3,4},{4,3},{5,2},{6,1},{7,0},{8,15},{9,14},{10,... | collective-permute-start | bytes 98312 | tf_op jit(solution)/shard_map/ppermute | solution.py:11
  5.0 1.5 %fusion.28 = f32[16,512]{1,0:T(8,128)S(1)} fusion(bf16[16,1024]{1,0:T(8,128)(2,1)} %param.6, bf16[1024,512]{1,0:T(8,128)(2,1)} %param.7), kind=kOutput, calls=%fused_computation.57 | convolution fusion | flops 16777216 | bytes 1114112 | tf_op jit(solution)/shard_map/dot_general | solution.py:80
  6.4 0.0 copy-start.4
  6.4 0.8 %constant_dynamic-slice_fusion.3 = (s32[16,512]{1,0:T(8,128)S(1)}, s32[16,512]{1,0:T(8,128)S(1)}, s32[16,512]{1,0:T(8,128)S(1)}, s32[16,512]{1,0:T(8,128)S(1)}) fusion(s32[64,512]{1,0:T(8,128)} %param.11, s32[]{:T(128)S(6)} %select_n.41, s32[]{:T(128)S(6)} %select_n.42, s32[]{:T(128)S(6)} %select_n.44, s32[]{:T(128)S(6)} %select_n.43), kind=kLoop, calls=%fused_computation.51 | loop fusion | bytes 262160 | tf_op jit(solution)/shard_map/dynamic_slice | solution.py:66
  7.3 0.0 copy-done.2
  7.3 0.0 collective-permute-done
  7.3 0.2 collective-permute-done.1
  7.5 1.3 %collective-permute-done.2 = bf16[16,1024]{1,0:T(8,128)(2,1)S(1)} collective-permute-done((bf16[16,1024]{1,0:T(8,128)(2,1)}, bf16[16,1024]{1,0:T(8,128)(2,1)S(1)}, u32[]{:S(2)}, u32[]{:S(2)}) %collective-permute-start.2) | collective-permute-done | bytes 32800 | tf_op jit(solution)/shard_map/ppermute | solution.py:11
  8.8 0.0 copy-done.1
  8.8 0.3 fusion.12
  9.1 0.0 copy-done.4
  9.2 0.0 copy-done
  9.2 0.2 fusion.6
  9.4 0.0 copy-start.3
  9.4 0.2 convolution_convert_fusion.3
  9.6 1.0 %collective-permute-start.3 = (bf16[64,512]{1,0:T(8,128)(2,1)S(1)}, bf16[64,512]{1,0:T(8,128)(2,1)S(1)}, u32[]{:S(2)}, u32[]{:S(2)}) collective-permute-start(bf16[64,512]{1,0:T(8,128)(2,1)S(1)} %convolution_convert_fusion.3), channel_id=1, source_target_pairs={{0,4},{1,5},{2,6},{3,7},{4,0},{5,1},{6,2},{7,3},{8,12},{9,13},{10,... | collective-permute-start | bytes 196616 | tf_op jit(solution)/shard_map/ppermute | solution.py:11
  10.7 0.9 %collective-permute-done.3 = bf16[64,512]{1,0:T(8,128)(2,1)S(1)} collective-permute-done((bf16[64,512]{1,0:T(8,128)(2,1)S(1)}, bf16[64,512]{1,0:T(8,128)(2,1)S(1)}, u32[]{:S(2)}, u32[]{:S(2)}) %collective-permute-start.3) | collective-permute-done | bytes 65568 | tf_op jit(solution)/shard_map/ppermute | solution.py:11
  11.6 0.5 %collective-permute-start.5 = (bf16[64,512]{1,0:T(8,128)(2,1)S(1)}, bf16[64,512]{1,0:T(8,128)(2,1)S(1)}, u32[]{:S(2)}, u32[]{:S(2)}) collective-permute-start(bf16[64,512]{1,0:T(8,128)(2,1)S(1)} %add_convert_fusion.3), channel_id=1, source_target_pairs={{0,6},{1,7},{2,4},{3,5},{4,2},{5,3},{6,0},{7,1},{8,14},{9,15},{10,... | collective-permute-start | bytes 196616 | tf_op jit(solution)/shard_map/ppermute | solution.py:11
  12.1 1.5 %collective-permute-start.6 = (bf16[64,512]{1,0:T(8,128)(2,1)S(1)}, bf16[64,512]{1,0:T(8,128)(2,1)S(1)}, u32[]{:S(2)}, u32[]{:S(2)}) collective-permute-start(bf16[64,512]{1,0:T(8,128)(2,1)S(1)} %add_convert_fusion.3), channel_id=1, source_target_pairs={{0,3},{1,2},{2,1},{3,0},{4,7},{5,6},{6,5},{7,4},{8,11},{9,10},{10,... | collective-permute-start | bytes 196616 | tf_op jit(solution)/shard_map/ppermute | solution.py:11
  13.6 1.0 %collective-permute-start.4 = (bf16[64,512]{1,0:T(8,128)(2,1)S(1)}, bf16[64,512]{1,0:T(8,128)(2,1)S(1)}, u32[]{:S(2)}, u32[]{:S(2)}) collective-permute-start(bf16[64,512]{1,0:T(8,128)(2,1)S(1)} %add_convert_fusion.3), channel_id=1, source_target_pairs={{0,5},{1,4},{2,7},{3,6},{4,1},{5,0},{6,3},{7,2},{8,13},{9,12},{10,... | collective-permute-start | bytes 196616 | tf_op jit(solution)/shard_map/ppermute | solution.py:11
  14.6 0.9 %collective-permute-done.5 = bf16[64,512]{1,0:T(8,128)(2,1)S(1)} collective-permute-done((bf16[64,512]{1,0:T(8,128)(2,1)S(1)}, bf16[64,512]{1,0:T(8,128)(2,1)S(1)}, u32[]{:S(2)}, u32[]{:S(2)}) %collective-permute-start.5) | collective-permute-done | bytes 65568 | tf_op jit(solution)/shard_map/ppermute | solution.py:11
  15.5 2.3 %collective-permute-done.6 = bf16[64,512]{1,0:T(8,128)(2,1)S(1)} collective-permute-done((bf16[64,512]{1,0:T(8,128)(2,1)S(1)}, bf16[64,512]{1,0:T(8,128)(2,1)S(1)}, u32[]{:S(2)}, u32[]{:S(2)}) %collective-permute-start.6) | collective-permute-done | bytes 65568 | tf_op jit(solution)/shard_map/ppermute | solution.py:11
  17.8 0.1 collective-permute-done.4
  18.0 1.8 %collective-permute-start.7 = (bf16[64,512]{1,0:T(8,128)(2,1)S(1)}, bf16[64,512]{1,0:T(8,128)(2,1)S(1)}, u32[]{:S(2)}, u32[]{:S(2)}) collective-permute-start(bf16[64,512]{1,0:T(8,128)(2,1)S(1)} %add_convert_fusion.2), channel_id=1, source_target_pairs={{0,12},{1,13},{2,14},{3,15},{4,8},{5,9},{6,10},{7,11},{8,4},{9,5},... | collective-permute-start | bytes 196616 | tf_op jit(solution)/shard_map/ppermute | solution.py:11
  19.8 2.1 %collective-permute-start.8 = (bf16[64,512]{1,0:T(8,128)(2,1)S(1)}, bf16[64,512]{1,0:T(8,128)(2,1)S(1)}, u32[]{:S(2)}, u32[]{:S(2)}) collective-permute-start(bf16[64,512]{1,0:T(8,128)(2,1)S(1)} %add_convert_fusion.2), channel_id=1, source_target_pairs={{0,20},{1,21},{2,22},{3,23},{4,16},{5,17},{6,18},{7,19},{8,28},{9,... | collective-permute-start | bytes 196616 | tf_op jit(solution)/shard_map/ppermute | solution.py:11
  21.9 0.3 collective-permute-start.9
  22.3 0.0 copy-done.3
  22.3 0.0 collective-permute-done.7
  22.3 4.0 %collective-permute-done.8 = bf16[64,512]{1,0:T(8,128)(2,1)S(1)} collective-permute-done((bf16[64,512]{1,0:T(8,128)(2,1)S(1)}, bf16[64,512]{1,0:T(8,128)(2,1)S(1)}, u32[]{:S(2)}, u32[]{:S(2)}) %collective-permute-start.8) | collective-permute-done | bytes 65568 | tf_op jit(solution)/shard_map/ppermute | solution.py:11
  26.3 2.1 %collective-permute-done.9 = bf16[64,512]{1,0:T(8,128)(2,1)S(1)} collective-permute-done((bf16[64,512]{1,0:T(8,128)(2,1)S(1)}, bf16[64,512]{1,0:T(8,128)(2,1)S(1)}, u32[]{:S(2)}, u32[]{:S(2)}) %collective-permute-start.9) | collective-permute-done | bytes 65568 | tf_op jit(solution)/shard_map/ppermute | solution.py:11
  28.4 0.1 fusion.9
  28.5 0.1 collective-permute-start.10
  28.5 0.3 fusion.4
  28.8 0.9 %collective-permute-done.10 = bf16[64,512]{1,0:T(8,128)(2,1)S(1)} collective-permute-done((bf16[64,512]{1,0:T(8,128)(2,1)S(1)}, bf16[64,512]{1,0:T(8,128)(2,1)S(1)}, u32[]{:S(2)}, u32[]{:S(2)}) %collective-permute-start.10) | collective-permute-done | bytes 65568 | tf_op jit(solution)/shard_map/ppermute | solution.py:11
  29.8 0.3 fusion.1
  30.1 0.4 convolution_convert_fusion.2
  30.5 1.4 %convolution_convert_fusion.1 = bf16[1024,512]{1,0:T(8,128)(2,1)} fusion(bf16[64,1024]{1,0:T(8,128)(2,1)S(1)} %constant_dynamic-update-slice_fusion, bf16[64,512]{1,0:T(8,128)(2,1)S(1)} %fusion.1), kind=kOutput, calls=%fused_computation.1 | convolution fusion | flops 67633152 | bytes 1245184 | tf_op jit(solution)/shard_map/dot_general | solution.py:127
  31.9 0.2 collective-permute-start.11
  32.1 1.4 %convolution_convert_fusion = bf16[512,1024]{1,0:T(8,128)(2,1)} fusion(bf16[64,512]{1,0:T(8,128)(2,1)S(1)} %fusion.11, bf16[64,512]{1,0:T(8,128)(2,1)S(1)} %get-tuple-element.9, bf16[64,512]{1,0:T(8,128)(2,1)S(1)} %get-tuple-element.8), kind=kOutput, calls=%fused_computation | convolution fusion | flops 67895296 | bytes 1245184 | tf_op jit(solution)/shard_map/dot_general | solution.py:124
  33.6 0.0 collective-permute-done.11
  33.6 1.1 %collective-permute-start.12 = (bf16[16,1024]{1,0:T(8,128)(2,1)S(1)}, bf16[16,1024]{1,0:T(8,128)(2,1)S(1)}, u32[]{:S(2)}, u32[]{:S(2)}) collective-permute-start(bf16[16,1024]{1,0:T(8,128)(2,1)S(1)} %get-tuple-element.5), channel_id=1, source_target_pairs={{0,5},{1,4},{2,7},{3,6},{4,1},{5,0},{6,3},{7,2},{8,13},{9,12},{10,... | collective-permute-start | bytes 98312 | tf_op jit(solution)/shard_map/ppermute | solution.py:11
  34.7 0.3 collective-permute-start.13
  35.0 1.8 %collective-permute-start.14 = (bf16[16,1024]{1,0:T(8,128)(2,1)S(1)}, bf16[16,1024]{1,0:T(8,128)(2,1)S(1)}, u32[]{:S(2)}, u32[]{:S(2)}) collective-permute-start(bf16[16,1024]{1,0:T(8,128)(2,1)S(1)} %get-tuple-element.6), channel_id=1, source_target_pairs={{0,7},{1,6},{2,5},{3,4},{4,3},{5,2},{6,1},{7,0},{8,15},{9,14},{10,... | collective-permute-start | bytes 98312 | tf_op jit(solution)/shard_map/ppermute | solution.py:11
  36.9 0.6 %convert_reduce_fusion = f32[1024]{0:T(1024)} fusion(bf16[64,1024]{1,0:T(8,128)(2,1)S(1)} %pad_maximum_fusion), kind=kLoop, calls=%fused_computation.14 | loop fusion | flops 130048 | bytes 135168 | tf_op jit(solution)/shard_map/reduce_sum | solution.py:130
  37.5 0.0 collective-permute-done.12
  37.5 0.6 %collective-permute-done.13 = bf16[16,1024]{1,0:T(8,128)(2,1)S(1)} collective-permute-done((bf16[16,1024]{1,0:T(8,128)(2,1)S(1)}, bf16[16,1024]{1,0:T(8,128)(2,1)S(1)}, u32[]{:S(2)}, u32[]{:S(2)}) %collective-permute-start.13) | collective-permute-done | bytes 32800 | tf_op jit(solution)/shard_map/ppermute | solution.py:11
  38.1 1.2 %collective-permute-done.14 = bf16[16,1024]{1,0:T(8,128)(2,1)S(1)} collective-permute-done((bf16[16,1024]{1,0:T(8,128)(2,1)S(1)}, bf16[16,1024]{1,0:T(8,128)(2,1)S(1)}, u32[]{:S(2)}, u32[]{:S(2)}) %collective-permute-start.14) | collective-permute-done | bytes 32800 | tf_op jit(solution)/shard_map/ppermute | solution.py:11
  39.3 1.4 %collective-permute-start.15 = (bf16[16,1024]{1,0:T(8,128)(2,1)S(1)}, bf16[16,1024]{1,0:T(8,128)(2,1)S(1)}, u32[]{:S(2)}, u32[]{:S(2)}) collective-permute-start(bf16[16,1024]{1,0:T(8,128)(2,1)S(1)} %add_convert_fusion.4), channel_id=1, source_target_pairs={{0,12},{1,13},{2,14},{3,15},{4,8},{5,9},{6,10},{7,11},{8,4},{9,5},... | collective-permute-start | bytes 98312 | tf_op jit(solution)/shard_map/ppermute | solution.py:11
  40.8 1.1 %collective-permute-start.16 = (bf16[16,1024]{1,0:T(8,128)(2,1)S(1)}, bf16[16,1024]{1,0:T(8,128)(2,1)S(1)}, u32[]{:S(2)}, u32[]{:S(2)}) collective-permute-start(bf16[16,1024]{1,0:T(8,128)(2,1)S(1)} %add_convert_fusion.4), channel_id=1, source_target_pairs={{0,20},{1,21},{2,22},{3,23},{4,16},{5,17},{6,18},{7,19},{8,28},{9,... | collective-permute-start | bytes 98312 | tf_op jit(solution)/shard_map/ppermute | solution.py:11
  41.8 1.6 %collective-permute-start.17 = (bf16[16,1024]{1,0:T(8,128)(2,1)S(1)}, bf16[16,1024]{1,0:T(8,128)(2,1)S(1)}, u32[]{:S(2)}, u32[]{:S(2)}) collective-permute-start(bf16[16,1024]{1,0:T(8,128)(2,1)S(1)} %add_convert_fusion.4), channel_id=1, source_target_pairs={{0,28},{1,29},{2,30},{3,31},{4,24},{5,25},{6,26},{7,27},{8,20},{9,... | collective-permute-start | bytes 98312 | tf_op jit(solution)/shard_map/ppermute | solution.py:11
  43.4 0.6 %convert_reduce_fusion.1 = f32[512]{0:T(512)} fusion(bf16[64,512]{1,0:T(8,128)(2,1)S(1)} %fusion.1), kind=kLoop, calls=%fused_computation.26 | loop fusion | flops 65024 | bytes 67584 | tf_op jit(solution)/shard_map/reduce_sum | solution.py:131
  44.0 0.0 collective-permute-done.15
  44.1 1.8 %collective-permute-done.16 = bf16[16,1024]{1,0:T(8,128)(2,1)S(1)} collective-permute-done((bf16[16,1024]{1,0:T(8,128)(2,1)S(1)}, bf16[16,1024]{1,0:T(8,128)(2,1)S(1)}, u32[]{:S(2)}, u32[]{:S(2)}) %collective-permute-start.16) | collective-permute-done | bytes 32800 | tf_op jit(solution)/shard_map/ppermute | solution.py:11
  45.9 1.2 %collective-permute-done.17 = bf16[16,1024]{1,0:T(8,128)(2,1)S(1)} collective-permute-done((bf16[16,1024]{1,0:T(8,128)(2,1)S(1)}, bf16[16,1024]{1,0:T(8,128)(2,1)S(1)}, u32[]{:S(2)}, u32[]{:S(2)}) %collective-permute-start.17) | collective-permute-done | bytes 32800 | tf_op jit(solution)/shard_map/ppermute | solution.py:11
  47.1 0.7 %convert_subtract_fusion.1 = f32[16,1024]{1,0:T(8,128)} fusion(bf16[16,1024]{1,0:T(8,128)(2,1)S(1)} %collective-permute-done.17, bf16[16,1024]{1,0:T(8,128)(2,1)S(1)} %collective-permute-done.16, bf16[16,1024]{1,0:T(8,128)(2,1)S(1)} %collective-permute-done.15, bf16[16,1024]{1,0:T(8,128)(2,1)S(1)} %add_convert_fusion.4, ...), kind=kLoop, calls=%fused_computation.35 | loop fusion | flops 196608 | bytes 327680 | tf_op jit(solution)/shard_map/sub | solution.py:135
  (16 shorter events, 0.2 us)
Async XLA Ops:
  0.6 8.5 %copy-start = (bf16[512,1024]{1,0:T(8,128)(2,1)S(1)}, bf16[512,1024]{1,0:T(8,128)(2,1)}, u32[]{:S(2)}) copy-start(bf16[512,1024]{1,0:T(8,128)(2,1)} %param.9) | copy-start | bytes 3145732
  0.6 6.6 %copy-start.2 = (bf16[16,1024]{1,0:T(8,128)(2,1)S(1)}, bf16[16,1024]{1,0:T(8,128)(2,1)}, u32[]{:S(2)}) copy-start(bf16[16,1024]{1,0:T(8,128)(2,1)} %param.6) | copy-start | bytes 98308
  0.7 8.2 %copy-start.1 = (bf16[1024,512]{1,0:T(8,128)(2,1)S(1)}, bf16[1024,512]{1,0:T(8,128)(2,1)}, u32[]{:S(2)}) copy-start(bf16[1024,512]{1,0:T(8,128)(2,1)} %param.7) | copy-start | bytes 3145732
  0.7 6.7 %collective-permute-start = (bf16[16,1024]{1,0:T(8,128)(2,1)}, bf16[16,1024]{1,0:T(8,128)(2,1)S(1)}, u32[]{:S(2)}, u32[]{:S(2)}) collective-permute-start(bf16[16,1024]{1,0:T(8,128)(2,1)} %param.6), channel_id=1, source_target_pairs={{0,1},{1,0},{2,3},{3,2},{4,5},{5,4},{6,7},{7,6},{8,9},{9,8},{10,11... | collective-permute-start | bytes 98312 | tf_op jit(solution)/shard_map/ppermute | solution.py:11
  3.7 3.8 %collective-permute-start.1 = (bf16[16,1024]{1,0:T(8,128)(2,1)}, bf16[16,1024]{1,0:T(8,128)(2,1)S(1)}, u32[]{:S(2)}, u32[]{:S(2)}) collective-permute-start(bf16[16,1024]{1,0:T(8,128)(2,1)} %param.6), channel_id=1, source_target_pairs={{0,6},{1,7},{2,4},{3,5},{4,2},{5,3},{6,0},{7,1},{8,14},{9,15},{10,... | collective-permute-start | bytes 98312 | tf_op jit(solution)/shard_map/ppermute | solution.py:11
  4.4 4.4 %collective-permute-start.2 = (bf16[16,1024]{1,0:T(8,128)(2,1)}, bf16[16,1024]{1,0:T(8,128)(2,1)S(1)}, u32[]{:S(2)}, u32[]{:S(2)}) collective-permute-start(bf16[16,1024]{1,0:T(8,128)(2,1)} %param.6), channel_id=1, source_target_pairs={{0,7},{1,6},{2,5},{3,4},{4,3},{5,2},{6,1},{7,0},{8,15},{9,14},{10,... | collective-permute-start | bytes 98312 | tf_op jit(solution)/shard_map/ppermute | solution.py:11
  6.4 2.7 %copy-start.4 = (f32[512]{0:T(512)S(1)}, f32[512]{0:T(512)}, u32[]{:S(2)}) copy-start(f32[512]{0:T(512)} %param.8) | copy-start | bytes 6148
  9.4 12.9 %copy-start.3 = (f32[1024]{0:T(1024)S(1)}, f32[1024]{0:T(1024)}, u32[]{:S(2)}) copy-start(f32[1024]{0:T(1024)} %param.10) | copy-start | bytes 12292
  9.6 1.9 %collective-permute-start.3 = (bf16[64,512]{1,0:T(8,128)(2,1)S(1)}, bf16[64,512]{1,0:T(8,128)(2,1)S(1)}, u32[]{:S(2)}, u32[]{:S(2)}) collective-permute-start(bf16[64,512]{1,0:T(8,128)(2,1)S(1)} %convolution_convert_fusion.3), channel_id=1, source_target_pairs={{0,4},{1,5},{2,6},{3,7},{4,0},{5,1},{6,2},{7,3},{8,12},{9,13},{10,... | collective-permute-start | bytes 196616 | tf_op jit(solution)/shard_map/ppermute | solution.py:11
  11.6 3.9 %collective-permute-start.5 = (bf16[64,512]{1,0:T(8,128)(2,1)S(1)}, bf16[64,512]{1,0:T(8,128)(2,1)S(1)}, u32[]{:S(2)}, u32[]{:S(2)}) collective-permute-start(bf16[64,512]{1,0:T(8,128)(2,1)S(1)} %add_convert_fusion.3), channel_id=1, source_target_pairs={{0,6},{1,7},{2,4},{3,5},{4,2},{5,3},{6,0},{7,1},{8,14},{9,15},{10,... | collective-permute-start | bytes 196616 | tf_op jit(solution)/shard_map/ppermute | solution.py:11
  12.1 5.7 %collective-permute-start.6 = (bf16[64,512]{1,0:T(8,128)(2,1)S(1)}, bf16[64,512]{1,0:T(8,128)(2,1)S(1)}, u32[]{:S(2)}, u32[]{:S(2)}) collective-permute-start(bf16[64,512]{1,0:T(8,128)(2,1)S(1)} %add_convert_fusion.3), channel_id=1, source_target_pairs={{0,3},{1,2},{2,1},{3,0},{4,7},{5,6},{6,5},{7,4},{8,11},{9,10},{10,... | collective-permute-start | bytes 196616 | tf_op jit(solution)/shard_map/ppermute | solution.py:11
  13.6 4.3 %collective-permute-start.4 = (bf16[64,512]{1,0:T(8,128)(2,1)S(1)}, bf16[64,512]{1,0:T(8,128)(2,1)S(1)}, u32[]{:S(2)}, u32[]{:S(2)}) collective-permute-start(bf16[64,512]{1,0:T(8,128)(2,1)S(1)} %add_convert_fusion.3), channel_id=1, source_target_pairs={{0,5},{1,4},{2,7},{3,6},{4,1},{5,0},{6,3},{7,2},{8,13},{9,12},{10,... | collective-permute-start | bytes 196616 | tf_op jit(solution)/shard_map/ppermute | solution.py:11
  18.0 4.3 %collective-permute-start.7 = (bf16[64,512]{1,0:T(8,128)(2,1)S(1)}, bf16[64,512]{1,0:T(8,128)(2,1)S(1)}, u32[]{:S(2)}, u32[]{:S(2)}) collective-permute-start(bf16[64,512]{1,0:T(8,128)(2,1)S(1)} %add_convert_fusion.2), channel_id=1, source_target_pairs={{0,12},{1,13},{2,14},{3,15},{4,8},{5,9},{6,10},{7,11},{8,4},{9,5},... | collective-permute-start | bytes 196616 | tf_op jit(solution)/shard_map/ppermute | solution.py:11
  19.8 6.5 %collective-permute-start.8 = (bf16[64,512]{1,0:T(8,128)(2,1)S(1)}, bf16[64,512]{1,0:T(8,128)(2,1)S(1)}, u32[]{:S(2)}, u32[]{:S(2)}) collective-permute-start(bf16[64,512]{1,0:T(8,128)(2,1)S(1)} %add_convert_fusion.2), channel_id=1, source_target_pairs={{0,20},{1,21},{2,22},{3,23},{4,16},{5,17},{6,18},{7,19},{8,28},{9,... | collective-permute-start | bytes 196616 | tf_op jit(solution)/shard_map/ppermute | solution.py:11
  21.9 6.5 %collective-permute-start.9 = (bf16[64,512]{1,0:T(8,128)(2,1)S(1)}, bf16[64,512]{1,0:T(8,128)(2,1)S(1)}, u32[]{:S(2)}, u32[]{:S(2)}) collective-permute-start(bf16[64,512]{1,0:T(8,128)(2,1)S(1)} %add_convert_fusion.2), channel_id=1, source_target_pairs={{0,24},{1,25},{2,26},{3,27},{4,28},{5,29},{6,30},{7,31},{8,16},{9,... | collective-permute-start | bytes 196616 | tf_op jit(solution)/shard_map/ppermute | solution.py:11
  28.5 1.3 %collective-permute-start.10 = (bf16[64,512]{1,0:T(8,128)(2,1)S(1)}, bf16[64,512]{1,0:T(8,128)(2,1)S(1)}, u32[]{:S(2)}, u32[]{:S(2)}) collective-permute-start(bf16[64,512]{1,0:T(8,128)(2,1)S(1)} %fusion.9), channel_id=1, source_target_pairs={{0,4},{1,5},{2,6},{3,7},{4,0},{5,1},{6,2},{7,3},{8,12},{9,13},{10,... | collective-permute-start | bytes 196616 | tf_op jit(solution)/shard_map/ppermute | solution.py:11
  31.9 1.6 %collective-permute-start.11 = (bf16[64,1024]{1,0:T(8,128)(2,1)S(1)}, bf16[64,1024]{1,0:T(8,128)(2,1)S(1)}, u32[]{:S(2)}, u32[]{:S(2)}) collective-permute-start(bf16[64,1024]{1,0:T(8,128)(2,1)S(1)} %convolution_convert_fusion.2), channel_id=1, source_target_pairs={{0,4},{1,5},{2,6},{3,7},{4,0},{5,1},{6,2},{7,3},{8,12},{9,13},{10,... | collective-permute-start | bytes 393224 | tf_op jit(solution)/shard_map/ppermute | solution.py:11
  33.6 3.9 %collective-permute-start.12 = (bf16[16,1024]{1,0:T(8,128)(2,1)S(1)}, bf16[16,1024]{1,0:T(8,128)(2,1)S(1)}, u32[]{:S(2)}, u32[]{:S(2)}) collective-permute-start(bf16[16,1024]{1,0:T(8,128)(2,1)S(1)} %get-tuple-element.5), channel_id=1, source_target_pairs={{0,5},{1,4},{2,7},{3,6},{4,1},{5,0},{6,3},{7,2},{8,13},{9,12},{10,... | collective-permute-start | bytes 98312 | tf_op jit(solution)/shard_map/ppermute | solution.py:11
  34.7 3.4 %collective-permute-start.13 = (bf16[16,1024]{1,0:T(8,128)(2,1)S(1)}, bf16[16,1024]{1,0:T(8,128)(2,1)S(1)}, u32[]{:S(2)}, u32[]{:S(2)}) collective-permute-start(bf16[16,1024]{1,0:T(8,128)(2,1)S(1)} %get-tuple-element.7), channel_id=1, source_target_pairs={{0,6},{1,7},{2,4},{3,5},{4,2},{5,3},{6,0},{7,1},{8,14},{9,15},{10,... | collective-permute-start | bytes 98312 | tf_op jit(solution)/shard_map/ppermute | solution.py:11
  35.0 4.2 %collective-permute-start.14 = (bf16[16,1024]{1,0:T(8,128)(2,1)S(1)}, bf16[16,1024]{1,0:T(8,128)(2,1)S(1)}, u32[]{:S(2)}, u32[]{:S(2)}) collective-permute-start(bf16[16,1024]{1,0:T(8,128)(2,1)S(1)} %get-tuple-element.6), channel_id=1, source_target_pairs={{0,7},{1,6},{2,5},{3,4},{4,3},{5,2},{6,1},{7,0},{8,15},{9,14},{10,... | collective-permute-start | bytes 98312 | tf_op jit(solution)/shard_map/ppermute | solution.py:11
  39.3 4.7 %collective-permute-start.15 = (bf16[16,1024]{1,0:T(8,128)(2,1)S(1)}, bf16[16,1024]{1,0:T(8,128)(2,1)S(1)}, u32[]{:S(2)}, u32[]{:S(2)}) collective-permute-start(bf16[16,1024]{1,0:T(8,128)(2,1)S(1)} %add_convert_fusion.4), channel_id=1, source_target_pairs={{0,12},{1,13},{2,14},{3,15},{4,8},{5,9},{6,10},{7,11},{8,4},{9,5},... | collective-permute-start | bytes 98312 | tf_op jit(solution)/shard_map/ppermute | solution.py:11
  40.8 5.1 %collective-permute-start.16 = (bf16[16,1024]{1,0:T(8,128)(2,1)S(1)}, bf16[16,1024]{1,0:T(8,128)(2,1)S(1)}, u32[]{:S(2)}, u32[]{:S(2)}) collective-permute-start(bf16[16,1024]{1,0:T(8,128)(2,1)S(1)} %add_convert_fusion.4), channel_id=1, source_target_pairs={{0,20},{1,21},{2,22},{3,23},{4,16},{5,17},{6,18},{7,19},{8,28},{9,... | collective-permute-start | bytes 98312 | tf_op jit(solution)/shard_map/ppermute | solution.py:11
  41.8 5.3 %collective-permute-start.17 = (bf16[16,1024]{1,0:T(8,128)(2,1)S(1)}, bf16[16,1024]{1,0:T(8,128)(2,1)S(1)}, u32[]{:S(2)}, u32[]{:S(2)}) collective-permute-start(bf16[16,1024]{1,0:T(8,128)(2,1)S(1)} %add_convert_fusion.4), channel_id=1, source_target_pairs={{0,28},{1,29},{2,30},{3,31},{4,24},{5,25},{6,26},{7,27},{8,20},{9,... | collective-permute-start | bytes 98312 | tf_op jit(solution)/shard_map/ppermute | solution.py:11

commit v4 on v3

--- a/solution.py
+++ b/solution.py
@@ -116,11 +116,16 @@
         back = lax.optimization_barrier(against(own, mine_at))
         back = back + against(other, half - mine_at)
         dpre = (gate * back).astype(jnp.bfloat16)
-        grad = lax.dot_general(
-            dpre, enc_weight, (((1,), (1,)), ((), ())), preferred_element_type=jnp.float32
-        )
-        grad = grad.astype(jnp.bfloat16)
-        x = (grad.astype(jnp.float32) + swap(grad, size, core).astype(jnp.float32)).astype(jnp.bfloat16)
+        dpre_other = swap(dpre, size, core)
+        weight = swap(enc_weight, size, core)
+
+        def spread(part, by):
+            return lax.dot_general(
+                part, by, (((1,), (1,)), ((), ())), preferred_element_type=jnp.float32
+            )
+
+        grad = lax.optimization_barrier(spread(dpre, enc_weight))
+        x = (grad + spread(dpre_other, weight)).astype(jnp.bfloat16)
         grad_dec = lax.dot_general(
             codes, resid, (((0,), (0,)), ((), ())), preferred_element_type=jnp.float32
         ).astype(jnp.bfloat16)

time: 48 us -> 49.3 us (1.027)
  matrix products: 6.07 us -> 7.24 us
  waiting for transfers between devices: 17.6 us -> 16.5 us
  local copies, waits for them, and re-layouts: 0.92 us -> 1.68 us
    ppermute x18 -> x19, waiting for transfers between devices: 17.6 us -> 16.5 us  [swap(): return lax.ppermute(x, AXES, [(i, i ^ mask) for i in range(size)])]
    dot_general x1, matrix products: 0.27 us -> 1.03 us  [per_device(): jnp.dot(every[rows:], enc_weight, preferred_element_type=jnp.float32)]
    unnamed x13, local copies, waits for them, and re-layouts: 0.05 us -> 0.81 us
    ppermute x18 -> x19, starting transfers between devices: 20.2 us -> 20.6 us  [swap(): return lax.ppermute(x, AXES, [(i, i ^ mask) for i in range(size)])]
  transfers between devices with their start and end apart: 18 -> 19, of which waited for: 13 -> 12; matrix products, arithmetic and copies ran while one was open for 11% -> 20% of each run, Pallas kernels for 0% -> 0%
where the time goes in v4:
time: 49.3 us; the launch traced here: 49 us
  starting transfers between devices  20.6 us (42%)
  waiting for transfers between devices  16.5 us (33%)
  matrix products  7.24 us (15%)
  other arithmetic  2.08 us (4%)
  local copies, waits for them, and re-layouts  1.68 us (3%)
  between operations  0.84 us (2%)
    ppermute x19, starting transfers between devices, swap(): return lax.ppermute(x, AXES, [(i, i ^ mask) for i in range(size)])  20.6 us
    ppermute x19, waiting for transfers between devices, swap(): return lax.ppermute(x, AXES, [(i, i ^ mask) for i in range(size)])  16.5 us
    dot_general x1, matrix products, per_device(): jnp.dot(passages, enc_weight, preferred_element_type=jnp.float32)  1.48 us
    dot_general x1, matrix products, per_device(): lax.dot_general(codes, resid, (((0,), (0,)), ((), ())), preferred_element...  1.43 us
    dot_general x1, matrix products, per_device(): lax.dot_general(every, dpre, (((0,), (0,)), ((), ())), preferred_element_...  1.43 us
    dot_general x1, matrix products, per_device(): jnp.dot(every[rows:], enc_weight, preferred_element_type=jnp.float32)  1.03 us
  transfers between devices with their start and end apart: 19, of which 12 were waited for; matrix products, arithmetic and copies ran while one was open for 20% of the time, Pallas kernels for 0%

profile of v4, /device:TPU:0, one launch (start us, length us, event | category | flops | bytes accessed | tf_op | source)
XLA Modules:
  0.0 49.0 jit_solution(252838315133814431)
XLA Ops:
  0.6 0.0 copy-start
  0.6 0.0 copy-start.2
  0.7 0.0 copy-start.1
  0.7 3.0 %collective-permute-start = (bf16[16,1024]{1,0:T(8,128)(2,1)}, bf16[16,1024]{1,0:T(8,128)(2,1)S(1)}, u32[]{:S(2)}, u32[]{:S(2)}) collective-permute-start(bf16[16,1024]{1,0:T(8,128)(2,1)} %param.6), channel_id=1, source_target_pairs={{0,1},{1,0},{2,3},{3,2},{4,5},{5,4},{6,7},{7,6},{8,9},{9,8},{10,11... | collective-permute-start | bytes 98312 | tf_op jit(solution)/shard_map/ppermute | solution.py:11
  3.7 0.7 %collective-permute-start.1 = (bf16[16,1024]{1,0:T(8,128)(2,1)}, bf16[16,1024]{1,0:T(8,128)(2,1)}, u32[]{:S(2)}, u32[]{:S(2)}) collective-permute-start(bf16[16,1024]{1,0:T(8,128)(2,1)} %param.6), channel_id=1, source_target_pairs={{0,6},{1,7},{2,4},{3,5},{4,2},{5,3},{6,0},{7,1},{8,14},{9,15},{10,... | collective-permute-start | bytes 98312 | tf_op jit(solution)/shard_map/ppermute | solution.py:11
  4.4 0.6 %collective-permute-start.2 = (bf16[16,1024]{1,0:T(8,128)(2,1)}, bf16[16,1024]{1,0:T(8,128)(2,1)S(1)}, u32[]{:S(2)}, u32[]{:S(2)}) collective-permute-start(bf16[16,1024]{1,0:T(8,128)(2,1)} %param.6), channel_id=1, source_target_pairs={{0,7},{1,6},{2,5},{3,4},{4,3},{5,2},{6,1},{7,0},{8,15},{9,14},{10,... | collective-permute-start | bytes 98312 | tf_op jit(solution)/shard_map/ppermute | solution.py:11
  5.0 0.4 collective-permute-start.12
  5.3 1.5 %fusion.29 = f32[16,512]{1,0:T(8,128)S(1)} fusion(bf16[16,1024]{1,0:T(8,128)(2,1)} %param.6, bf16[1024,512]{1,0:T(8,128)(2,1)} %param.7), kind=kOutput, calls=%fused_computation.57 | convolution fusion | flops 16777216 | bytes 1114112 | tf_op jit(solution)/shard_map/dot_general | solution.py:80
  6.8 0.0 copy-start.4
  6.8 0.8 %constant_dynamic-slice_fusion.3 = (s32[16,512]{1,0:T(8,128)S(1)}, s32[16,512]{1,0:T(8,128)S(1)}, s32[16,512]{1,0:T(8,128)S(1)}, s32[16,512]{1,0:T(8,128)S(1)}) fusion(s32[64,512]{1,0:T(8,128)} %param.11, s32[]{:T(128)S(6)} %select_n.41, s32[]{:T(128)S(6)} %select_n.42, s32[]{:T(128)S(6)} %select_n.44, s32[]{:T(128)S(6)} %select_n.43), kind=kLoop, calls=%fused_computation.51 | loop fusion | bytes 262160 | tf_op jit(solution)/shard_map/dynamic_slice | solution.py:66
  7.7 0.0 copy-done.2
  7.7 0.0 collective-permute-done
  7.7 0.0 collective-permute-done.1
  7.7 1.1 %collective-permute-done.2 = bf16[16,1024]{1,0:T(8,128)(2,1)S(1)} collective-permute-done((bf16[16,1024]{1,0:T(8,128)(2,1)}, bf16[16,1024]{1,0:T(8,128)(2,1)S(1)}, u32[]{:S(2)}, u32[]{:S(2)}) %collective-permute-start.2) | collective-permute-done | bytes 32800 | tf_op jit(solution)/shard_map/ppermute | solution.py:11
  8.8 0.0 copy-done.1
  8.8 1.0 %fusion.13 = f32[48,512]{1,0:T(8,128)S(1)} fusion(bf16[1024,512]{1,0:T(8,128)(2,1)S(1)} %copy-done.1, bf16[16,1024]{1,0:T(8,128)(2,1)S(1)} %collective-permute-done.2, bf16[16,1024]{1,0:T(8,128)(2,1)} %collective-permute-done.1, bf16[16,1024]{1,0:T(8,128)(2,1)S(1)} %collective-permute-done), kind=kOutput, calls=%fused_computation.29 | convolution fusion | flops 50626560 | bytes 1245184 | tf_op jit(solution)/shard_map/dot_general | solution.py:81
  9.9 0.0 copy-done.4
  9.9 0.0 copy-done
  9.9 0.2 fusion.7
  10.1 0.0 copy-start.3
  10.2 0.2 convolution_convert_fusion.2
  10.4 1.0 %collective-permute-start.3 = (bf16[64,512]{1,0:T(8,128)(2,1)S(1)}, bf16[64,512]{1,0:T(8,128)(2,1)S(1)}, u32[]{:S(2)}, u32[]{:S(2)}) collective-permute-start(bf16[64,512]{1,0:T(8,128)(2,1)S(1)} %convolution_convert_fusion.2), channel_id=1, source_target_pairs={{0,4},{1,5},{2,6},{3,7},{4,0},{5,1},{6,2},{7,3},{8,12},{9,13},{10,... | collective-permute-start | bytes 196616 | tf_op jit(solution)/shard_map/ppermute | solution.py:11
  11.4 0.8 %constant_dynamic-update-slice_fusion.1 = bf16[64,1024]{1,0:T(8,128)(2,1)S(1)} fusion(bf16[64,1024]{1,0:T(8,128)(2,1)S(1)} %constant_dynamic-update-slice_fusion.2, bf16[16,1024]{1,0:T(8,128)(2,1)} %collective-permute-done.1), kind=kLoop, calls=%fused_computation.41 | loop fusion | bytes 65536
  12.2 0.1 collective-permute-done.3
  12.3 0.5 %collective-permute-start.5 = (bf16[64,512]{1,0:T(8,128)(2,1)S(1)}, bf16[64,512]{1,0:T(8,128)(2,1)S(1)}, u32[]{:S(2)}, u32[]{:S(2)}) collective-permute-start(bf16[64,512]{1,0:T(8,128)(2,1)S(1)} %add_convert_fusion.2), channel_id=1, source_target_pairs={{0,6},{1,7},{2,4},{3,5},{4,2},{5,3},{6,0},{7,1},{8,14},{9,15},{10,... | collective-permute-start | bytes 196616 | tf_op jit(solution)/shard_map/ppermute | solution.py:11
  12.9 1.5 %collective-permute-start.6 = (bf16[64,512]{1,0:T(8,128)(2,1)S(1)}, bf16[64,512]{1,0:T(8,128)(2,1)S(1)}, u32[]{:S(2)}, u32[]{:S(2)}) collective-permute-start(bf16[64,512]{1,0:T(8,128)(2,1)S(1)} %add_convert_fusion.2), channel_id=1, source_target_pairs={{0,3},{1,2},{2,1},{3,0},{4,7},{5,6},{6,5},{7,4},{8,11},{9,10},{10,... | collective-permute-start | bytes 196616 | tf_op jit(solution)/shard_map/ppermute | solution.py:11
  14.3 1.0 %collective-permute-start.4 = (bf16[64,512]{1,0:T(8,128)(2,1)S(1)}, bf16[64,512]{1,0:T(8,128)(2,1)S(1)}, u32[]{:S(2)}, u32[]{:S(2)}) collective-permute-start(bf16[64,512]{1,0:T(8,128)(2,1)S(1)} %add_convert_fusion.2), channel_id=1, source_target_pairs={{0,5},{1,4},{2,7},{3,6},{4,1},{5,0},{6,3},{7,2},{8,13},{9,12},{10,... | collective-permute-start | bytes 196616 | tf_op jit(solution)/shard_map/ppermute | solution.py:11
  15.3 0.9 %collective-permute-done.5 = bf16[64,512]{1,0:T(8,128)(2,1)S(1)} collective-permute-done((bf16[64,512]{1,0:T(8,128)(2,1)S(1)}, bf16[64,512]{1,0:T(8,128)(2,1)S(1)}, u32[]{:S(2)}, u32[]{:S(2)}) %collective-permute-start.5) | collective-permute-done | bytes 65568 | tf_op jit(solution)/shard_map/ppermute | solution.py:11
  16.3 2.0 %collective-permute-done.6 = bf16[64,512]{1,0:T(8,128)(2,1)S(1)} collective-permute-done((bf16[64,512]{1,0:T(8,128)(2,1)S(1)}, bf16[64,512]{1,0:T(8,128)(2,1)S(1)}, u32[]{:S(2)}, u32[]{:S(2)}) %collective-permute-start.6) | collective-permute-done | bytes 65568 | tf_op jit(solution)/shard_map/ppermute | solution.py:11
  18.2 0.4 collective-permute-done.4
  18.7 1.8 %collective-permute-start.7 = (bf16[64,512]{1,0:T(8,128)(2,1)S(1)}, bf16[64,512]{1,0:T(8,128)(2,1)S(1)}, u32[]{:S(2)}, u32[]{:S(2)}) collective-permute-start(bf16[64,512]{1,0:T(8,128)(2,1)S(1)} %add_convert_fusion.1), channel_id=1, source_target_pairs={{0,12},{1,13},{2,14},{3,15},{4,8},{5,9},{6,10},{7,11},{8,4},{9,5},... | collective-permute-start | bytes 196616 | tf_op jit(solution)/shard_map/ppermute | solution.py:11
  20.6 2.1 %collective-permute-start.8 = (bf16[64,512]{1,0:T(8,128)(2,1)S(1)}, bf16[64,512]{1,0:T(8,128)(2,1)S(1)}, u32[]{:S(2)}, u32[]{:S(2)}) collective-permute-start(bf16[64,512]{1,0:T(8,128)(2,1)S(1)} %add_convert_fusion.1), channel_id=1, source_target_pairs={{0,20},{1,21},{2,22},{3,23},{4,16},{5,17},{6,18},{7,19},{8,28},{9,... | collective-permute-start | bytes 196616 | tf_op jit(solution)/shard_map/ppermute | solution.py:11
  22.7 0.3 collective-permute-start.9
  23.0 0.0 copy-done.3
  23.1 0.0 collective-permute-done.7
  23.1 4.0 %collective-permute-done.8 = bf16[64,512]{1,0:T(8,128)(2,1)S(1)} collective-permute-done((bf16[64,512]{1,0:T(8,128)(2,1)S(1)}, bf16[64,512]{1,0:T(8,128)(2,1)S(1)}, u32[]{:S(2)}, u32[]{:S(2)}) %collective-permute-start.8) | collective-permute-done | bytes 65568 | tf_op jit(solution)/shard_map/ppermute | solution.py:11
  27.1 2.1 %collective-permute-done.9 = bf16[64,512]{1,0:T(8,128)(2,1)S(1)} collective-permute-done((bf16[64,512]{1,0:T(8,128)(2,1)S(1)}, bf16[64,512]{1,0:T(8,128)(2,1)S(1)}, u32[]{:S(2)}, u32[]{:S(2)}) %collective-permute-start.9) | collective-permute-done | bytes 65568 | tf_op jit(solution)/shard_map/ppermute | solution.py:11
  29.2 0.1 fusion.10
  29.2 0.1 collective-permute-start.10
  29.3 0.3 fusion.5
  29.6 0.9 %collective-permute-done.10 = bf16[64,512]{1,0:T(8,128)(2,1)S(1)} collective-permute-done((bf16[64,512]{1,0:T(8,128)(2,1)S(1)}, bf16[64,512]{1,0:T(8,128)(2,1)S(1)}, u32[]{:S(2)}, u32[]{:S(2)}) %collective-permute-start.10) | collective-permute-done | bytes 65568 | tf_op jit(solution)/shard_map/ppermute | solution.py:11
  30.5 0.3 fusion.2
  30.8 0.2 collective-permute-start.11
  31.0 0.4 fusion.30
  31.5 1.4 %convolution_convert_fusion = bf16[512,1024]{1,0:T(8,128)(2,1)} fusion(bf16[64,512]{1,0:T(8,128)(2,1)S(1)} %fusion.12, bf16[64,512]{1,0:T(8,128)(2,1)S(1)} %get-tuple-element.9, bf16[64,512]{1,0:T(8,128)(2,1)S(1)} %get-tuple-element.8), kind=kOutput, calls=%fused_computation | convolution fusion | flops 67895296 | bytes 1245184 | tf_op jit(solution)/shard_map/dot_general | solution.py:129
  32.9 1.4 %convolution_convert_fusion.1 = bf16[1024,512]{1,0:T(8,128)(2,1)} fusion(bf16[64,1024]{1,0:T(8,128)(2,1)S(1)} %constant_dynamic-update-slice_fusion, bf16[64,512]{1,0:T(8,128)(2,1)S(1)} %fusion.2), kind=kOutput, calls=%fused_computation.1 | convolution fusion | flops 67633152 | bytes 1245184 | tf_op jit(solution)/shard_map/dot_general | solution.py:132
  34.4 0.0 collective-permute-done.11
  34.4 0.0 collective-permute-done.12
  34.4 0.4 fusion
  34.8 1.1 %collective-permute-start.13 = (bf16[16,1024]{1,0:T(8,128)(2,1)S(1)}, bf16[16,1024]{1,0:T(8,128)(2,1)S(1)}, u32[]{:S(2)}, u32[]{:S(2)}) collective-permute-start(bf16[16,1024]{1,0:T(8,128)(2,1)S(1)} %get-tuple-element.5), channel_id=1, source_target_pairs={{0,5},{1,4},{2,7},{3,6},{4,1},{5,0},{6,3},{7,2},{8,13},{9,12},{10,... | collective-permute-start | bytes 98312 | tf_op jit(solution)/shard_map/ppermute | solution.py:11
  35.9 0.3 collective-permute-start.14
  36.3 1.8 %collective-permute-start.15 = (bf16[16,1024]{1,0:T(8,128)(2,1)S(1)}, bf16[16,1024]{1,0:T(8,128)(2,1)S(1)}, u32[]{:S(2)}, u32[]{:S(2)}) collective-permute-start(bf16[16,1024]{1,0:T(8,128)(2,1)S(1)} %get-tuple-element.6), channel_id=1, source_target_pairs={{0,7},{1,6},{2,5},{3,4},{4,3},{5,2},{6,1},{7,0},{8,15},{9,14},{10,... | collective-permute-start | bytes 98312 | tf_op jit(solution)/shard_map/ppermute | solution.py:11
  38.1 0.6 %convert_reduce_fusion = f32[1024]{0:T(1024)} fusion(bf16[64,1024]{1,0:T(8,128)(2,1)S(1)} %pad_maximum_fusion), kind=kLoop, calls=%fused_computation.14 | loop fusion | flops 130048 | bytes 135168 | tf_op jit(solution)/shard_map/reduce_sum | solution.py:135
  38.7 0.0 collective-permute-done.13
  38.7 0.6 %collective-permute-done.14 = bf16[16,1024]{1,0:T(8,128)(2,1)S(1)} collective-permute-done((bf16[16,1024]{1,0:T(8,128)(2,1)S(1)}, bf16[16,1024]{1,0:T(8,128)(2,1)S(1)}, u32[]{:S(2)}, u32[]{:S(2)}) %collective-permute-start.14) | collective-permute-done | bytes 32800 | tf_op jit(solution)/shard_map/ppermute | solution.py:11
  39.3 1.2 %collective-permute-done.15 = bf16[16,1024]{1,0:T(8,128)(2,1)S(1)} collective-permute-done((bf16[16,1024]{1,0:T(8,128)(2,1)S(1)}, bf16[16,1024]{1,0:T(8,128)(2,1)S(1)}, u32[]{:S(2)}, u32[]{:S(2)}) %collective-permute-start.15) | collective-permute-done | bytes 32800 | tf_op jit(solution)/shard_map/ppermute | solution.py:11
  40.5 1.5 %collective-permute-start.16 = (bf16[16,1024]{1,0:T(8,128)(2,1)S(1)}, bf16[16,1024]{1,0:T(8,128)(2,1)S(1)}, u32[]{:S(2)}, u32[]{:S(2)}) collective-permute-start(bf16[16,1024]{1,0:T(8,128)(2,1)S(1)} %add_convert_fusion.3), channel_id=1, source_target_pairs={{0,12},{1,13},{2,14},{3,15},{4,8},{5,9},{6,10},{7,11},{8,4},{9,5},... | collective-permute-start | bytes 98312 | tf_op jit(solution)/shard_map/ppermute | solution.py:11
  42.0 1.1 %collective-permute-start.17 = (bf16[16,1024]{1,0:T(8,128)(2,1)S(1)}, bf16[16,1024]{1,0:T(8,128)(2,1)S(1)}, u32[]{:S(2)}, u32[]{:S(2)}) collective-permute-start(bf16[16,1024]{1,0:T(8,128)(2,1)S(1)} %add_convert_fusion.3), channel_id=1, source_target_pairs={{0,20},{1,21},{2,22},{3,23},{4,16},{5,17},{6,18},{7,19},{8,28},{9,... | collective-permute-start | bytes 98312 | tf_op jit(solution)/shard_map/ppermute | solution.py:11
  43.1 1.6 %collective-permute-start.18 = (bf16[16,1024]{1,0:T(8,128)(2,1)S(1)}, bf16[16,1024]{1,0:T(8,128)(2,1)S(1)}, u32[]{:S(2)}, u32[]{:S(2)}) collective-permute-start(bf16[16,1024]{1,0:T(8,128)(2,1)S(1)} %add_convert_fusion.3), channel_id=1, source_target_pairs={{0,28},{1,29},{2,30},{3,31},{4,24},{5,25},{6,26},{7,27},{8,20},{9,... | collective-permute-start | bytes 98312 | tf_op jit(solution)/shard_map/ppermute | solution.py:11
  44.7 0.6 %convert_reduce_fusion.1 = f32[512]{0:T(512)} fusion(bf16[64,512]{1,0:T(8,128)(2,1)S(1)} %fusion.2), kind=kLoop, calls=%fused_computation.26 | loop fusion | flops 65024 | bytes 67584 | tf_op jit(solution)/shard_map/reduce_sum | solution.py:136
  45.3 0.0 collective-permute-done.16
  45.3 1.9 %collective-permute-done.17 = bf16[16,1024]{1,0:T(8,128)(2,1)S(1)} collective-permute-done((bf16[16,1024]{1,0:T(8,128)(2,1)S(1)}, bf16[16,1024]{1,0:T(8,128)(2,1)S(1)}, u32[]{:S(2)}, u32[]{:S(2)}) %collective-permute-start.17) | collective-permute-done | bytes 32800 | tf_op jit(solution)/shard_map/ppermute | solution.py:11
  47.1 1.2 %collective-permute-done.18 = bf16[16,1024]{1,0:T(8,128)(2,1)S(1)} collective-permute-done((bf16[16,1024]{1,0:T(8,128)(2,1)S(1)}, bf16[16,1024]{1,0:T(8,128)(2,1)S(1)}, u32[]{:S(2)}, u32[]{:S(2)}) %collective-permute-start.18) | collective-permute-done | bytes 32800 | tf_op jit(solution)/shard_map/ppermute | solution.py:11
  48.3 0.7 %convert_subtract_fusion.1 = f32[16,1024]{1,0:T(8,128)} fusion(bf16[16,1024]{1,0:T(8,128)(2,1)S(1)} %collective-permute-done.18, bf16[16,1024]{1,0:T(8,128)(2,1)S(1)} %collective-permute-done.17, bf16[16,1024]{1,0:T(8,128)(2,1)S(1)} %collective-permute-done.16, bf16[16,1024]{1,0:T(8,128)(2,1)S(1)} %add_convert_fusion.3, ...), kind=kLoop, calls=%fused_computation.35 | loop fusion | flops 196608 | bytes 327680 | tf_op jit(solution)/shard_map/sub | solution.py:140
  (14 shorter events, 0.2 us)
Async XLA Ops:
  0.6 9.3 %copy-start = (bf16[512,1024]{1,0:T(8,128)(2,1)S(1)}, bf16[512,1024]{1,0:T(8,128)(2,1)}, u32[]{:S(2)}) copy-start(bf16[512,1024]{1,0:T(8,128)(2,1)} %param.9) | copy-start | bytes 3145732
  0.6 7.0 %copy-start.2 = (bf16[16,1024]{1,0:T(8,128)(2,1)S(1)}, bf16[16,1024]{1,0:T(8,128)(2,1)}, u32[]{:S(2)}) copy-start(bf16[16,1024]{1,0:T(8,128)(2,1)} %param.6) | copy-start | bytes 98308
  0.7 8.2 %copy-start.1 = (bf16[1024,512]{1,0:T(8,128)(2,1)S(1)}, bf16[1024,512]{1,0:T(8,128)(2,1)}, u32[]{:S(2)}) copy-start(bf16[1024,512]{1,0:T(8,128)(2,1)} %param.7) | copy-start | bytes 3145732
  0.7 7.0 %collective-permute-start = (bf16[16,1024]{1,0:T(8,128)(2,1)}, bf16[16,1024]{1,0:T(8,128)(2,1)S(1)}, u32[]{:S(2)}, u32[]{:S(2)}) collective-permute-start(bf16[16,1024]{1,0:T(8,128)(2,1)} %param.6), channel_id=1, source_target_pairs={{0,1},{1,0},{2,3},{3,2},{4,5},{5,4},{6,7},{7,6},{8,9},{9,8},{10,11... | collective-permute-start | bytes 98312 | tf_op jit(solution)/shard_map/ppermute | solution.py:11
  3.7 4.0 %collective-permute-start.1 = (bf16[16,1024]{1,0:T(8,128)(2,1)}, bf16[16,1024]{1,0:T(8,128)(2,1)}, u32[]{:S(2)}, u32[]{:S(2)}) collective-permute-start(bf16[16,1024]{1,0:T(8,128)(2,1)} %param.6), channel_id=1, source_target_pairs={{0,6},{1,7},{2,4},{3,5},{4,2},{5,3},{6,0},{7,1},{8,14},{9,15},{10,... | collective-permute-start | bytes 98312 | tf_op jit(solution)/shard_map/ppermute | solution.py:11
  4.4 4.4 %collective-permute-start.2 = (bf16[16,1024]{1,0:T(8,128)(2,1)}, bf16[16,1024]{1,0:T(8,128)(2,1)S(1)}, u32[]{:S(2)}, u32[]{:S(2)}) collective-permute-start(bf16[16,1024]{1,0:T(8,128)(2,1)} %param.6), channel_id=1, source_target_pairs={{0,7},{1,6},{2,5},{3,4},{4,3},{5,2},{6,1},{7,0},{8,15},{9,14},{10,... | collective-permute-start | bytes 98312 | tf_op jit(solution)/shard_map/ppermute | solution.py:11
  5.0 29.4 %collective-permute-start.12 = (bf16[1024,512]{1,0:T(8,128)(2,1)}, bf16[1024,512]{1,0:T(8,128)(2,1)S(1)}, u32[]{:S(2)}, u32[]{:S(2)}) collective-permute-start(bf16[1024,512]{1,0:T(8,128)(2,1)} %param.7), channel_id=1, source_target_pairs={{0,4},{1,5},{2,6},{3,7},{4,0},{5,1},{6,2},{7,3},{8,12},{9,13},{10,... | collective-permute-start | bytes 3145736 | tf_op jit(solution)/shard_map/ppermute | solution.py:11
  6.8 3.1 %copy-start.4 = (f32[512]{0:T(512)S(1)}, f32[512]{0:T(512)}, u32[]{:S(2)}) copy-start(f32[512]{0:T(512)} %param.8) | copy-start | bytes 6148
  10.1 12.9 %copy-start.3 = (f32[1024]{0:T(1024)S(1)}, f32[1024]{0:T(1024)}, u32[]{:S(2)}) copy-start(f32[1024]{0:T(1024)} %param.10) | copy-start | bytes 12292
  10.4 1.9 %collective-permute-start.3 = (bf16[64,512]{1,0:T(8,128)(2,1)S(1)}, bf16[64,512]{1,0:T(8,128)(2,1)S(1)}, u32[]{:S(2)}, u32[]{:S(2)}) collective-permute-start(bf16[64,512]{1,0:T(8,128)(2,1)S(1)} %convolution_convert_fusion.2), channel_id=1, source_target_pairs={{0,4},{1,5},{2,6},{3,7},{4,0},{5,1},{6,2},{7,3},{8,12},{9,13},{10,... | collective-permute-start | bytes 196616 | tf_op jit(solution)/shard_map/ppermute | solution.py:11
  12.3 3.9 %collective-permute-start.5 = (bf16[64,512]{1,0:T(8,128)(2,1)S(1)}, bf16[64,512]{1,0:T(8,128)(2,1)S(1)}, u32[]{:S(2)}, u32[]{:S(2)}) collective-permute-start(bf16[64,512]{1,0:T(8,128)(2,1)S(1)} %add_convert_fusion.2), channel_id=1, source_target_pairs={{0,6},{1,7},{2,4},{3,5},{4,2},{5,3},{6,0},{7,1},{8,14},{9,15},{10,... | collective-permute-start | bytes 196616 | tf_op jit(solution)/shard_map/ppermute | solution.py:11
  12.9 5.4 %collective-permute-start.6 = (bf16[64,512]{1,0:T(8,128)(2,1)S(1)}, bf16[64,512]{1,0:T(8,128)(2,1)S(1)}, u32[]{:S(2)}, u32[]{:S(2)}) collective-permute-start(bf16[64,512]{1,0:T(8,128)(2,1)S(1)} %add_convert_fusion.2), channel_id=1, source_target_pairs={{0,3},{1,2},{2,1},{3,0},{4,7},{5,6},{6,5},{7,4},{8,11},{9,10},{10,... | collective-permute-start | bytes 196616 | tf_op jit(solution)/shard_map/ppermute | solution.py:11
  14.3 4.3 %collective-permute-start.4 = (bf16[64,512]{1,0:T(8,128)(2,1)S(1)}, bf16[64,512]{1,0:T(8,128)(2,1)S(1)}, u32[]{:S(2)}, u32[]{:S(2)}) collective-permute-start(bf16[64,512]{1,0:T(8,128)(2,1)S(1)} %add_convert_fusion.2), channel_id=1, source_target_pairs={{0,5},{1,4},{2,7},{3,6},{4,1},{5,0},{6,3},{7,2},{8,13},{9,12},{10,... | collective-permute-start | bytes 196616 | tf_op jit(solution)/shard_map/ppermute | solution.py:11
  18.7 4.3 %collective-permute-start.7 = (bf16[64,512]{1,0:T(8,128)(2,1)S(1)}, bf16[64,512]{1,0:T(8,128)(2,1)S(1)}, u32[]{:S(2)}, u32[]{:S(2)}) collective-permute-start(bf16[64,512]{1,0:T(8,128)(2,1)S(1)} %add_convert_fusion.1), channel_id=1, source_target_pairs={{0,12},{1,13},{2,14},{3,15},{4,8},{5,9},{6,10},{7,11},{8,4},{9,5},... | collective-permute-start | bytes 196616 | tf_op jit(solution)/shard_map/ppermute | solution.py:11
  20.6 6.5 %collective-permute-start.8 = (bf16[64,512]{1,0:T(8,128)(2,1)S(1)}, bf16[64,512]{1,0:T(8,128)(2,1)S(1)}, u32[]{:S(2)}, u32[]{:S(2)}) collective-permute-start(bf16[64,512]{1,0:T(8,128)(2,1)S(1)} %add_convert_fusion.1), channel_id=1, source_target_pairs={{0,20},{1,21},{2,22},{3,23},{4,16},{5,17},{6,18},{7,19},{8,28},{9,... | collective-permute-start | bytes 196616 | tf_op jit(solution)/shard_map/ppermute | solution.py:11
  22.7 6.5 %collective-permute-start.9 = (bf16[64,512]{1,0:T(8,128)(2,1)S(1)}, bf16[64,512]{1,0:T(8,128)(2,1)S(1)}, u32[]{:S(2)}, u32[]{:S(2)}) collective-permute-start(bf16[64,512]{1,0:T(8,128)(2,1)S(1)} %add_convert_fusion.1), channel_id=1, source_target_pairs={{0,24},{1,25},{2,26},{3,27},{4,28},{5,29},{6,30},{7,31},{8,16},{9,... | collective-permute-start | bytes 196616 | tf_op jit(solution)/shard_map/ppermute | solution.py:11
  29.2 1.3 %collective-permute-start.10 = (bf16[64,512]{1,0:T(8,128)(2,1)S(1)}, bf16[64,512]{1,0:T(8,128)(2,1)S(1)}, u32[]{:S(2)}, u32[]{:S(2)}) collective-permute-start(bf16[64,512]{1,0:T(8,128)(2,1)S(1)} %fusion.10), channel_id=1, source_target_pairs={{0,4},{1,5},{2,6},{3,7},{4,0},{5,1},{6,2},{7,3},{8,12},{9,13},{10,... | collective-permute-start | bytes 196616 | tf_op jit(solution)/shard_map/ppermute | solution.py:11
  30.8 3.6 %collective-permute-start.11 = (bf16[64,512]{1,0:T(8,128)(2,1)S(1)}, bf16[64,512]{1,0:T(8,128)(2,1)S(1)}, u32[]{:S(2)}, u32[]{:S(2)}) collective-permute-start(bf16[64,512]{1,0:T(8,128)(2,1)S(1)} %fusion.2), channel_id=1, source_target_pairs={{0,4},{1,5},{2,6},{3,7},{4,0},{5,1},{6,2},{7,3},{8,12},{9,13},{10,... | collective-permute-start | bytes 196616 | tf_op jit(solution)/shard_map/ppermute | solution.py:11
  34.8 3.9 %collective-permute-start.13 = (bf16[16,1024]{1,0:T(8,128)(2,1)S(1)}, bf16[16,1024]{1,0:T(8,128)(2,1)S(1)}, u32[]{:S(2)}, u32[]{:S(2)}) collective-permute-start(bf16[16,1024]{1,0:T(8,128)(2,1)S(1)} %get-tuple-element.5), channel_id=1, source_target_pairs={{0,5},{1,4},{2,7},{3,6},{4,1},{5,0},{6,3},{7,2},{8,13},{9,12},{10,... | collective-permute-start | bytes 98312 | tf_op jit(solution)/shard_map/ppermute | solution.py:11
  35.9 3.4 %collective-permute-start.14 = (bf16[16,1024]{1,0:T(8,128)(2,1)S(1)}, bf16[16,1024]{1,0:T(8,128)(2,1)S(1)}, u32[]{:S(2)}, u32[]{:S(2)}) collective-permute-start(bf16[16,1024]{1,0:T(8,128)(2,1)S(1)} %get-tuple-element.7), channel_id=1, source_target_pairs={{0,6},{1,7},{2,4},{3,5},{4,2},{5,3},{6,0},{7,1},{8,14},{9,15},{10,... | collective-permute-start | bytes 98312 | tf_op jit(solution)/shard_map/ppermute | solution.py:11
  36.3 4.2 %collective-permute-start.15 = (bf16[16,1024]{1,0:T(8,128)(2,1)S(1)}, bf16[16,1024]{1,0:T(8,128)(2,1)S(1)}, u32[]{:S(2)}, u32[]{:S(2)}) collective-permute-start(bf16[16,1024]{1,0:T(8,128)(2,1)S(1)} %get-tuple-element.6), channel_id=1, source_target_pairs={{0,7},{1,6},{2,5},{3,4},{4,3},{5,2},{6,1},{7,0},{8,15},{9,14},{10,... | collective-permute-start | bytes 98312 | tf_op jit(solution)/shard_map/ppermute | solution.py:11
  40.5 4.7 %collective-permute-start.16 = (bf16[16,1024]{1,0:T(8,128)(2,1)S(1)}, bf16[16,1024]{1,0:T(8,128)(2,1)S(1)}, u32[]{:S(2)}, u32[]{:S(2)}) collective-permute-start(bf16[16,1024]{1,0:T(8,128)(2,1)S(1)} %add_convert_fusion.3), channel_id=1, source_target_pairs={{0,12},{1,13},{2,14},{3,15},{4,8},{5,9},{6,10},{7,11},{8,4},{9,5},... | collective-permute-start | bytes 98312 | tf_op jit(solution)/shard_map/ppermute | solution.py:11
  42.0 5.2 %collective-permute-start.17 = (bf16[16,1024]{1,0:T(8,128)(2,1)S(1)}, bf16[16,1024]{1,0:T(8,128)(2,1)S(1)}, u32[]{:S(2)}, u32[]{:S(2)}) collective-permute-start(bf16[16,1024]{1,0:T(8,128)(2,1)S(1)} %add_convert_fusion.3), channel_id=1, source_target_pairs={{0,20},{1,21},{2,22},{3,23},{4,16},{5,17},{6,18},{7,19},{8,28},{9,... | collective-permute-start | bytes 98312 | tf_op jit(solution)/shard_map/ppermute | solution.py:11
  43.1 5.2 %collective-permute-start.18 = (bf16[16,1024]{1,0:T(8,128)(2,1)S(1)}, bf16[16,1024]{1,0:T(8,128)(2,1)S(1)}, u32[]{:S(2)}, u32[]{:S(2)}) collective-permute-start(bf16[16,1024]{1,0:T(8,128)(2,1)S(1)} %add_convert_fusion.3), channel_id=1, source_target_pairs={{0,28},{1,29},{2,30},{3,31},{4,24},{5,25},{6,26},{7,27},{8,20},{9,... | collective-permute-start | bytes 98312 | tf_op jit(solution)/shard_map/ppermute | solution.py:11

commit v5 on v4

--- a/solution.py
+++ b/solution.py
@@ -105,18 +105,25 @@
         resid = join(own, other)
         mine_at = jnp.where(high, half, 0)
 
-        def against(part, at):
+        dec_other = swap(dec_weight, size, core)
+        gate_other = swap(gate.astype(jnp.bfloat16), size, core)
+
+        def against(part, by, at):
             return lax.dot_general(
                 part,
-                lax.dynamic_slice_in_dim(dec_weight, at, half, 1),
+                lax.dynamic_slice_in_dim(by, at, half, 1),
                 (((1,), (1,)), ((), ())),
                 preferred_element_type=jnp.float32,
             )
 
-        back = lax.optimization_barrier(against(own, mine_at))
-        back = back + against(other, half - mine_at)
+        back = lax.optimization_barrier(against(own, dec_weight, mine_at))
+        back_other = lax.optimization_barrier(against(own, dec_other, mine_at))
+        back = back + against(other, dec_weight, half - mine_at)
+        back_other = back_other + against(other, dec_other, half - mine_at)
         dpre = (gate * back).astype(jnp.bfloat16)
-        dpre_other = swap(dpre, size, core)
+        dpre_other = lax.optimization_barrier(
+            (gate_other.astype(jnp.float32) * back_other).astype(jnp.bfloat16)
+        )
         weight = swap(enc_weight, size, core)
 
         def spread(part, by):

time: 49.3 us -> 51.7 us (1.049)
  matrix products: 7.24 us -> 9.05 us
  other arithmetic: 2.08 us -> 2.75 us
    dot_general x2, matrix products: 0.87 us -> 2.1 us  [spread(): lax.dot_general(part, by, (((1,), (1,)), ((), ())), preferred_element_typ...]
    convert_element_type x0 -> x2, other arithmetic: none -> 0.67 us  [the longest x1 0.64 us: per_device(): gate_other = swap(gate.astype(jnp.bfloat16), size, core)]
    dot_general x2 -> x4, matrix products: 0.58 us -> 1.15 us  [against(): lax.dot_general(part, lax.dynamic_slice_in_dim(by, at, half, 1), (((1,),...]
    ppermute x19 -> x20, starting transfers between devices: 20.6 us -> 20.1 us  [swap(): return lax.ppermute(x, AXES, [(i, i ^ mask) for i in range(size)])]
    ppermute x19 -> x20, waiting for transfers between devices: 16.5 us -> 16.8 us  [swap(): return lax.ppermute(x, AXES, [(i, i ^ mask) for i in range(size)])]
  transfers between devices with their start and end apart: 19 -> 20, of which waited for: 12 -> 12; matrix products, arithmetic and copies ran while one was open for 20% -> 22% of each run, Pallas kernels for 0% -> 0%
where the time goes in v5:
time: 51.7 us; the launch traced here: 51.3 us
  starting transfers between devices  20.1 us (39%)
  waiting for transfers between devices  16.8 us (32%)
  matrix products  9.05 us (18%)
  other arithmetic  2.75 us (5%)
  local copies, waits for them, and re-layouts  1.75 us (3%)
  between operations  0.83 us (2%)
    ppermute x20, starting transfers between devices, swap(): return lax.ppermute(x, AXES, [(i, i ^ mask) for i in range(size)])  20.1 us
    ppermute x20, waiting for transfers between devices, swap(): return lax.ppermute(x, AXES, [(i, i ^ mask) for i in range(size)])  16.8 us
    dot_general x2, matrix products, spread(): lax.dot_general(part, by, (((1,), (1,)), ((), ())), preferred_element_typ...  2.1 us
    dot_general x1, matrix products, per_device(): jnp.dot(passages, enc_weight, preferred_element_type=jnp.float32)  1.48 us
    dot_general x1, matrix products, per_device(): lax.dot_general(every, dpre, (((0,), (0,)), ((), ())), preferred_element_...  1.43 us
    dot_general x1, matrix products, per_device(): lax.dot_general(codes, resid, (((0,), (0,)), ((), ())), preferred_element...  1.43 us
    dot_general x4, matrix products, against(): lax.dot_general(part, lax.dynamic_slice_in_dim(by, at, half, 1), (((1,),...  1.15 us
  transfers between devices with their start and end apart: 20, of which 12 were waited for; matrix products, arithmetic and copies ran while one was open for 22% of the time, Pallas kernels for 0%

profile of v5, /device:TPU:0, one launch (start us, length us, event | category | flops | bytes accessed | tf_op | source)
XLA Modules:
  0.0 51.3 jit_solution(6081718414237731744)
XLA Ops:
  0.6 0.0 copy-start.2
  0.6 0.0 copy-start
  0.7 3.0 %collective-permute-start = (bf16[16,1024]{1,0:T(8,128)(2,1)}, bf16[16,1024]{1,0:T(8,128)(2,1)S(1)}, u32[]{:S(2)}, u32[]{:S(2)}) collective-permute-start(bf16[16,1024]{1,0:T(8,128)(2,1)} %param.6), channel_id=1, source_target_pairs={{0,1},{1,0},{2,3},{3,2},{4,5},{5,4},{6,7},{7,6},{8,9},{9,8},{10,11... | collective-permute-start | bytes 98312 | tf_op jit(solution)/shard_map/ppermute | solution.py:11
  3.7 0.7 %collective-permute-start.1 = (bf16[16,1024]{1,0:T(8,128)(2,1)}, bf16[16,1024]{1,0:T(8,128)(2,1)}, u32[]{:S(2)}, u32[]{:S(2)}) collective-permute-start(bf16[16,1024]{1,0:T(8,128)(2,1)} %param.6), channel_id=1, source_target_pairs={{0,6},{1,7},{2,4},{3,5},{4,2},{5,3},{6,0},{7,1},{8,14},{9,15},{10,... | collective-permute-start | bytes 98312 | tf_op jit(solution)/shard_map/ppermute | solution.py:11
  4.4 0.6 %collective-permute-start.2 = (bf16[16,1024]{1,0:T(8,128)(2,1)}, bf16[16,1024]{1,0:T(8,128)(2,1)S(1)}, u32[]{:S(2)}, u32[]{:S(2)}) collective-permute-start(bf16[16,1024]{1,0:T(8,128)(2,1)} %param.6), channel_id=1, source_target_pairs={{0,7},{1,6},{2,5},{3,4},{4,3},{5,2},{6,1},{7,0},{8,15},{9,14},{10,... | collective-permute-start | bytes 98312 | tf_op jit(solution)/shard_map/ppermute | solution.py:11
  4.9 0.4 collective-permute-start.12
  5.3 0.1 collective-permute-start.13
  5.5 1.5 %fusion.36 = f32[16,512]{1,0:T(8,128)S(1)} fusion(bf16[16,1024]{1,0:T(8,128)(2,1)} %param.6, bf16[1024,512]{1,0:T(8,128)(2,1)} %param.7), kind=kOutput, calls=%fused_computation.65 | convolution fusion | flops 16777216 | bytes 1114112 | tf_op jit(solution)/shard_map/dot_general | solution.py:80
  6.9 0.9 %constant_dynamic-slice_fusion.3 = (s32[16,512]{1,0:T(8,128)S(1)}, s32[16,512]{1,0:T(8,128)S(1)}, s32[16,512]{1,0:T(8,128)S(1)}, s32[16,512]{1,0:T(8,128)S(1)}) fusion(s32[64,512]{1,0:T(8,128)} %param.11, s32[]{:T(128)S(6)} %select_n.43, s32[]{:T(128)S(6)} %select_n.44, s32[]{:T(128)S(6)} %select_n.46, s32[]{:T(128)S(6)} %select_n.45), kind=kLoop, calls=%fused_computation.59 | loop fusion | bytes 262160 | tf_op jit(solution)/shard_map/dynamic_slice | solution.py:66
  7.9 0.6 %fusion.24 = bf16[64,512]{1,0:T(8,128)(2,1)} fusion(s32[16,512]{1,0:T(8,128)S(1)} %get-tuple-element.12, s32[16,512]{1,0:T(8,128)S(1)} %get-tuple-element.13, s32[16,512]{1,0:T(8,128)S(1)} %get-tuple-element.11, s32[16,512]{1,0:T(8,128)S(1)} %get-tuple-element.10), kind=kLoop, calls=%fused_computation.45 | loop fusion | flops 163840 | bytes 196608 | tf_op jit(solution)/shard_map/convert_element_type | solution.py:109
  8.5 0.0 collective-permute-done
  8.5 0.0 collective-permute-done.1
  8.5 0.3 collective-permute-done.2
  8.8 1.0 %fusion.17 = f32[48,512]{1,0:T(8,128)S(1)} fusion(bf16[1024,512]{1,0:T(8,128)(2,1)S(1)} %copy-done, bf16[16,1024]{1,0:T(8,128)(2,1)S(1)} %collective-permute-done.2, bf16[16,1024]{1,0:T(8,128)(2,1)} %collective-permute-done.1, bf16[16,1024]{1,0:T(8,128)(2,1)S(1)} %collective-permute-done), kind=kOutput, calls=%fused_computation.34 | convolution fusion | flops 50626560 | bytes 1245184 | tf_op jit(solution)/shard_map/dot_general | solution.py:81
  9.8 0.0 copy-done.5
  9.9 0.2 fusion.11
  10.1 0.0 copy-start.4
  10.1 0.0 copy-start.3
  10.2 0.2 convolution_convert_fusion.2
  10.4 1.0 %collective-permute-start.3 = (bf16[64,512]{1,0:T(8,128)(2,1)S(1)}, bf16[64,512]{1,0:T(8,128)(2,1)S(1)}, u32[]{:S(2)}, u32[]{:S(2)}) collective-permute-start(bf16[64,512]{1,0:T(8,128)(2,1)S(1)} %convolution_convert_fusion.2), channel_id=1, source_target_pairs={{0,4},{1,5},{2,6},{3,7},{4,0},{5,1},{6,2},{7,3},{8,12},{9,13},{10,... | collective-permute-start | bytes 196616 | tf_op jit(solution)/shard_map/ppermute | solution.py:11
  11.4 0.8 %constant_dynamic-update-slice_fusion.1 = bf16[64,1024]{1,0:T(8,128)(2,1)S(1)} fusion(bf16[64,1024]{1,0:T(8,128)(2,1)S(1)} %constant_dynamic-update-slice_fusion.2, bf16[16,1024]{1,0:T(8,128)(2,1)} %collective-permute-done.1), kind=kLoop, calls=%fused_computation.47 | loop fusion | bytes 65536
  12.2 0.1 collective-permute-done.3
  12.3 0.9 %collective-permute-start.5 = (bf16[64,512]{1,0:T(8,128)(2,1)S(1)}, bf16[64,512]{1,0:T(8,128)(2,1)S(1)}, u32[]{:S(2)}, u32[]{:S(2)}) collective-permute-start(bf16[64,512]{1,0:T(8,128)(2,1)S(1)} %add_convert_fusion.2), channel_id=1, source_target_pairs={{0,6},{1,7},{2,4},{3,5},{4,2},{5,3},{6,0},{7,1},{8,14},{9,15},{10,... | collective-permute-start | bytes 196616 | tf_op jit(solution)/shard_map/ppermute | solution.py:11
  13.3 1.4 %collective-permute-start.6 = (bf16[64,512]{1,0:T(8,128)(2,1)S(1)}, bf16[64,512]{1,0:T(8,128)(2,1)S(1)}, u32[]{:S(2)}, u32[]{:S(2)}) collective-permute-start(bf16[64,512]{1,0:T(8,128)(2,1)S(1)} %add_convert_fusion.2), channel_id=1, source_target_pairs={{0,3},{1,2},{2,1},{3,0},{4,7},{5,6},{6,5},{7,4},{8,11},{9,10},{10,... | collective-permute-start | bytes 196616 | tf_op jit(solution)/shard_map/ppermute | solution.py:11
  14.7 0.6 %collective-permute-start.4 = (bf16[64,512]{1,0:T(8,128)(2,1)S(1)}, bf16[64,512]{1,0:T(8,128)(2,1)S(1)}, u32[]{:S(2)}, u32[]{:S(2)}) collective-permute-start(bf16[64,512]{1,0:T(8,128)(2,1)S(1)} %add_convert_fusion.2), channel_id=1, source_target_pairs={{0,5},{1,4},{2,7},{3,6},{4,1},{5,0},{6,3},{7,2},{8,13},{9,12},{10,... | collective-permute-start | bytes 196616 | tf_op jit(solution)/shard_map/ppermute | solution.py:11
  15.3 0.9 %collective-permute-done.5 = bf16[64,512]{1,0:T(8,128)(2,1)S(1)} collective-permute-done((bf16[64,512]{1,0:T(8,128)(2,1)S(1)}, bf16[64,512]{1,0:T(8,128)(2,1)S(1)}, u32[]{:S(2)}, u32[]{:S(2)}) %collective-permute-start.5) | collective-permute-done | bytes 65568 | tf_op jit(solution)/shard_map/ppermute | solution.py:11
  16.3 2.3 %collective-permute-done.6 = bf16[64,512]{1,0:T(8,128)(2,1)S(1)} collective-permute-done((bf16[64,512]{1,0:T(8,128)(2,1)S(1)}, bf16[64,512]{1,0:T(8,128)(2,1)S(1)}, u32[]{:S(2)}, u32[]{:S(2)}) %collective-permute-start.6) | collective-permute-done | bytes 65568 | tf_op jit(solution)/shard_map/ppermute | solution.py:11
  18.5 0.6 %collective-permute-done.4 = bf16[64,512]{1,0:T(8,128)(2,1)S(1)} collective-permute-done((bf16[64,512]{1,0:T(8,128)(2,1)S(1)}, bf16[64,512]{1,0:T(8,128)(2,1)S(1)}, u32[]{:S(2)}, u32[]{:S(2)}) %collective-permute-start.4) | collective-permute-done | bytes 65568 | tf_op jit(solution)/shard_map/ppermute | solution.py:11
  19.1 1.5 %collective-permute-start.7 = (bf16[64,512]{1,0:T(8,128)(2,1)S(1)}, bf16[64,512]{1,0:T(8,128)(2,1)S(1)}, u32[]{:S(2)}, u32[]{:S(2)}) collective-permute-start(bf16[64,512]{1,0:T(8,128)(2,1)S(1)} %add_convert_fusion.1), channel_id=1, source_target_pairs={{0,12},{1,13},{2,14},{3,15},{4,8},{5,9},{6,10},{7,11},{8,4},{9,5},... | collective-permute-start | bytes 196616 | tf_op jit(solution)/shard_map/ppermute | solution.py:11
  20.6 2.5 %collective-permute-start.8 = (bf16[64,512]{1,0:T(8,128)(2,1)S(1)}, bf16[64,512]{1,0:T(8,128)(2,1)S(1)}, u32[]{:S(2)}, u32[]{:S(2)}) collective-permute-start(bf16[64,512]{1,0:T(8,128)(2,1)S(1)} %add_convert_fusion.1), channel_id=1, source_target_pairs={{0,20},{1,21},{2,22},{3,23},{4,16},{5,17},{6,18},{7,19},{8,28},{9,... | collective-permute-start | bytes 196616 | tf_op jit(solution)/shard_map/ppermute | solution.py:11
  23.1 0.2 collective-permute-start.9
  23.3 0.0 collective-permute-done.7
  23.4 0.1 collective-permute-start.11
  23.4 2.2 %collective-permute-done.8 = bf16[64,512]{1,0:T(8,128)(2,1)S(1)} collective-permute-done((bf16[64,512]{1,0:T(8,128)(2,1)S(1)}, bf16[64,512]{1,0:T(8,128)(2,1)S(1)}, u32[]{:S(2)}, u32[]{:S(2)}) %collective-permute-start.8) | collective-permute-done | bytes 65568 | tf_op jit(solution)/shard_map/ppermute | solution.py:11
  25.6 3.6 %collective-permute-done.9 = bf16[64,512]{1,0:T(8,128)(2,1)S(1)} collective-permute-done((bf16[64,512]{1,0:T(8,128)(2,1)S(1)}, bf16[64,512]{1,0:T(8,128)(2,1)S(1)}, u32[]{:S(2)}, u32[]{:S(2)}) %collective-permute-start.9) | collective-permute-done | bytes 65568 | tf_op jit(solution)/shard_map/ppermute | solution.py:11
  29.2 0.1 fusion.14
  29.2 0.1 collective-permute-start.10
  29.3 0.3 fusion.9
  29.6 0.9 %collective-permute-done.10 = bf16[64,512]{1,0:T(8,128)(2,1)S(1)} collective-permute-done((bf16[64,512]{1,0:T(8,128)(2,1)S(1)}, bf16[64,512]{1,0:T(8,128)(2,1)S(1)}, u32[]{:S(2)}, u32[]{:S(2)}) %collective-permute-start.10) | collective-permute-done | bytes 65568 | tf_op jit(solution)/shard_map/ppermute | solution.py:11
  30.6 0.3 fusion.2
  30.9 0.4 fusion.37
  31.3 1.4 %convolution_convert_fusion = bf16[512,1024]{1,0:T(8,128)(2,1)} fusion(bf16[64,512]{1,0:T(8,128)(2,1)S(1)} %fusion.16, bf16[64,512]{1,0:T(8,128)(2,1)S(1)} %get-tuple-element.9, bf16[64,512]{1,0:T(8,128)(2,1)S(1)} %get-tuple-element.8), kind=kOutput, calls=%fused_computation | convolution fusion | flops 67895296 | bytes 1245184 | tf_op jit(solution)/shard_map/dot_general | solution.py:136
  32.8 1.4 %convolution_convert_fusion.1 = bf16[1024,512]{1,0:T(8,128)(2,1)} fusion(bf16[64,1024]{1,0:T(8,128)(2,1)S(1)} %constant_dynamic-update-slice_fusion, bf16[64,512]{1,0:T(8,128)(2,1)S(1)} %fusion.2), kind=kOutput, calls=%fused_computation.1 | convolution fusion | flops 67633152 | bytes 1245184 | tf_op jit(solution)/shard_map/dot_general | solution.py:139
  34.2 0.0 collective-permute-done.12
  34.2 0.3 fusion.3
  34.5 0.3 fusion.5
  34.8 0.0 collective-permute-done.11
  34.8 0.0 collective-permute-done.13
  34.8 1.7 %fusion = bf16[64,1024]{1,0:T(8,128)(2,1)S(1)} fusion(f32[64,1024]{1,0:T(8,128)S(1)} %fusion.37, bf16[64,512]{1,0:T(8,128)(2,1)S(1)} %multiply_convert_fusion, bf16[1024,512]{1,0:T(8,128)(2,1)} %collective-permute-done.13), kind=kOutput, calls=%fused_computation.3 | convolution fusion | flops 67239936 | bytes 1507328 | tf_op jit(solution)/shard_map/dot_general | solution.py:130
  36.5 1.3 %collective-permute-start.14 = (bf16[16,1024]{1,0:T(8,128)(2,1)S(1)}, bf16[16,1024]{1,0:T(8,128)(2,1)S(1)}, u32[]{:S(2)}, u32[]{:S(2)}) collective-permute-start(bf16[16,1024]{1,0:T(8,128)(2,1)S(1)} %get-tuple-element.5), channel_id=1, source_target_pairs={{0,5},{1,4},{2,7},{3,6},{4,1},{5,0},{6,3},{7,2},{8,13},{9,12},{10,... | collective-permute-start | bytes 98312 | tf_op jit(solution)/shard_map/ppermute | solution.py:11
  37.8 0.9 %collective-permute-start.15 = (bf16[16,1024]{1,0:T(8,128)(2,1)S(1)}, bf16[16,1024]{1,0:T(8,128)(2,1)S(1)}, u32[]{:S(2)}, u32[]{:S(2)}) collective-permute-start(bf16[16,1024]{1,0:T(8,128)(2,1)S(1)} %get-tuple-element.7), channel_id=1, source_target_pairs={{0,6},{1,7},{2,4},{3,5},{4,2},{5,3},{6,0},{7,1},{8,14},{9,15},{10,... | collective-permute-start | bytes 98312 | tf_op jit(solution)/shard_map/ppermute | solution.py:11
  38.8 0.8 %collective-permute-start.16 = (bf16[16,1024]{1,0:T(8,128)(2,1)S(1)}, bf16[16,1024]{1,0:T(8,128)(2,1)S(1)}, u32[]{:S(2)}, u32[]{:S(2)}) collective-permute-start(bf16[16,1024]{1,0:T(8,128)(2,1)S(1)} %get-tuple-element.6), channel_id=1, source_target_pairs={{0,7},{1,6},{2,5},{3,4},{4,3},{5,2},{6,1},{7,0},{8,15},{9,14},{10,... | collective-permute-start | bytes 98312 | tf_op jit(solution)/shard_map/ppermute | solution.py:11
  39.5 0.6 %convert_reduce_fusion = f32[1024]{0:T(1024)} fusion(bf16[64,1024]{1,0:T(8,128)(2,1)S(1)} %pad_maximum_fusion), kind=kLoop, calls=%fused_computation.18 | loop fusion | flops 130048 | bytes 135168 | tf_op jit(solution)/shard_map/reduce_sum | solution.py:142
  40.2 0.0 collective-permute-done.14
  40.2 1.0 %collective-permute-done.15 = bf16[16,1024]{1,0:T(8,128)(2,1)S(1)} collective-permute-done((bf16[16,1024]{1,0:T(8,128)(2,1)S(1)}, bf16[16,1024]{1,0:T(8,128)(2,1)S(1)}, u32[]{:S(2)}, u32[]{:S(2)}) %collective-permute-start.15) | collective-permute-done | bytes 32800 | tf_op jit(solution)/shard_map/ppermute | solution.py:11
  41.2 1.8 %collective-permute-done.16 = bf16[16,1024]{1,0:T(8,128)(2,1)S(1)} collective-permute-done((bf16[16,1024]{1,0:T(8,128)(2,1)S(1)}, bf16[16,1024]{1,0:T(8,128)(2,1)S(1)}, u32[]{:S(2)}, u32[]{:S(2)}) %collective-permute-start.16) | collective-permute-done | bytes 32800 | tf_op jit(solution)/shard_map/ppermute | solution.py:11
  43.0 1.3 %collective-permute-start.17 = (bf16[16,1024]{1,0:T(8,128)(2,1)S(1)}, bf16[16,1024]{1,0:T(8,128)(2,1)S(1)}, u32[]{:S(2)}, u32[]{:S(2)}) collective-permute-start(bf16[16,1024]{1,0:T(8,128)(2,1)S(1)} %add_convert_fusion.3), channel_id=1, source_target_pairs={{0,12},{1,13},{2,14},{3,15},{4,8},{5,9},{6,10},{7,11},{8,4},{9,5},... | collective-permute-start | bytes 98312 | tf_op jit(solution)/shard_map/ppermute | solution.py:11
  44.3 1.1 %collective-permute-start.18 = (bf16[16,1024]{1,0:T(8,128)(2,1)S(1)}, bf16[16,1024]{1,0:T(8,128)(2,1)S(1)}, u32[]{:S(2)}, u32[]{:S(2)}) collective-permute-start(bf16[16,1024]{1,0:T(8,128)(2,1)S(1)} %add_convert_fusion.3), channel_id=1, source_target_pairs={{0,20},{1,21},{2,22},{3,23},{4,16},{5,17},{6,18},{7,19},{8,28},{9,... | collective-permute-start | bytes 98312 | tf_op jit(solution)/shard_map/ppermute | solution.py:11
  45.4 1.5 %collective-permute-start.19 = (bf16[16,1024]{1,0:T(8,128)(2,1)S(1)}, bf16[16,1024]{1,0:T(8,128)(2,1)S(1)}, u32[]{:S(2)}, u32[]{:S(2)}) collective-permute-start(bf16[16,1024]{1,0:T(8,128)(2,1)S(1)} %add_convert_fusion.3), channel_id=1, source_target_pairs={{0,28},{1,29},{2,30},{3,31},{4,24},{5,25},{6,26},{7,27},{8,20},{9,... | collective-permute-start | bytes 98312 | tf_op jit(solution)/shard_map/ppermute | solution.py:11
  47.0 0.6 %convert_reduce_fusion.1 = f32[512]{0:T(512)} fusion(bf16[64,512]{1,0:T(8,128)(2,1)S(1)} %fusion.2), kind=kLoop, calls=%fused_computation.31 | loop fusion | flops 65024 | bytes 67584 | tf_op jit(solution)/shard_map/reduce_sum | solution.py:143
  47.6 0.0 collective-permute-done.17
  47.6 1.2 %collective-permute-done.18 = bf16[16,1024]{1,0:T(8,128)(2,1)S(1)} collective-permute-done((bf16[16,1024]{1,0:T(8,128)(2,1)S(1)}, bf16[16,1024]{1,0:T(8,128)(2,1)S(1)}, u32[]{:S(2)}, u32[]{:S(2)}) %collective-permute-start.18) | collective-permute-done | bytes 32800 | tf_op jit(solution)/shard_map/ppermute | solution.py:11
  48.8 1.9 %collective-permute-done.19 = bf16[16,1024]{1,0:T(8,128)(2,1)S(1)} collective-permute-done((bf16[16,1024]{1,0:T(8,128)(2,1)S(1)}, bf16[16,1024]{1,0:T(8,128)(2,1)S(1)}, u32[]{:S(2)}, u32[]{:S(2)}) %collective-permute-start.19) | collective-permute-done | bytes 32800 | tf_op jit(solution)/shard_map/ppermute | solution.py:11
  50.7 0.7 %convert_subtract_fusion.1 = f32[16,1024]{1,0:T(8,128)} fusion(bf16[16,1024]{1,0:T(8,128)(2,1)S(1)} %collective-permute-done.19, bf16[16,1024]{1,0:T(8,128)(2,1)S(1)} %collective-permute-done.18, bf16[16,1024]{1,0:T(8,128)(2,1)S(1)} %collective-permute-done.17, bf16[16,1024]{1,0:T(8,128)(2,1)S(1)} %add_convert_fusion.3, ...), kind=kLoop, calls=%fused_computation.40 | loop fusion | flops 196608 | bytes 327680 | tf_op jit(solution)/shard_map/sub | solution.py:147
  (22 shorter events, 0.2 us)
Async XLA Ops:
  0.6 7.9 %copy-start.2 = (bf16[16,1024]{1,0:T(8,128)(2,1)S(1)}, bf16[16,1024]{1,0:T(8,128)(2,1)}, u32[]{:S(2)}) copy-start(bf16[16,1024]{1,0:T(8,128)(2,1)} %param.6) | copy-start | bytes 98308
  0.6 8.2 %copy-start = (bf16[1024,512]{1,0:T(8,128)(2,1)S(1)}, bf16[1024,512]{1,0:T(8,128)(2,1)}, u32[]{:S(2)}) copy-start(bf16[1024,512]{1,0:T(8,128)(2,1)} %param.7) | copy-start | bytes 3145732
  0.7 7.9 %collective-permute-start = (bf16[16,1024]{1,0:T(8,128)(2,1)}, bf16[16,1024]{1,0:T(8,128)(2,1)S(1)}, u32[]{:S(2)}, u32[]{:S(2)}) collective-permute-start(bf16[16,1024]{1,0:T(8,128)(2,1)} %param.6), channel_id=1, source_target_pairs={{0,1},{1,0},{2,3},{3,2},{4,5},{5,4},{6,7},{7,6},{8,9},{9,8},{10,11... | collective-permute-start | bytes 98312 | tf_op jit(solution)/shard_map/ppermute | solution.py:11
  3.7 4.8 %collective-permute-start.1 = (bf16[16,1024]{1,0:T(8,128)(2,1)}, bf16[16,1024]{1,0:T(8,128)(2,1)}, u32[]{:S(2)}, u32[]{:S(2)}) collective-permute-start(bf16[16,1024]{1,0:T(8,128)(2,1)} %param.6), channel_id=1, source_target_pairs={{0,6},{1,7},{2,4},{3,5},{4,2},{5,3},{6,0},{7,1},{8,14},{9,15},{10,... | collective-permute-start | bytes 98312 | tf_op jit(solution)/shard_map/ppermute | solution.py:11
  4.4 4.4 %collective-permute-start.2 = (bf16[16,1024]{1,0:T(8,128)(2,1)}, bf16[16,1024]{1,0:T(8,128)(2,1)S(1)}, u32[]{:S(2)}, u32[]{:S(2)}) collective-permute-start(bf16[16,1024]{1,0:T(8,128)(2,1)} %param.6), channel_id=1, source_target_pairs={{0,7},{1,6},{2,5},{3,4},{4,3},{5,2},{6,1},{7,0},{8,15},{9,14},{10,... | collective-permute-start | bytes 98312 | tf_op jit(solution)/shard_map/ppermute | solution.py:11
  4.9 29.3 %collective-permute-start.12 = (bf16[512,1024]{1,0:T(8,128)(2,1)}, bf16[512,1024]{1,0:T(8,128)(2,1)S(1)}, u32[]{:S(2)}, u32[]{:S(2)}) collective-permute-start(bf16[512,1024]{1,0:T(8,128)(2,1)} %param.9), channel_id=1, source_target_pairs={{0,4},{1,5},{2,6},{3,7},{4,0},{5,1},{6,2},{7,3},{8,12},{9,13},{10,... | collective-permute-start | bytes 3145736 | tf_op jit(solution)/shard_map/ppermute | solution.py:11
  5.3 29.5 %collective-permute-start.13 = (bf16[1024,512]{1,0:T(8,128)(2,1)}, bf16[1024,512]{1,0:T(8,128)(2,1)}, u32[]{:S(2)}, u32[]{:S(2)}) collective-permute-start(bf16[1024,512]{1,0:T(8,128)(2,1)} %param.7), channel_id=1, source_target_pairs={{0,4},{1,5},{2,6},{3,7},{4,0},{5,1},{6,2},{7,3},{8,12},{9,13},{10,... | collective-permute-start | bytes 3145736 | tf_op jit(solution)/shard_map/ppermute | solution.py:11
  6.9 2.9 %copy-start.5 = (f32[512]{0:T(512)S(1)}, f32[512]{0:T(512)}, u32[]{:S(2)}) copy-start(f32[512]{0:T(512)} %param.8) | copy-start | bytes 6148
  6.9 3.0 %copy-start.1 = (bf16[512,1024]{1,0:T(8,128)(2,1)S(1)}, bf16[512,1024]{1,0:T(8,128)(2,1)}, u32[]{:S(2)}) copy-start(bf16[512,1024]{1,0:T(8,128)(2,1)} %param.9) | copy-start | bytes 3145732
  10.1 13.2 %copy-start.4 = (f32[1024]{0:T(1024)S(1)}, f32[1024]{0:T(1024)}, u32[]{:S(2)}) copy-start(f32[1024]{0:T(1024)} %param.10) | copy-start | bytes 12292
  10.1 13.2 %copy-start.3 = (bf16[64,512]{1,0:T(8,128)(2,1)S(1)}, bf16[64,512]{1,0:T(8,128)(2,1)}, u32[]{:S(2)}) copy-start(bf16[64,512]{1,0:T(8,128)(2,1)} %fusion.24) | copy-start | bytes 196612
  10.4 1.9 %collective-permute-start.3 = (bf16[64,512]{1,0:T(8,128)(2,1)S(1)}, bf16[64,512]{1,0:T(8,128)(2,1)S(1)}, u32[]{:S(2)}, u32[]{:S(2)}) collective-permute-start(bf16[64,512]{1,0:T(8,128)(2,1)S(1)} %convolution_convert_fusion.2), channel_id=1, source_target_pairs={{0,4},{1,5},{2,6},{3,7},{4,0},{5,1},{6,2},{7,3},{8,12},{9,13},{10,... | collective-permute-start | bytes 196616 | tf_op jit(solution)/shard_map/ppermute | solution.py:11
  12.3 3.9 %collective-permute-start.5 = (bf16[64,512]{1,0:T(8,128)(2,1)S(1)}, bf16[64,512]{1,0:T(8,128)(2,1)S(1)}, u32[]{:S(2)}, u32[]{:S(2)}) collective-permute-start(bf16[64,512]{1,0:T(8,128)(2,1)S(1)} %add_convert_fusion.2), channel_id=1, source_target_pairs={{0,6},{1,7},{2,4},{3,5},{4,2},{5,3},{6,0},{7,1},{8,14},{9,15},{10,... | collective-permute-start | bytes 196616 | tf_op jit(solution)/shard_map/ppermute | solution.py:11
  13.3 5.2 %collective-permute-start.6 = (bf16[64,512]{1,0:T(8,128)(2,1)S(1)}, bf16[64,512]{1,0:T(8,128)(2,1)S(1)}, u32[]{:S(2)}, u32[]{:S(2)}) collective-permute-start(bf16[64,512]{1,0:T(8,128)(2,1)S(1)} %add_convert_fusion.2), channel_id=1, source_target_pairs={{0,3},{1,2},{2,1},{3,0},{4,7},{5,6},{6,5},{7,4},{8,11},{9,10},{10,... | collective-permute-start | bytes 196616 | tf_op jit(solution)/shard_map/ppermute | solution.py:11
  14.7 4.4 %collective-permute-start.4 = (bf16[64,512]{1,0:T(8,128)(2,1)S(1)}, bf16[64,512]{1,0:T(8,128)(2,1)S(1)}, u32[]{:S(2)}, u32[]{:S(2)}) collective-permute-start(bf16[64,512]{1,0:T(8,128)(2,1)S(1)} %add_convert_fusion.2), channel_id=1, source_target_pairs={{0,5},{1,4},{2,7},{3,6},{4,1},{5,0},{6,3},{7,2},{8,13},{9,12},{10,... | collective-permute-start | bytes 196616 | tf_op jit(solution)/shard_map/ppermute | solution.py:11
  19.1 4.2 %collective-permute-start.7 = (bf16[64,512]{1,0:T(8,128)(2,1)S(1)}, bf16[64,512]{1,0:T(8,128)(2,1)S(1)}, u32[]{:S(2)}, u32[]{:S(2)}) collective-permute-start(bf16[64,512]{1,0:T(8,128)(2,1)S(1)} %add_convert_fusion.1), channel_id=1, source_target_pairs={{0,12},{1,13},{2,14},{3,15},{4,8},{5,9},{6,10},{7,11},{8,4},{9,5},... | collective-permute-start | bytes 196616 | tf_op jit(solution)/shard_map/ppermute | solution.py:11
  20.6 5.0 %collective-permute-start.8 = (bf16[64,512]{1,0:T(8,128)(2,1)S(1)}, bf16[64,512]{1,0:T(8,128)(2,1)S(1)}, u32[]{:S(2)}, u32[]{:S(2)}) collective-permute-start(bf16[64,512]{1,0:T(8,128)(2,1)S(1)} %add_convert_fusion.1), channel_id=1, source_target_pairs={{0,20},{1,21},{2,22},{3,23},{4,16},{5,17},{6,18},{7,19},{8,28},{9,... | collective-permute-start | bytes 196616 | tf_op jit(solution)/shard_map/ppermute | solution.py:11
  23.1 6.1 %collective-permute-start.9 = (bf16[64,512]{1,0:T(8,128)(2,1)S(1)}, bf16[64,512]{1,0:T(8,128)(2,1)S(1)}, u32[]{:S(2)}, u32[]{:S(2)}) collective-permute-start(bf16[64,512]{1,0:T(8,128)(2,1)S(1)} %add_convert_fusion.1), channel_id=1, source_target_pairs={{0,24},{1,25},{2,26},{3,27},{4,28},{5,29},{6,30},{7,31},{8,16},{9,... | collective-permute-start | bytes 196616 | tf_op jit(solution)/shard_map/ppermute | solution.py:11
  23.4 11.4 %collective-permute-start.11 = (bf16[64,512]{1,0:T(8,128)(2,1)S(1)}, bf16[64,512]{1,0:T(8,128)(2,1)S(1)}, u32[]{:S(2)}, u32[]{:S(2)}) collective-permute-start(bf16[64,512]{1,0:T(8,128)(2,1)S(1)} %copy-done.3), channel_id=1, source_target_pairs={{0,4},{1,5},{2,6},{3,7},{4,0},{5,1},{6,2},{7,3},{8,12},{9,13},{10,... | collective-permute-start | bytes 196616 | tf_op jit(solution)/shard_map/ppermute | solution.py:11
  29.2 1.3 %collective-permute-start.10 = (bf16[64,512]{1,0:T(8,128)(2,1)S(1)}, bf16[64,512]{1,0:T(8,128)(2,1)S(1)}, u32[]{:S(2)}, u32[]{:S(2)}) collective-permute-start(bf16[64,512]{1,0:T(8,128)(2,1)S(1)} %fusion.14), channel_id=1, source_target_pairs={{0,4},{1,5},{2,6},{3,7},{4,0},{5,1},{6,2},{7,3},{8,12},{9,13},{10,... | collective-permute-start | bytes 196616 | tf_op jit(solution)/shard_map/ppermute | solution.py:11
  36.5 3.7 %collective-permute-start.14 = (bf16[16,1024]{1,0:T(8,128)(2,1)S(1)}, bf16[16,1024]{1,0:T(8,128)(2,1)S(1)}, u32[]{:S(2)}, u32[]{:S(2)}) collective-permute-start(bf16[16,1024]{1,0:T(8,128)(2,1)S(1)} %get-tuple-element.5), channel_id=1, source_target_pairs={{0,5},{1,4},{2,7},{3,6},{4,1},{5,0},{6,3},{7,2},{8,13},{9,12},{10,... | collective-permute-start | bytes 98312 | tf_op jit(solution)/shard_map/ppermute | solution.py:11
  37.8 3.3 %collective-permute-start.15 = (bf16[16,1024]{1,0:T(8,128)(2,1)S(1)}, bf16[16,1024]{1,0:T(8,128)(2,1)S(1)}, u32[]{:S(2)}, u32[]{:S(2)}) collective-permute-start(bf16[16,1024]{1,0:T(8,128)(2,1)S(1)} %get-tuple-element.7), channel_id=1, source_target_pairs={{0,6},{1,7},{2,4},{3,5},{4,2},{5,3},{6,0},{7,1},{8,14},{9,15},{10,... | collective-permute-start | bytes 98312 | tf_op jit(solution)/shard_map/ppermute | solution.py:11
  38.8 4.2 %collective-permute-start.16 = (bf16[16,1024]{1,0:T(8,128)(2,1)S(1)}, bf16[16,1024]{1,0:T(8,128)(2,1)S(1)}, u32[]{:S(2)}, u32[]{:S(2)}) collective-permute-start(bf16[16,1024]{1,0:T(8,128)(2,1)S(1)} %get-tuple-element.6), channel_id=1, source_target_pairs={{0,7},{1,6},{2,5},{3,4},{4,3},{5,2},{6,1},{7,0},{8,15},{9,14},{10,... | collective-permute-start | bytes 98312 | tf_op jit(solution)/shard_map/ppermute | solution.py:11
  43.0 4.5 %collective-permute-start.17 = (bf16[16,1024]{1,0:T(8,128)(2,1)S(1)}, bf16[16,1024]{1,0:T(8,128)(2,1)S(1)}, u32[]{:S(2)}, u32[]{:S(2)}) collective-permute-start(bf16[16,1024]{1,0:T(8,128)(2,1)S(1)} %add_convert_fusion.3), channel_id=1, source_target_pairs={{0,12},{1,13},{2,14},{3,15},{4,8},{5,9},{6,10},{7,11},{8,4},{9,5},... | collective-permute-start | bytes 98312 | tf_op jit(solution)/shard_map/ppermute | solution.py:11
  44.3 4.5 %collective-permute-start.18 = (bf16[16,1024]{1,0:T(8,128)(2,1)S(1)}, bf16[16,1024]{1,0:T(8,128)(2,1)S(1)}, u32[]{:S(2)}, u32[]{:S(2)}) collective-permute-start(bf16[16,1024]{1,0:T(8,128)(2,1)S(1)} %add_convert_fusion.3), channel_id=1, source_target_pairs={{0,20},{1,21},{2,22},{3,23},{4,16},{5,17},{6,18},{7,19},{8,28},{9,... | collective-permute-start | bytes 98312 | tf_op jit(solution)/shard_map/ppermute | solution.py:11
  45.4 5.2 %collective-permute-start.19 = (bf16[16,1024]{1,0:T(8,128)(2,1)S(1)}, bf16[16,1024]{1,0:T(8,128)(2,1)S(1)}, u32[]{:S(2)}, u32[]{:S(2)}) collective-permute-start(bf16[16,1024]{1,0:T(8,128)(2,1)S(1)} %add_convert_fusion.3), channel_id=1, source_target_pairs={{0,28},{1,29},{2,30},{3,31},{4,24},{5,25},{6,26},{7,27},{8,20},{9,... | collective-permute-start | bytes 98312 | tf_op jit(solution)/shard_map/ppermute | solution.py:11
